TPU v7x, 256 devices: a whole 4x4x8 slice. The times are simulated.
256 devices in a mesh: replica: 16 (over z, core), mp: 16 (over y, x).
Axes of the slice: x: 4, y: 4, z: 8, core: 2. Of those that a mesh axis runs over, the one named last changes fastest.
Arguments:
- gradients: bfloat16 [16, 8, 768, 3072], P('replica', None, 'mp'), may hold values from -6 to 6
- feedback: bfloat16 [16, 8, 768, 3072], P('replica', None, 'mp'), may hold values from -4 to 4
- right_init: bfloat16 [8, 3072, 32], replicated, may hold values from -0.109375 to 0.109375
- gram_root: float32 [8, 32, 32], replicated, as said below
- owners: int32 [8], replicated, may hold values from 0 to 15, as said below
- momentum: float32 [16, 1, 768, 3072], P('mp', None, 'replica'), may hold values from -4 to 4
- master_weights: float32 [16, 1, 768, 3072], P('mp', None, 'replica'), may hold values from -1.5 to 1.5
- vector_grads: float32 [16, 10752], P('replica', 'mp'), may hold values from -6 to 6
- vector_momentum: float32 [10752], P('mp'), may hold values from -6 to 6
- vector_params: float32 [10752], P('mp'), may hold values from -6 to 6
Outputs:
- new_feedback: bfloat16 [16, 8, 768, 3072], P('replica', None, 'mp')
- new_momentum: float32 [16, 1, 768, 3072], P('mp', None, 'replica')
- new_master: float32 [16, 1, 768, 3072], P('mp', None, 'replica')
- new_weights: bfloat16 [8, 768, 3072], P(None, 'replica')
- new_vector_momentum: float32 [10752], P('mp')
- new_vector_params: float32 [10752], P('mp')
Inputs may be any that keep to these rules, and one draw needn't show every extreme that they name: `owners`: every matrix has one owner; no owner holds more than 1 of the 8 matrices, and one owner holds exactly 1. `gram_root`: each matrix is the identity plus off-diagonal terms, times a positive scale.
All inputs are finite; a program needn't handle non-finite values.
Results may differ from a plain program's by a relative error of at most 0.007.
Values may be sent and summed in bfloat16 or wider, within the bound.
A program may use at most 192 MiB of HBM per device.

v0:
```python
import jax
import jax.numpy as jnp
from jax import lax
from jax.sharding import PartitionSpec as P


def per_device(
    gradients,
    feedback,
    right_init,
    gram_root,
    owners,
    momentum,
    master_weights,
    vector_grads,
    vector_momentum,
    vector_params,
):
    highest = lax.Precision.HIGHEST
    compensated = (gradients[0].astype(jnp.float32) + feedback[0].astype(jnp.float32)).astype(
        jnp.bfloat16
    )
    owner_count = lax.axis_size("mp")
    capacity = momentum.shape[1]
    matrices = owners.shape[0]
    replica_rows = momentum.shape[2]
    mp_index = lax.axis_index("mp")
    replica_index = lax.axis_index("replica")
    same_owner = owners[:, None] == owners[None, :]
    earlier = jnp.arange(matrices)[:, None] < jnp.arange(matrices)[None, :]
    ranks = jnp.sum((same_owner & earlier).astype(jnp.int32), axis=0)
    slots = owners * capacity + ranks
    slot_table = (slots[None, :] == jnp.arange(owner_count * capacity)[:, None]).astype(jnp.float32)
    table_narrow = slot_table.astype(jnp.bfloat16)
    table_mine = lax.dynamic_slice_in_dim(slot_table, mp_index * capacity, capacity, 0)
    left_terms = jnp.einsum(
        "kmn,knr->kmr", compensated, right_init, preferred_element_type=jnp.float32
    )
    left_sum = lax.psum(left_terms, "replica")
    left_rows = jnp.einsum("kmr,krs->kms", left_sum, gram_root, precision=highest).astype(
        jnp.bfloat16
    )
    right_terms = jnp.einsum(
        "kmn,kms->kns", compensated, left_rows, preferred_element_type=jnp.float32
    )
    right_new = lax.psum(right_terms, ("replica", "mp"))
    left_all = lax.all_gather(left_rows, "mp", axis=1, tiled=True)
    approx_rows = jnp.einsum(
        "kms,kns->kmn", left_rows.astype(jnp.float32), right_new, precision=highest
    )
    new_feedback = (compensated.astype(jnp.float32) - approx_rows).astype(jnp.bfloat16)
    left_chosen = jnp.einsum(
        "ck,kmr->cmr", table_mine.astype(jnp.bfloat16), left_all, preferred_element_type=jnp.float32
    )
    left_chosen = lax.dynamic_slice_in_dim(
        left_chosen, replica_index * replica_rows, replica_rows, 1
    )
    right_chosen = jnp.einsum("ck,knr->cnr", table_mine, right_new, precision=highest)
    approx_slots = jnp.einsum("cmr,cnr->cmn", left_chosen, right_chosen, precision=highest)
    new_momentum = 0.9 * momentum[0] + approx_slots
    new_master = master_weights[0] - 0.1 * new_momentum
    master_narrow = new_master.astype(jnp.bfloat16)
    weight_slots = lax.all_gather(master_narrow, "mp", axis=0, tiled=True)
    new_weights = jnp.einsum(
        "sk,smn->kmn", table_narrow, weight_slots, preferred_element_type=jnp.float32
    ).astype(jnp.bfloat16)
    vector_total = lax.psum(vector_grads[0], "replica")
    new_vector_momentum = 0.9 * vector_momentum + vector_total
    new_vector_params = vector_params - 0.1 * new_vector_momentum
    return (
        new_feedback[None],
        new_momentum[None],
        new_master[None],
        new_weights,
        new_vector_momentum,
        new_vector_params,
    )


def solution(mesh):
    return jax.shard_map(
        per_device,
        mesh=mesh,
        in_specs=(
            P("replica", None, "mp", None),
            P("replica", None, "mp", None),
            P(),
            P(),
            P(),
            P("mp", None, "replica", None),
            P("mp", None, "replica", None),
            P("replica", "mp"),
            P("mp"),
            P("mp"),
        ),
        out_specs=(
            P("replica", None, "mp", None),
            P("mp", None, "replica", None),
            P("mp", None, "replica", None),
            P(None, "replica", None),
            P("mp"),
            P("mp"),
        ),
        check_vma=False,
    )
```

profile of v0, /device:TPU:1, one launch (start us, length us, event | category | flops | bytes accessed | tf_op | source)
XLA Modules:
  0.0 481.2 jit_solution(16211220204946410669)
XLA Ops:
  7.2 0.0 copy-start
  7.2 0.0 all-reduce.3.cloned.1.call-start
  7.2 0.8 reduce.1
  8.0 0.6 copy-done
  8.6 3.1 fusion.27
  11.8 50.5 %all-reduce = (f32[8,48,32]{1,2,0:T(8,128)S(1)}, f32[672]{0:T(1024)S(1)}) all-reduce(f32[8,48,32]{1,2,0:T(8,128)S(1)} %fusion.27, f32[672]{0:T(1024)S(1)} %reduce.1), channel_id=1, replica_groups=mesh['replica'=16,'mp'=16] {'replica'}, use_global_device_ids=true, to_apply=%region_0.0 | all-reduce | flops 12960 | bytes 103680 | tf_op jit(solution)/shard_map/psum | solution.py:39
  62.2 0.0 copy-done.5
  62.3 0.4 convolution_convert_fusion
  62.6 4.7 fusion.25
  67.3 0.0 all-reduce.3.cloned.1.call-update
  67.4 0.0 all-gather.3.cloned.1.call-start
  67.4 0.1 copy.26
  67.6 0.4 copy-done.8
  68.0 0.1 convert_reduce_fusion
  68.1 22.7 %all_gather.6 = bf16[8,768,32]{2,0,1:T(8,128)(2,1)S(1)} all-gather(bf16[8,48,32]{2,0,1:T(8,128)(2,1)S(1)} %copy.26), channel_id=1, replica_groups=mesh['replica'=16,'mp'=16] {'mp'}, dimensions={1}, use_global_device_ids=true | all-gather | bytes 417792 | tf_op jit(solution)/shard_map/all_gather | solution.py:47
  90.8 1.1 multiply_reduce_fusion
  91.9 239.2 %all-reduce.3.cloned.1.call-done = f32[8,3072,32]{1,2,0:T(8,128)} async-done(((f32[8,3072,32]{1,2,0:T(8,128)}), f32[8,3072,32]{1,2,0:T(8,128)}) %all-reduce.3.cloned.1.call-update) | async-done | bytes 3145744 | tf_op jit(solution)/shard_map/psum | solution.py:46
  331.1 44.7 %fusion.6 = f32[1,3072,32]{0,1,2:T(8,128)} fusion(f32[8,3072,32]{1,2,0:T(8,128)} %all-reduce.3.cloned.1.call-done, pred[16,8]{1,0:T(8,128)(4,1)S(1)} %get-tuple-element.31, s32[]{:T(128)S(6)} %select_n.6), kind=kOutput, calls=%fused_computation.7 | convolution fusion | flops 9437184 | bytes 3539460 | tf_op jit(solution)/shard_map/ck,knr->cnr/dot_general | solution.py:58
  375.7 27.1 %copy.35 = f32[1,3072,32]{1,2,0:T(8,128)S(1)} copy(f32[1,3072,32]{0,1,2:T(8,128)} %fusion.6) | data formatting | bytes 786432 | tf_op jit(solution)/shard_map/ck,knr->cnr/dot_general | solution.py:58
  402.9 0.0 copy-start.6
  402.9 0.0 copy-start.7
  402.9 0.6 convolution_add_fusion
  403.6 0.0 copy-start.2
  403.6 1.2 fusion.10
  404.7 0.0 all-gather.3.cloned.1.call-update
  404.8 0.6 multiply_subtract_fusion
  405.4 7.4 %fusion.5 = bf16[1,8,48,3072]{3,2,1,0:T(8,128)(2,1)} fusion(bf16[8,48,32]{1,2,0:T(8,128)(2,1)S(1)} %convolution_convert_fusion, f32[8,3072,32]{1,2,0:T(8,128)} %all-reduce.3.cloned.1.call-done, bf16[1,8,48,3072]{3,2,1,0:T(8,128)(2,1)} %param.11, bf16[1,8,48,3072]{3,2,1,0:T(8,128)(2,1)} %param.10), kind=kOutput, calls=%fused_computation.5 | convolution fusion | flops 461242368 | bytes 10248192 | tf_op jit(solution)/shard_map/kms,kns->kmn/dot_general | solution.py:48
  412.8 0.0 copy-done.2
  412.8 51.4 %all-gather.3.cloned.1.call-done = bf16[768,3072]{1,0:T(8,128)(2,1)} async-done(((bf16[48,3072]{1,0:T(8,128)(2,1)}), bf16[768,3072]{1,0:T(8,128)(2,1)}) %all-gather.3.cloned.1.call-update) | async-done | bytes 4718608 | tf_op jit(solution)/shard_map/all_gather | solution.py:63
  464.2 7.5 %fusion.2 = bf16[8,48,3072]{2,0,1:T(8,128)(2,1)S(1)} fusion(bf16[16,48,3072]{2,1,0:T(8,128)(2,1)} %bitcast.41, s32[8]{0:T(128)S(1)} %add.27), kind=kOutput, calls=%fused_computation.4 | convolution fusion | flops 38928768 | bytes 7077920 | tf_op jit(solution)/shard_map/sk,smn->kmn/dot_general | solution.py:64
  471.7 2.7 copy.29
  474.4 0.0 copy-done.1
  (12 shorter events, 0.0 us)
Async XLA Ops:
  7.2 1.4 copy-start
  7.2 323.9 %all-reduce.3.cloned.1.call-start = ((), (), s32[]{:S(2)}) async-start(), calls=%async_computation | async-start | bytes 6291456 | tf_op jit(solution)/shard_map/psum | solution.py:46
  8.6 53.6 %copy-start.5 = (f32[8,32,32]{2,1,0:T(8,128)S(1)}, f32[8,32,32]{2,1,0:T(8,128)}, u32[]{:S(2)}) copy-start(f32[8,32,32]{2,1,0:T(8,128)} %param.13) | copy-start | bytes 98308
  67.3 0.7 copy-start.8
  67.4 396.9 %all-gather.3.cloned.1.call-start = ((), (), s32[]{:S(2)}) async-start(), calls=%async_computation.1 | async-start | bytes 5013504 | tf_op jit(solution)/shard_map/all_gather | solution.py:63
  375.7 27.1 %copy-start.3 = (f32[1,1,48,3072]{3,2,1,0:T(8,128)S(1)}, f32[1,1,48,3072]{3,2,1,0:T(8,128)}, u32[]{:S(2)}) copy-start(f32[1,1,48,3072]{3,2,1,0:T(8,128)} %param.15) | copy-start | bytes 1769476
  375.7 27.8 %copy-start.4 = (f32[1,1,48,3072]{3,2,1,0:T(8,128)S(1)}, f32[1,1,48,3072]{3,2,1,0:T(8,128)}, u32[]{:S(2)}) copy-start(f32[1,1,48,3072]{3,2,1,0:T(8,128)} %param.16) | copy-start | bytes 1769476
  402.9 1.9 copy-start.6
  402.9 1.9 copy-start.7
  403.6 9.2 %copy-start.2 = (f32[48,3072]{1,0:T(8,128)}, f32[48,3072]{1,0:T(8,128)S(1)}, u32[]{:S(2)}) copy-start(f32[48,3072]{1,0:T(8,128)S(1)} %convolution_add_fusion) | copy-start | bytes 1769476
  464.2 10.2 %copy-start.1 = (bf16[8,3072,32]{1,2,0:T(8,128)(2,1)S(1)}, bf16[8,3072,32]{1,2,0:T(8,128)(2,1)}, u32[]{:S(2)}) copy-start(bf16[8,3072,32]{1,2,0:T(8,128)(2,1)} %param.12) | copy-start | bytes 4718596
Sparse Core Ops, SparseCore 0:
  67.5 263.5 all-reduce.2
  404.9 59.2 all-gather.2
where the time goes:
time: 482 us; the launch traced here: 481 us
  waiting for transfers between devices  291 us (60%)
  blocking collectives  73.2 us (15%)
  matrix products  68.4 us (14%)
  local copies, waits for them, and re-layouts  31 us (6%)
  between operations  14.2 us (3%)
    psum x1, waiting for transfers between devices, per_device(): right_new = lax.psum(right_terms, ('replica', 'mp'))  239 us
    all_gather x1, waiting for transfers between devices, per_device(): weight_slots = lax.all_gather(master_narrow, 'mp', axis=0, tiled=True)  51.4 us
    psum x1, blocking collectives, per_device(): left_sum = lax.psum(left_terms, 'replica')  50.5 us
    dot_general x1, matrix products, per_device(): jnp.einsum('ck,knr->cnr', table_mine, right_new, precision=highest)  44.7 us
    dot_general x1, local copies, waits for them, and re-layouts, per_device(): jnp.einsum('ck,knr->cnr', table_mine, right_new, precision=highest)  27.1 us
    all_gather x1, blocking collectives, per_device(): left_all = lax.all_gather(left_rows, 'mp', axis=1, tiled=True)  22.7 us
  transfers between devices with their start and end apart: 2, of which 2 were waited for; matrix products, arithmetic and copies ran while one was open for 2% of the time, Pallas kernels for 0%

commit v1 on v0

--- a/solution.py
+++ b/solution.py
@@ -30,9 +30,9 @@
     earlier = jnp.arange(matrices)[:, None] < jnp.arange(matrices)[None, :]
     ranks = jnp.sum((same_owner & earlier).astype(jnp.int32), axis=0)
     slots = owners * capacity + ranks
-    slot_table = (slots[None, :] == jnp.arange(owner_count * capacity)[:, None]).astype(jnp.float32)
-    table_narrow = slot_table.astype(jnp.bfloat16)
-    table_mine = lax.dynamic_slice_in_dim(slot_table, mp_index * capacity, capacity, 0)
+    mine = slots[None, :] == (mp_index * capacity + jnp.arange(capacity))[:, None]
+    has = jnp.any(mine, axis=1)
+    chosen = jnp.argmax(mine, axis=1)
     left_terms = jnp.einsum(
         "kmn,knr->kmr", compensated, right_init, preferred_element_type=jnp.float32
     )
@@ -43,27 +43,27 @@
     right_terms = jnp.einsum(
         "kmn,kms->kns", compensated, left_rows, preferred_element_type=jnp.float32
     )
-    right_new = lax.psum(right_terms, ("replica", "mp"))
+    right_part = lax.psum_scatter(right_terms.reshape(-1), "mp", scatter_dimension=0, tiled=True)
+    right_part = lax.psum(right_part, "replica")
+    right_new = lax.all_gather(right_part.astype(jnp.bfloat16), "mp", axis=0, tiled=True).reshape(
+        right_terms.shape
+    )
     left_all = lax.all_gather(left_rows, "mp", axis=1, tiled=True)
     approx_rows = jnp.einsum(
-        "kms,kns->kmn", left_rows.astype(jnp.float32), right_new, precision=highest
+        "kms,kns->kmn", left_rows, right_new, preferred_element_type=jnp.float32
     )
     new_feedback = (compensated.astype(jnp.float32) - approx_rows).astype(jnp.bfloat16)
-    left_chosen = jnp.einsum(
-        "ck,kmr->cmr", table_mine.astype(jnp.bfloat16), left_all, preferred_element_type=jnp.float32
-    )
+    scale = has.astype(jnp.float32)[:, None, None]
     left_chosen = lax.dynamic_slice_in_dim(
-        left_chosen, replica_index * replica_rows, replica_rows, 1
-    )
-    right_chosen = jnp.einsum("ck,knr->cnr", table_mine, right_new, precision=highest)
+        left_all[chosen], replica_index * replica_rows, replica_rows, 1
+    ).astype(jnp.float32) * scale
+    right_chosen = right_new[chosen].astype(jnp.float32) * scale
     approx_slots = jnp.einsum("cmr,cnr->cmn", left_chosen, right_chosen, precision=highest)
     new_momentum = 0.9 * momentum[0] + approx_slots
     new_master = master_weights[0] - 0.1 * new_momentum
     master_narrow = new_master.astype(jnp.bfloat16)
     weight_slots = lax.all_gather(master_narrow, "mp", axis=0, tiled=True)
-    new_weights = jnp.einsum(
-        "sk,smn->kmn", table_narrow, weight_slots, preferred_element_type=jnp.float32
-    ).astype(jnp.bfloat16)
+    new_weights = jnp.take(weight_slots, slots, axis=0)
     vector_total = lax.psum(vector_grads[0], "replica")
     new_vector_momentum = 0.9 * vector_momentum + vector_total
     new_vector_params = vector_params - 0.1 * new_vector_momentum

time: 482 us -> 370 us (0.77)
  waiting for transfers between devices: 291 us -> 178 us
  blocking collectives: 73.2 us -> 120 us
  matrix products: 68.4 us -> 23.4 us
  local copies, waits for them, and re-layouts: 31 us -> 25.3 us
    psum x1 -> x0, waiting for transfers between devices: 239 us -> none  [per_device(): right_new = lax.psum(right_terms, ('replica', 'mp'))]
    unnamed x2 -> x4, waiting for transfers between devices: 0.03 us -> 104 us
    dot_general x3 -> x1, matrix products: 59.5 us -> 7.93 us  [per_device(): jnp.einsum('kms,kns->kmn', left_rows, right_new, preferred_element_type=j...]
    psum x0 -> x1, blocking collectives: none -> 48.4 us  [per_device(): right_part = lax.psum(right_part, 'replica')]
    dot_general x1 -> x0, local copies, waits for them, and re-layouts: 27.1 us -> none  [per_device(): jnp.einsum('ck,knr->cnr', table_mine, right_new, precision=highest)]
    all_gather x0 -> x1, waiting for transfers between devices: none -> 22.4 us  [per_device(): lax.all_gather(right_part.astype(jnp.bfloat16), 'mp', axis=0, tiled=True)]
    reshape x0 -> x2, local copies, waits for them, and re-layouts: none -> 17.2 us  [the longest x1 9.41 us: per_device(): right_terms.reshape(-1)]
  transfers between devices with their start and end apart: 2 -> 3, of which waited for: 2 -> 3; matrix products, arithmetic and copies ran while one was open for 2% -> 3% of each run, Pallas kernels for 0% -> 0%
where the time goes in v1:
time: 370 us
  waiting for transfers between devices  178 us (48%)
  blocking collectives  120 us (32%)
  local copies, waits for them, and re-layouts  25.3 us (7%)
  matrix products  23.4 us (6%)
  between operations  17.2 us (5%)
  other arithmetic  6.49 us (2%)
    unnamed x4, waiting for transfers between devices  104 us
    all_gather x1, waiting for transfers between devices, per_device(): weight_slots = lax.all_gather(master_narrow, 'mp', axis=0, tiled=True)  51 us
    psum x1, blocking collectives, per_device(): left_sum = lax.psum(left_terms, 'replica')  49.7 us
    psum x1, blocking collectives, per_device(): right_part = lax.psum(right_part, 'replica')  48.4 us
    all_gather x1, waiting for transfers between devices, per_device(): lax.all_gather(right_part.astype(jnp.bfloat16), 'mp', axis=0, tiled=True)  22.4 us
    all_gather x1, blocking collectives, per_device(): left_all = lax.all_gather(left_rows, 'mp', axis=1, tiled=True)  21.6 us
    reshape x1, local copies, waits for them, and re-layouts, per_device(): right_terms.reshape(-1)  9.41 us
    dot_general x1, matrix products, per_device(): jnp.einsum('kmn,kms->kns', compensated, left_rows, preferred_element_type...  8.99 us
  transfers between devices with their start and end apart: 3, of which 3 were waited for; matrix products, arithmetic and copies ran while one was open for 3% of the time, Pallas kernels for 0%

profile of v1, /device:TPU:1, one launch (start us, length us, event | category | flops | bytes accessed | tf_op | source)
XLA Modules:
  0.0 369.8 jit_solution(15668243150370292519)
XLA Ops:
  7.2 0.0 copy-start
  7.2 0.0 all-reduce.5.cloned.1.call-start
  7.2 1.3 copy-done
  8.6 3.1 fusion.14
  11.7 49.7 %psum.21 = f32[8,48,32]{1,2,0:T(8,128)S(1)} all-reduce(f32[8,48,32]{1,2,0:T(8,128)S(1)} %fusion.14), channel_id=1, replica_groups=mesh['replica'=16,'mp'=16] {'replica'}, use_global_device_ids=true, to_apply=%region_0.0 | all-reduce | flops 12288 | bytes 98304 | tf_op jit(solution)/shard_map/psum | solution.py:39
  61.4 0.4 convolution_convert_fusion
  61.8 9.0 %fusion.12 = f32[8,3072,32]{2,1,0:T(8,128)} fusion(bf16[8,48,32]{1,2,0:T(8,128)(2,1)S(1)} %convolution_convert_fusion, bf16[1,8,48,3072]{3,2,1,0:T(8,128)(2,1)} %param.11, bf16[1,8,48,3072]{3,2,1,0:T(8,128)(2,1)} %param.10), kind=kOutput, calls=%fused_computation.29 | convolution fusion | flops 80216064 | bytes 7888896 | tf_op jit(solution)/shard_map/kmn,kms->kns/dot_general | solution.py:43
  70.8 9.4 %reshape.76 = f32[786432]{0:T(1024)} reshape(f32[8,3072,32]{2,1,0:T(8,128)} %fusion.12) | data formatting | bytes 6291456 | tf_op jit(solution)/shard_map/reshape | solution.py:46
  80.2 0.0 all-reduce.5.cloned.1.call-update
  80.2 0.0 all-gather.4.cloned.1.call-start
  80.3 0.6 copy-done.9
  80.9 0.6 dynamic-slice.8
  82.1 104.3 %all-reduce.5.cloned.1.call-done = f32[786432]{0:T(1024)} async-done(((f32[786432]{0:T(1024)}), f32[786432]{0:T(1024)}) %all-reduce.5.cloned.1.call-update) | async-done | bytes 3145744
  186.4 0.9 dynamic-slice.9
  187.3 48.4 %all-reduce.6 = (bf16[49152]{0:T(1024)(128)(2,1)}, f32[672]{0:T(1024)S(1)}) all-reduce(f32[49152]{0:T(1024)S(1)} %dynamic-slice.9, f32[672]{0:T(1024)S(1)} %reduce.20), channel_id=1, replica_groups=mesh['replica'=16,'mp'=16] {'replica'}, use_global_device_ids=true, to_apply=%region_2.0 | all-reduce | flops 49824 | bytes 300288 | tf_op jit(solution)/shard_map/psum | solution.py:47
  235.7 0.0 all-gather.4.cloned.1.call-update
  235.7 0.0 all-gather.6.cloned.1.call-start
  235.8 0.1 copy.27
  235.9 0.1 convert_reduce_fusion
  236.0 0.7 bitcast_reduce_fusion
  238.0 0.6 compare_and_fusion
  239.9 21.6 %all_gather.10 = bf16[8,768,32]{2,0,1:T(8,128)(2,1)S(1)} all-gather(bf16[8,48,32]{2,0,1:T(8,128)(2,1)S(1)} %copy.27), channel_id=1, replica_groups=mesh['replica'=16,'mp'=16] {'mp'}, dimensions={1}, use_global_device_ids=true | all-gather | bytes 417792 | tf_op jit(solution)/shard_map/all_gather | solution.py:51
  261.5 22.4 %all-gather.4.cloned.1.call-done = bf16[786432]{0:T(1024)(128)(2,1)} async-done(((bf16[49152]{0:T(1024)(128)(2,1)}), bf16[786432]{0:T(1024)(128)(2,1)}) %all-gather.4.cloned.1.call-update) | async-done | bytes 1572880 | tf_op jit(solution)/shard_map/all_gather | solution.py:48
  283.9 7.8 %reshape.77 = bf16[8,3072,32]{2,1,0:T(8,128)(2,1)} reshape(bf16[786432]{0:T(1024)(128)(2,1)} %all-gather.4.cloned.1.call-done) | data formatting | bytes 3145728 | tf_op jit(solution)/shard_map/reshape | solution.py:48
  291.8 3.0 convolution_add_fusion
  294.8 1.1 fusion.7
  295.9 0.0 all-gather.6.cloned.1.call-update
  295.9 0.6 multiply_subtract_fusion
  296.5 7.9 %fusion = bf16[1,8,48,3072]{3,2,1,0:T(8,128)(2,1)} fusion(bf16[8,48,32]{1,2,0:T(8,128)(2,1)S(1)} %convolution_convert_fusion, bf16[8,3072,32]{2,1,0:T(8,128)(2,1)} %reshape.77, bf16[1,8,48,3072]{3,2,1,0:T(8,128)(2,1)} %param.11, bf16[1,8,48,3072]{3,2,1,0:T(8,128)(2,1)} %param.10), kind=kOutput, calls=%fused_computation.3 | convolution fusion | flops 83755008 | bytes 8675328 | tf_op jit(solution)/shard_map/kms,kns->kmn/dot_general | solution.py:52
  304.4 51.0 %all-gather.6.cloned.1.call-done = bf16[768,3072]{1,0:T(8,128)(2,1)} async-done(((bf16[48,3072]{1,0:T(8,128)(2,1)}), bf16[768,3072]{1,0:T(8,128)(2,1)}) %all-gather.6.cloned.1.call-update) | async-done | bytes 4718608 | tf_op jit(solution)/shard_map/all_gather | solution.py:65
  355.4 4.4 %gather_fusion = bf16[8,48,3072]{2,1,0:T(8,128)(2,1)} fusion(bf16[16,48,3072]{2,1,0:T(8,128)(2,1)} %bitcast.36, s32[1024]{0:T(1024)S(1)} %pad_clamp_fusion), kind=kCustom, calls=%fused_computation | custom fusion | bytes 4718624 | tf_op jit(solution)/shard_map/jit(_take)/gather | solution.py:66
  359.9 3.4 broadcast_select_fusion
  (20 shorter events, 0.1 us)
Async XLA Ops:
  7.2 1.4 copy-start
  7.2 54.2 %copy-start.4 = (f32[8,32,32]{2,1,0:T(8,128)S(1)}, f32[8,32,32]{2,1,0:T(8,128)}, u32[]{:S(2)}) copy-start(f32[8,32,32]{2,1,0:T(8,128)} %param.13) | copy-start | bytes 98308
  7.2 179.2 %all-reduce.5.cloned.1.call-start = ((), (), s32[]{:S(2)}) async-start(), calls=%async_computation.2 | async-start | bytes 6291456
  80.2 0.7 copy-start.9
  80.2 1.9 copy-start.7
  80.2 155.7 %copy-start.8 = (s32[8]{0:T(128)S(1)}, s32[8]{0:T(128)}, u32[]{:S(2)}) copy-start(s32[8]{0:T(128)} %param.14) | copy-start | bytes 100
  80.2 203.7 %all-gather.4.cloned.1.call-start = ((), (), s32[]{:S(2)}) async-start(), calls=%async_computation | async-start | bytes 1671168 | tf_op jit(solution)/shard_map/all_gather | solution.py:48
  235.7 119.7 %all-gather.6.cloned.1.call-start = ((), (), s32[]{:S(2)}) async-start(), calls=%async_computation.1 | async-start | bytes 5013504 | tf_op jit(solution)/shard_map/all_gather | solution.py:65
  261.5 30.2 %copy-start.2 = (f32[1,1,48,3072]{3,2,1,0:T(8,128)S(1)}, f32[1,1,48,3072]{3,2,1,0:T(8,128)}, u32[]{:S(2)}) copy-start(f32[1,1,48,3072]{3,2,1,0:T(8,128)} %param.15) | copy-start | bytes 1769476
  291.7 3.0 copy-start.3
  291.8 4.1 %copy-start.5 = (f32[672]{0:T(1024)S(1)}, f32[672]{0:T(1024)}, u32[]{:S(2)}) copy-start(f32[672]{0:T(1024)} %param.19) | copy-start | bytes 8068
  291.8 4.2 %copy-start.6 = (f32[672]{0:T(1024)S(1)}, f32[672]{0:T(1024)}, u32[]{:S(2)}) copy-start(f32[672]{0:T(1024)} %param.18) | copy-start | bytes 8068
  294.8 9.7 %copy-start.1 = (f32[48,3072]{1,0:T(8,128)}, f32[48,3072]{1,0:T(8,128)S(1)}, u32[]{:S(2)}) copy-start(f32[48,3072]{1,0:T(8,128)S(1)} %convolution_add_fusion) | copy-start | bytes 1769476
Sparse Core Ops, SparseCore 0:
  80.3 106.0 all-reduce.4
  235.8 48.0 all-gather.3
  296.0 59.3 all-gather.5

commit v2 on v1

--- a/solution.py
+++ b/solution.py
@@ -1,7 +1,66 @@
+import functools
+
 import jax
 import jax.numpy as jnp
 from jax import lax
+from jax.experimental import pallas as pl
+from jax.experimental.pallas import tpu as pltpu
 from jax.sharding import PartitionSpec as P
+
+MESH_IDS = pl.DeviceIdType.MESH
+
+
+def _exchange_kernel(n, x_ref, o_ref, recv, send_sem, recv_sem):
+    me = lax.axis_index("replica")
+    mp = lax.axis_index("mp")
+    barrier = pltpu.get_barrier_semaphore()
+    for d in range(1, n):
+        peer = lax.rem(me + d, n)
+        pl.semaphore_signal(barrier, inc=1, device_id=(peer, mp), device_id_type=MESH_IDS)
+    pl.semaphore_wait(barrier, n - 1)
+    copies = []
+    for d in range(1, n):
+        peer = lax.rem(me + d, n)
+        copy = pltpu.make_async_remote_copy(
+            src_ref=x_ref.at[peer],
+            dst_ref=recv.at[me],
+            send_sem=send_sem.at[d],
+            recv_sem=recv_sem.at[me],
+            device_id=(peer, mp),
+            device_id_type=MESH_IDS,
+        )
+        copy.start()
+        copies.append(copy)
+    recv[me] = x_ref[me]
+    for d in range(1, n):
+        source = lax.rem(me + n - d, n)
+        pltpu.make_async_remote_copy(
+            src_ref=x_ref.at[source],
+            dst_ref=recv.at[source],
+            send_sem=send_sem.at[d],
+            recv_sem=recv_sem.at[source],
+            device_id=(source, mp),
+            device_id_type=MESH_IDS,
+        ).wait_recv()
+    for copy in copies:
+        copy.wait_send()
+    o_ref[...] = recv[...]
+
+
+def exchange(x, cid):
+    n = x.shape[0]
+    return pl.pallas_call(
+        functools.partial(_exchange_kernel, n),
+        out_shape=jax.ShapeDtypeStruct(x.shape, x.dtype),
+        in_specs=[pl.BlockSpec(memory_space=pltpu.VMEM)],
+        out_specs=pl.BlockSpec(memory_space=pltpu.VMEM),
+        scratch_shapes=[
+            pltpu.VMEM(x.shape, x.dtype),
+            pltpu.SemaphoreType.DMA((n,)),
+            pltpu.SemaphoreType.DMA((n,)),
+        ],
+        compiler_params=pltpu.CompilerParams(collective_id=cid, has_side_effects=True),
+    )(x)
 
 
 def per_device(
@@ -36,7 +95,16 @@
     left_terms = jnp.einsum(
         "kmn,knr->kmr", compensated, right_init, preferred_element_type=jnp.float32
     )
-    left_sum = lax.psum(left_terms, "replica")
+    replicas = lax.axis_size("replica")
+    vector_len = vector_grads.shape[1]
+    packed = jnp.concatenate([left_terms.reshape(-1), vector_grads[0]])
+    lanes = 128
+    rows = -(-packed.shape[0] // (8 * lanes)) * 8
+    packed = jnp.pad(packed, (0, rows * lanes - packed.shape[0])).reshape(rows, lanes)
+    packed = jnp.sum(exchange(jnp.broadcast_to(packed, (replicas, rows, lanes)), 0), axis=0)
+    packed = packed.reshape(-1)
+    left_sum = packed[: left_terms.size].reshape(left_terms.shape)
+    vector_total = packed[left_terms.size : left_terms.size + vector_len]
     left_rows = jnp.einsum("kmr,krs->kms", left_sum, gram_root, precision=highest).astype(
         jnp.bfloat16
     )
@@ -44,7 +112,9 @@
         "kmn,kms->kns", compensated, left_rows, preferred_element_type=jnp.float32
     )
     right_part = lax.psum_scatter(right_terms.reshape(-1), "mp", scatter_dimension=0, tiled=True)
-    right_part = lax.psum(right_part, "replica")
+    right_part = right_part.reshape(replicas, -1, lanes)
+    right_chunk = jnp.sum(exchange(right_part, 1), axis=0)
+    right_part = exchange(jnp.broadcast_to(right_chunk, right_part.shape), 2).reshape(-1)
     right_new = lax.all_gather(right_part.astype(jnp.bfloat16), "mp", axis=0, tiled=True).reshape(
         right_terms.shape
     )
@@ -64,7 +134,6 @@
     master_narrow = new_master.astype(jnp.bfloat16)
     weight_slots = lax.all_gather(master_narrow, "mp", axis=0, tiled=True)
     new_weights = jnp.take(weight_slots, slots, axis=0)
-    vector_total = lax.psum(vector_grads[0], "replica")
     new_vector_momentum = 0.9 * vector_momentum + vector_total
     new_vector_params = vector_params - 0.1 * new_vector_momentum
     return (

time: 370 us -> 333 us (0.900)
  blocking collectives: 120 us -> 21.1 us
  Pallas kernels: 0 us -> 57 us
  other arithmetic: 6.49 us -> 10.2 us
    psum x2 -> x0, blocking collectives: 98 us -> none  [the longest x1 49.7 us: per_device(): left_sum = lax.psum(left_terms, 'replica')]
    pallas_call x0 -> x3, Pallas kernels: none -> 57 us  [exchange(): pl.pallas_call(functools.partial(_exchange_kernel, n), out_shape=jax.Shap...]
where the time goes in v2:
time: 333 us; the launch traced here: 332 us
  waiting for transfers between devices  175 us (53%)
  Pallas kernels  57 us (17%)
  local copies, waits for them, and re-layouts  27.8 us (8%)
  matrix products  23.5 us (7%)
  blocking collectives  21.1 us (6%)
  between operations  17.2 us (5%)
  other arithmetic  10.2 us (3%)
    unnamed x4, waiting for transfers between devices  103 us
    pallas_call x3, Pallas kernels, exchange(): pl.pallas_call(functools.partial(_exchange_kernel, n), out_shape=jax.Shap...  57 us
    all_gather x1, waiting for transfers between devices, per_device(): weight_slots = lax.all_gather(master_narrow, 'mp', axis=0, tiled=True)  51 us
    all_gather x1, blocking collectives, per_device(): left_all = lax.all_gather(left_rows, 'mp', axis=1, tiled=True)  21.1 us
    all_gather x1, waiting for transfers between devices, per_device(): lax.all_gather(right_part.astype(jnp.bfloat16), 'mp', axis=0, tiled=True)  20.7 us
    reshape x1, local copies, waits for them, and re-layouts, per_device(): right_terms.reshape(-1)  9.41 us
    dot_general x1, matrix products, per_device(): jnp.einsum('kmn,kms->kns', compensated, left_rows, preferred_element_type...  8.99 us
    dot_general x1, matrix products, per_device(): jnp.einsum('kms,kns->kmn', left_rows, right_new, preferred_element_type=j...  7.93 us
  transfers between devices with their start and end apart: 3, of which 3 were waited for; matrix products, arithmetic and copies ran while one was open for 3% of the time, Pallas kernels for 0%

profile of v2, /device:TPU:1, one launch (start us, length us, event | category | flops | bytes accessed | tf_op | source)
XLA Modules:
  0.0 332.1 jit_solution(2495333568382916609)
XLA Ops:
  7.2 1.3 copy-done
  8.6 3.2 fusion.15
  11.8 0.1 reshape.95
  11.9 1.0 broadcast_in_dim.37.x_ref
  12.9 30.8 %shard_map.145 = f32[16,104,128]{2,1,0:T(8,128)} custom-call(f32[16,104,128]{2,1,0:T(8,128)} %broadcast_in_dim.37.x_ref), custom_call_target="tpu_custom_call" | custom-call | tf_op jit(solution)/shard_map/pallas_call | solution.py:52
  43.6 1.2 reduce_sum.27
  44.9 0.1 reshape.97
  45.0 0.5 convolution_convert_fusion
  45.5 9.0 %fusion.13 = f32[8,3072,32]{2,1,0:T(8,128)} fusion(bf16[8,48,32]{1,2,0:T(8,128)(2,1)S(1)} %convolution_convert_fusion, bf16[1,8,48,3072]{3,2,1,0:T(8,128)(2,1)} %param.11, bf16[1,8,48,3072]{3,2,1,0:T(8,128)(2,1)} %param.10), kind=kOutput, calls=%fused_computation.32 | convolution fusion | flops 80216064 | bytes 7888896 | tf_op jit(solution)/shard_map/kmn,kms->kns/dot_general | solution.py:111
  54.5 9.4 %reshape.98 = f32[786432]{0:T(1024)} reshape(f32[8,3072,32]{2,1,0:T(8,128)} %fusion.13) | data formatting | bytes 6291456 | tf_op jit(solution)/shard_map/reshape | solution.py:114
  63.9 0.6 copy-done.9
  64.5 0.6 dynamic-slice.8
  65.8 103.4 %all-reduce.4.cloned.1.call-done = f32[786432]{0:T(1024)} async-done(((f32[786432]{0:T(1024)}), f32[786432]{0:T(1024)}) %all-reduce.4.cloned.1.call-update) | async-done | bytes 3145744
  169.2 1.6 dynamic-slice.9
  170.8 14.2 %shard_map.146 = f32[16,24,128]{2,1,0:T(8,128)} custom-call(f32[16,24,128]{2,1,0:T(8,128)} %bitcast.42), custom_call_target="tpu_custom_call" | custom-call | tf_op jit(solution)/shard_map/pallas_call | solution.py:52
  185.0 1.0 reduce_sum.28
  186.0 0.7 broadcast_in_dim.38.x_ref
  186.7 12.0 %shard_map.147 = f32[16,24,128]{2,1,0:T(8,128)} custom-call(f32[16,24,128]{2,1,0:T(8,128)} %broadcast_in_dim.38.x_ref), custom_call_target="tpu_custom_call" | custom-call | tf_op jit(solution)/shard_map/pallas_call | solution.py:52
  198.7 1.6 convert_element_type.72
  200.3 0.1 copy.33
  200.5 0.7 bitcast_reduce_fusion
  202.5 0.6 compare_and_fusion
  204.5 21.1 %all_gather.10 = bf16[8,768,32]{2,0,1:T(8,128)(2,1)S(1)} all-gather(bf16[8,48,32]{2,0,1:T(8,128)(2,1)S(1)} %copy.33), channel_id=1, replica_groups=mesh['replica'=16,'mp'=16] {'mp'}, dimensions={1}, use_global_device_ids=true | all-gather | bytes 417792 | tf_op jit(solution)/shard_map/all_gather | solution.py:121
  225.6 20.7 %all-gather.4.cloned.1.call-done = bf16[786432]{0:T(1024)(128)(2,1)} async-done(((bf16[49152]{0:T(1024)(128)(2,1)}), bf16[786432]{0:T(1024)(128)(2,1)}) %all-gather.4.cloned.1.call-update) | async-done | bytes 1572880 | tf_op jit(solution)/shard_map/all_gather | solution.py:118
  246.3 7.8 %reshape.100 = bf16[8,3072,32]{2,1,0:T(8,128)(2,1)} reshape(bf16[786432]{0:T(1024)(128)(2,1)} %all-gather.4.cloned.1.call-done) | data formatting | bytes 3145728 | tf_op jit(solution)/shard_map/reshape | solution.py:118
  254.1 3.0 convolution_add_fusion
  257.2 1.1 fusion.7
  258.3 0.6 multiply_subtract_fusion
  258.9 7.9 %fusion = bf16[1,8,48,3072]{3,2,1,0:T(8,128)(2,1)} fusion(bf16[8,48,32]{1,2,0:T(8,128)(2,1)S(1)} %convolution_convert_fusion, bf16[8,3072,32]{2,1,0:T(8,128)(2,1)} %reshape.100, bf16[1,8,48,3072]{3,2,1,0:T(8,128)(2,1)} %param.11, bf16[1,8,48,3072]{3,2,1,0:T(8,128)(2,1)} %param.10), kind=kOutput, calls=%fused_computation.3 | convolution fusion | flops 83755008 | bytes 8675328 | tf_op jit(solution)/shard_map/kms,kns->kmn/dot_general | solution.py:122
  266.8 51.0 %all-gather.6.cloned.1.call-done = bf16[768,3072]{1,0:T(8,128)(2,1)} async-done(((bf16[48,3072]{1,0:T(8,128)(2,1)}), bf16[768,3072]{1,0:T(8,128)(2,1)}) %all-gather.6.cloned.1.call-update) | async-done | bytes 4718608 | tf_op jit(solution)/shard_map/all_gather | solution.py:135
  317.8 4.4 %gather_fusion = bf16[8,48,3072]{2,1,0:T(8,128)(2,1)} fusion(bf16[16,48,3072]{2,1,0:T(8,128)(2,1)} %bitcast.41, s32[1024]{0:T(1024)S(1)} %pad_clamp_fusion), kind=kCustom, calls=%fused_computation | custom fusion | bytes 4718624 | tf_op jit(solution)/shard_map/jit(_take)/gather | solution.py:136
  322.3 3.4 %broadcast_select_fusion = bf16[8,48,3072]{2,1,0:T(8,128)(2,1)} fusion(bf16[8,48,3072]{2,1,0:T(8,128)(2,1)} %gather_fusion, pred[8]{0:T(512)(128)(4,1)S(1)} %get-tuple-element.32), kind=kLoop, calls=%fused_computation.6 | loop fusion | flops 1179648 | bytes 4718600 | tf_op jit(solution)/shard_map/jit(_take)/select_n | solution.py:136
  (30 shorter events, 0.4 us)
Async XLA Ops:
  7.2 1.4 copy-start
  7.2 4.7 %copy-start.7 = (f32[1,672]{1,0:T(1,128)S(1)}, f32[1,672]{1,0:T(1,128)}, u32[]{:S(2)}) copy-start(f32[1,672]{1,0:T(1,128)} %param.17) | copy-start | bytes 8068
  7.2 162.0 %all-reduce.4.cloned.1.call-start = ((), (), s32[]{:S(2)}) async-start(), calls=%async_computation.2 | async-start | bytes 6291456
  11.8 33.2 %copy-start.4 = (f32[8,32,32]{2,1,0:T(8,128)S(1)}, f32[8,32,32]{2,1,0:T(8,128)}, u32[]{:S(2)}) copy-start(f32[8,32,32]{2,1,0:T(8,128)} %param.13) | copy-start | bytes 98308
  63.9 0.7 copy-start.9
  63.9 136.6 %copy-start.8 = (s32[8]{0:T(128)S(1)}, s32[8]{0:T(128)}, u32[]{:S(2)}) copy-start(s32[8]{0:T(128)} %param.14) | copy-start | bytes 100
  63.9 182.4 %all-gather.4.cloned.1.call-start = ((), (), s32[]{:S(2)}) async-start(), calls=%async_computation | async-start | bytes 1671168 | tf_op jit(solution)/shard_map/all_gather | solution.py:118
  200.3 117.6 %all-gather.6.cloned.1.call-start = ((), (), s32[]{:S(2)}) async-start(), calls=%async_computation.1 | async-start | bytes 5013504 | tf_op jit(solution)/shard_map/all_gather | solution.py:135
  225.6 28.6 %copy-start.2 = (f32[1,1,48,3072]{3,2,1,0:T(8,128)S(1)}, f32[1,1,48,3072]{3,2,1,0:T(8,128)}, u32[]{:S(2)}) copy-start(f32[1,1,48,3072]{3,2,1,0:T(8,128)} %param.15) | copy-start | bytes 1769476
  254.1 3.0 copy-start.3
  254.1 4.1 %copy-start.5 = (f32[672]{0:T(1024)S(1)}, f32[672]{0:T(1024)}, u32[]{:S(2)}) copy-start(f32[672]{0:T(1024)} %param.19) | copy-start | bytes 8068
  254.1 4.2 %copy-start.6 = (f32[672]{0:T(1024)S(1)}, f32[672]{0:T(1024)}, u32[]{:S(2)}) copy-start(f32[672]{0:T(1024)} %param.18) | copy-start | bytes 8068
  257.1 9.7 %copy-start.1 = (f32[48,3072]{1,0:T(8,128)}, f32[48,3072]{1,0:T(8,128)S(1)}, u32[]{:S(2)}) copy-start(f32[48,3072]{1,0:T(8,128)S(1)} %convolution_add_fusion) | copy-start | bytes 1769476
Sparse Core Ops, SparseCore 0:
  64.0 105.1 all-reduce.3
  200.4 45.8 all-gather.3
  258.4 59.3 all-gather.5

commit v3 on v2

--- a/solution.py
+++ b/solution.py
@@ -10,13 +10,20 @@
 MESH_IDS = pl.DeviceIdType.MESH
 
 
-def _exchange_kernel(n, x_ref, o_ref, recv, send_sem, recv_sem):
-    me = lax.axis_index("replica")
-    mp = lax.axis_index("mp")
+def _exchange_kernel(n, axis, x_ref, o_ref, recv, send_sem, recv_sem):
+    me = lax.axis_index(axis)
+    here = [lax.axis_index("replica"), lax.axis_index("mp")]
+    where = 0 if axis == "replica" else 1
+
+    def device(peer):
+        ids = list(here)
+        ids[where] = peer
+        return tuple(ids)
+
     barrier = pltpu.get_barrier_semaphore()
     for d in range(1, n):
         peer = lax.rem(me + d, n)
-        pl.semaphore_signal(barrier, inc=1, device_id=(peer, mp), device_id_type=MESH_IDS)
+        pl.semaphore_signal(barrier, inc=1, device_id=device(peer), device_id_type=MESH_IDS)
     pl.semaphore_wait(barrier, n - 1)
     copies = []
     for d in range(1, n):
@@ -26,7 +33,7 @@
             dst_ref=recv.at[me],
             send_sem=send_sem.at[d],
             recv_sem=recv_sem.at[me],
-            device_id=(peer, mp),
+            device_id=device(peer),
             device_id_type=MESH_IDS,
         )
         copy.start()
@@ -39,7 +46,7 @@
             dst_ref=recv.at[source],
             send_sem=send_sem.at[d],
             recv_sem=recv_sem.at[source],
-            device_id=(source, mp),
+            device_id=device(source),
             device_id_type=MESH_IDS,
         ).wait_recv()
     for copy in copies:
@@ -47,10 +54,10 @@
     o_ref[...] = recv[...]
 
 
-def exchange(x, cid):
+def exchange(x, axis, cid):
     n = x.shape[0]
     return pl.pallas_call(
-        functools.partial(_exchange_kernel, n),
+        functools.partial(_exchange_kernel, n, axis),
         out_shape=jax.ShapeDtypeStruct(x.shape, x.dtype),
         in_specs=[pl.BlockSpec(memory_space=pltpu.VMEM)],
         out_specs=pl.BlockSpec(memory_space=pltpu.VMEM),
@@ -59,7 +66,9 @@
             pltpu.SemaphoreType.DMA((n,)),
             pltpu.SemaphoreType.DMA((n,)),
         ],
-        compiler_params=pltpu.CompilerParams(collective_id=cid, has_side_effects=True),
+        compiler_params=pltpu.CompilerParams(
+            collective_id=cid, has_side_effects=True, vmem_limit_bytes=48 * 1024 * 1024
+        ),
     )(x)
 
 
@@ -101,34 +110,41 @@
     lanes = 128
     rows = -(-packed.shape[0] // (8 * lanes)) * 8
     packed = jnp.pad(packed, (0, rows * lanes - packed.shape[0])).reshape(rows, lanes)
-    packed = jnp.sum(exchange(jnp.broadcast_to(packed, (replicas, rows, lanes)), 0), axis=0)
+    packed = jnp.sum(exchange(jnp.broadcast_to(packed, (replicas, rows, lanes)), "replica", 0), axis=0)
     packed = packed.reshape(-1)
     left_sum = packed[: left_terms.size].reshape(left_terms.shape)
     vector_total = packed[left_terms.size : left_terms.size + vector_len]
     left_rows = jnp.einsum("kmr,krs->kms", left_sum, gram_root, precision=highest).astype(
         jnp.bfloat16
     )
+    owners_count = lax.axis_size("mp")
     right_terms = jnp.einsum(
-        "kmn,kms->kns", compensated, left_rows, preferred_element_type=jnp.float32
+        "kmn,kms->ksn", compensated, left_rows, preferred_element_type=jnp.float32
     )
-    right_part = lax.psum_scatter(right_terms.reshape(-1), "mp", scatter_dimension=0, tiled=True)
+    right_slots = right_terms.reshape(owners_count, -1, right_terms.shape[2])
+    right_part = jnp.sum(exchange(right_slots, "mp", 1), axis=0)
+    part_shape = right_part.shape
     right_part = right_part.reshape(replicas, -1, lanes)
-    right_chunk = jnp.sum(exchange(right_part, 1), axis=0)
-    right_part = exchange(jnp.broadcast_to(right_chunk, right_part.shape), 2).reshape(-1)
-    right_new = lax.all_gather(right_part.astype(jnp.bfloat16), "mp", axis=0, tiled=True).reshape(
-        right_terms.shape
-    )
-    left_all = lax.all_gather(left_rows, "mp", axis=1, tiled=True)
+    right_chunk = jnp.sum(exchange(right_part, "replica", 2), axis=0)
+    right_part = exchange(jnp.broadcast_to(right_chunk, right_part.shape), "replica", 3)
+    right_part = right_part.reshape(part_shape).astype(jnp.bfloat16)
+    right_new = exchange(
+        jnp.broadcast_to(right_part, right_slots.shape), "mp", 4
+    ).reshape(right_terms.shape)
+    pairs = [
+        (a * owners_count + b, b * owners_count + a)
+        for a in range(replicas)
+        for b in range(owners_count)
+    ]
+    left_block = lax.ppermute(left_rows, ("replica", "mp"), pairs)
     approx_rows = jnp.einsum(
-        "kms,kns->kmn", left_rows, right_new, preferred_element_type=jnp.float32
+        "kms,ksn->kmn", left_rows, right_new, preferred_element_type=jnp.float32
     )
     new_feedback = (compensated.astype(jnp.float32) - approx_rows).astype(jnp.bfloat16)
     scale = has.astype(jnp.float32)[:, None, None]
-    left_chosen = lax.dynamic_slice_in_dim(
-        left_all[chosen], replica_index * replica_rows, replica_rows, 1
-    ).astype(jnp.float32) * scale
+    left_chosen = left_block[chosen].astype(jnp.float32) * scale
     right_chosen = right_new[chosen].astype(jnp.float32) * scale
-    approx_slots = jnp.einsum("cmr,cnr->cmn", left_chosen, right_chosen, precision=highest)
+    approx_slots = jnp.einsum("cmr,crn->cmn", left_chosen, right_chosen, precision=highest)
     new_momentum = 0.9 * momentum[0] + approx_slots
     new_master = master_weights[0] - 0.1 * new_momentum
     master_narrow = new_master.astype(jnp.bfloat16)

time: 333 us -> 245 us (0.74)
  waiting for transfers between devices: 175 us -> 49.9 us
  Pallas kernels: 57 us -> 141 us
  blocking collectives: 21.1 us -> 0 us
  local copies, waits for them, and re-layouts: 27.8 us -> 8.79 us
  matrix products: 23.5 us -> 14.8 us
    unnamed x4 -> x1, waiting for transfers between devices: 103 us -> 0.02 us
    pallas_call x3 -> x5, Pallas kernels: 57 us -> 141 us  [exchange(): pl.pallas_call(functools.partial(_exchange_kernel, n, axis), out_shape=ja...]
    all_gather x1 -> x0, blocking collectives: 21.1 us -> none  [per_device(): left_all = lax.all_gather(left_rows, 'mp', axis=1, tiled=True)]
    all_gather x1 -> x0, waiting for transfers between devices: 20.7 us -> none  [per_device(): lax.all_gather(right_part.astype(jnp.bfloat16), 'mp', axis=0, tiled=True)]
    reshape x2 -> x0, local copies, waits for them, and re-layouts: 17.2 us -> none  [the longest x1 9.41 us: per_device(): right_terms.reshape(-1)]
    dot_general x3, matrix products: 19.9 us -> 11.2 us  [the longest x1 4.72 us: per_device(): jnp.einsum('kmn,kms->ksn', compensated, left_rows, preferred_element_type...]
  transfers between devices with their start and end apart: 3 -> 2, of which waited for: 3 -> 1; matrix products, arithmetic and copies ran while one was open for 3% -> 6% of each run, Pallas kernels for 0% -> 46%
where the time goes in v3:
time: 245 us
  Pallas kernels  141 us (58%)
  waiting for transfers between devices  49.9 us (20%)
  between operations  16.9 us (7%)
  matrix products  14.8 us (6%)
  other arithmetic  9.57 us (4%)
  local copies, waits for them, and re-layouts  8.79 us (4%)
  starting transfers between devices  3.05 us (1%)
    pallas_call x5, Pallas kernels, exchange(): pl.pallas_call(functools.partial(_exchange_kernel, n, axis), out_shape=ja...  141 us
    all_gather x1, waiting for transfers between devices, per_device(): weight_slots = lax.all_gather(master_narrow, 'mp', axis=0, tiled=True)  49.9 us
  transfers between devices with their start and end apart: 2, of which 1 were waited for; matrix products, arithmetic and copies ran while one was open for 6% of the time, Pallas kernels for 46%

profile of v3, /device:TPU:1, one launch (start us, length us, event | category | flops | bytes accessed | tf_op | source)
XLA Modules:
  0.0 244.6 jit_solution(14524572441629542579)
XLA Ops:
  7.2 0.0 copy-start
  7.2 0.0 all-gather.3.cloned.1.call-start
  7.2 1.3 copy-done
  8.6 3.2 %fusion.19 = f32[8,48,32]{2,1,0:T(8,128)S(1)} fusion(bf16[8,3072,32]{1,2,0:T(8,128)(2,1)S(1)} %copy-done, bf16[1,8,48,3072]{3,2,1,0:T(8,128)(2,1)} %param.11, bf16[1,8,48,3072]{3,2,1,0:T(8,128)(2,1)} %param.10), kind=kOutput, calls=%fused_computation.37 | convolution fusion | flops 80216064 | bytes 6340608 | tf_op jit(solution)/shard_map/kmn,knr->kmr/dot_general | solution.py:104
  11.8 0.0 copy-start.3
  11.8 0.1 reshape.113
  11.9 0.1 broadcast_in_dim.40.x_ref
  12.0 28.9 %shard_map.145 = f32[16,104,128]{2,1,0:T(8,128)S(1)} custom-call(f32[16,104,128]{2,1,0:T(8,128)S(1)} %broadcast_in_dim.40.x_ref), custom_call_target="tpu_custom_call" | custom-call | tf_op jit(solution)/shard_map/pallas_call | solution.py:59
  41.0 0.1 reshape.115
  41.1 0.5 convolution_convert_fusion
  41.6 3.0 %collective-permute-start = (bf16[8,48,32]{1,2,0:T(8,128)(2,1)S(1)}, bf16[8,48,32]{1,2,0:T(8,128)(2,1)S(1)}, u32[]{:S(2)}, u32[]{:S(2)}) collective-permute-start(bf16[8,48,32]{1,2,0:T(8,128)(2,1)S(1)} %convolution_convert_fusion), channel_id=1, source_target_pairs={{0,0},{1,16},{2,32},{3,48},{4,64},{5,80},{6,96},{7,112},{8,128},{9... | collective-permute-start | bytes 73736 | tf_op jit(solution)/shard_map/ppermute | solution.py:139
  44.6 4.7 %fusion.17 = f32[8,32,3072]{2,1,0:T(8,128)} fusion(bf16[8,48,32]{1,2,0:T(8,128)(2,1)S(1)} %convolution_convert_fusion, bf16[1,8,48,3072]{3,2,1,0:T(8,128)(2,1)} %param.11, bf16[1,8,48,3072]{3,2,1,0:T(8,128)(2,1)} %param.10), kind=kOutput, calls=%fused_computation.36 | convolution fusion | flops 80216064 | bytes 7888896 | tf_op jit(solution)/shard_map/kmn,kms->ksn/dot_general | solution.py:121
  49.4 0.1 convert_reduce_fusion
  49.4 0.7 bitcast_reduce_fusion
  50.1 0.6 compare_and_fusion
  52.0 60.8 %shard_map.146 = f32[16,16,3072]{2,1,0:T(8,128)S(1)} custom-call(f32[16,16,3072]{2,1,0:T(8,128)} %bitcast.49), custom_call_target="tpu_custom_call" | custom-call | tf_op jit(solution)/shard_map/pallas_call | solution.py:59
  112.8 1.7 copy-done.1
  114.5 2.1 reduce_sum.37
  116.6 11.2 %shard_map.147 = f32[16,24,128]{2,1,0:T(8,128)S(1)} custom-call(f32[16,24,128]{2,1,0:T(8,128)S(1)} %bitcast.48), custom_call_target="tpu_custom_call" | custom-call | tf_op jit(solution)/shard_map/pallas_call | solution.py:59
  127.8 11.6 %shard_map.148 = f32[16,24,128]{2,1,0:T(8,128)S(1)} custom-call(f32[16,24,128]{2,1,0:T(8,128)S(1)} %broadcast_in_dim.41.x_ref), custom_call_target="tpu_custom_call" | custom-call | tf_op jit(solution)/shard_map/pallas_call | solution.py:59
  139.5 0.2 broadcast_in_dim.42.x_ref
  139.6 29.0 %shard_map.149 = bf16[16,16,3072]{2,1,0:T(8,128)(2,1)S(1)} custom-call(bf16[16,16,3072]{2,1,0:T(8,128)(2,1)S(1)} %broadcast_in_dim.42.x_ref), custom_call_target="tpu_custom_call" | custom-call | tf_op jit(solution)/shard_map/pallas_call | solution.py:59
  170.0 1.7 convolution_add_fusion
  171.8 0.0 copy-start.2
  171.8 0.8 copy-done.2
  172.6 2.0 fusion.5
  174.7 0.0 all-gather.3.cloned.1.call-update
  174.7 0.6 multiply_subtract_fusion
  175.3 4.7 %fusion = bf16[1,8,48,3072]{3,2,1,0:T(8,128)(2,1)} fusion(bf16[8,48,32]{1,2,0:T(8,128)(2,1)S(1)} %convolution_convert_fusion, bf16[8,32,3072]{2,1,0:T(8,128)(2,1)S(1)} %bitcast.47, bf16[1,8,48,3072]{3,2,1,0:T(8,128)(2,1)} %param.11, bf16[1,8,48,3072]{3,2,1,0:T(8,128)(2,1)} %param.10), kind=kOutput, calls=%fused_computation.3 | convolution fusion | flops 83755008 | bytes 8675328 | tf_op jit(solution)/shard_map/kms,ksn->kmn/dot_general | solution.py:140
  180.0 49.9 %all-gather.3.cloned.1.call-done = bf16[768,3072]{1,0:T(8,128)(2,1)} async-done(((bf16[48,3072]{1,0:T(8,128)(2,1)}), bf16[768,3072]{1,0:T(8,128)(2,1)}) %all-gather.3.cloned.1.call-update) | async-done | bytes 4718608 | tf_op jit(solution)/shard_map/all_gather | solution.py:151
  229.9 4.4 %gather_fusion = bf16[8,48,3072]{2,1,0:T(8,128)(2,1)} fusion(bf16[16,48,3072]{2,1,0:T(8,128)(2,1)} %bitcast.51, s32[1024]{0:T(1024)S(1)} %pad_clamp_fusion), kind=kCustom, calls=%fused_computation | custom fusion | bytes 4718624 | tf_op jit(solution)/shard_map/jit(_take)/gather | solution.py:152
  234.4 3.4 %broadcast_select_fusion = bf16[8,48,3072]{2,1,0:T(8,128)(2,1)} fusion(bf16[8,48,3072]{2,1,0:T(8,128)(2,1)} %gather_fusion, pred[8]{0:T(512)(128)(4,1)S(1)} %get-tuple-element.32), kind=kLoop, calls=%fused_computation.6 | loop fusion | flops 1179648 | bytes 4718600 | tf_op jit(solution)/shard_map/jit(_take)/select_n | solution.py:152
  (21 shorter events, 0.2 us)
Async XLA Ops:
  7.2 1.4 copy-start
  7.2 4.7 %copy-start.6 = (f32[1,672]{1,0:T(1,128)S(1)}, f32[1,672]{1,0:T(1,128)}, u32[]{:S(2)}) copy-start(f32[1,672]{1,0:T(1,128)} %param.17) | copy-start | bytes 8068
  7.2 222.7 %all-gather.3.cloned.1.call-start = ((), (), s32[]{:S(2)}) async-start(), calls=%async_computation | async-start | bytes 5013504 | tf_op jit(solution)/shard_map/all_gather | solution.py:151
  11.8 29.3 %copy-start.3 = (f32[8,32,32]{2,1,0:T(8,128)S(1)}, f32[8,32,32]{2,1,0:T(8,128)}, u32[]{:S(2)}) copy-start(f32[8,32,32]{2,1,0:T(8,128)} %param.13) | copy-start | bytes 98308
  41.6 128.4 %collective-permute-start = (bf16[8,48,32]{1,2,0:T(8,128)(2,1)S(1)}, bf16[8,48,32]{1,2,0:T(8,128)(2,1)S(1)}, u32[]{:S(2)}, u32[]{:S(2)}) collective-permute-start(bf16[8,48,32]{1,2,0:T(8,128)(2,1)S(1)} %convolution_convert_fusion), channel_id=1, source_target_pairs={{0,0},{1,16},{2,32},{3,48},{4,64},{5,80},{6,96},{7,112},{8,128},{9... | collective-permute-start | bytes 73736 | tf_op jit(solution)/shard_map/ppermute | solution.py:139
  44.6 4.7 %copy-start.7 = (s32[8]{0:T(128)S(1)}, s32[8]{0:T(128)}, u32[]{:S(2)}) copy-start(s32[8]{0:T(128)} %param.14) | copy-start | bytes 100
  112.8 1.7 copy-start.1
  168.7 6.0 %copy-start.4 = (f32[672]{0:T(1024)S(1)}, f32[672]{0:T(1024)}, u32[]{:S(2)}) copy-start(f32[672]{0:T(1024)} %param.19) | copy-start | bytes 8068
  168.7 6.0 %copy-start.5 = (f32[672]{0:T(1024)S(1)}, f32[672]{0:T(1024)}, u32[]{:S(2)}) copy-start(f32[672]{0:T(1024)} %param.18) | copy-start | bytes 8068
  171.8 0.8 copy-start.2
Sparse Core Ops, SparseCore 0:
  174.8 55.0 all-gather.2

commit v4 on v3

--- a/solution.py
+++ b/solution.py
@@ -101,6 +101,8 @@
     mine = slots[None, :] == (mp_index * capacity + jnp.arange(capacity))[:, None]
     has = jnp.any(mine, axis=1)
     chosen = jnp.argmax(mine, axis=1)
+    weight_base = master_weights[0] - 0.1 * (0.9 * momentum[0])
+    weight_slots = lax.all_gather(weight_base.astype(jnp.bfloat16), "mp", axis=0, tiled=True)
     left_terms = jnp.einsum(
         "kmn,knr->kmr", compensated, right_init, preferred_element_type=jnp.float32
     )
@@ -147,9 +149,12 @@
     approx_slots = jnp.einsum("cmr,crn->cmn", left_chosen, right_chosen, precision=highest)
     new_momentum = 0.9 * momentum[0] + approx_slots
     new_master = master_weights[0] - 0.1 * new_momentum
-    master_narrow = new_master.astype(jnp.bfloat16)
-    weight_slots = lax.all_gather(master_narrow, "mp", axis=0, tiled=True)
-    new_weights = jnp.take(weight_slots, slots, axis=0)
+    block_approx = jnp.einsum(
+        "kms,ksn->kmn", left_block, right_new, preferred_element_type=jnp.float32
+    )
+    new_weights = (
+        jnp.take(weight_slots, slots, axis=0).astype(jnp.float32) - 0.1 * block_approx
+    ).astype(jnp.bfloat16)
     new_vector_momentum = 0.9 * vector_momentum + vector_total
     new_vector_params = vector_params - 0.1 * new_vector_momentum
     return (

time: 245 us -> 201 us (0.82)
  waiting for transfers between devices: 49.9 us -> 0.02 us
  Pallas kernels: 141 us -> 148 us
    all_gather x1, waiting for transfers between devices: 49.9 us -> 0.01 us  [per_device(): lax.all_gather(weight_base.astype(jnp.bfloat16), 'mp', axis=0, tiled=True)]
    pallas_call x5, Pallas kernels: 141 us -> 148 us  [exchange(): pl.pallas_call(functools.partial(_exchange_kernel, n, axis), out_shape=ja...]
    dot_general x0 -> x1, matrix products: none -> 4.05 us  [per_device(): jnp.einsum('kms,ksn->kmn', left_block, right_new, preferred_element_type=...]
    select_n x1 -> x0, other arithmetic: 3.36 us -> none  [per_device(): new_weights = jnp.take(weight_slots, slots, axis=0)]
  transfers between devices with their start and end apart: 2 -> 2, of which waited for: 1 -> 0; matrix products, arithmetic and copies ran while one was open for 6% -> 10% of each run, Pallas kernels for 46% -> 74%
where the time goes in v4:
time: 201 us; the launch traced here: 200 us
  Pallas kernels  148 us (74%)
  between operations  16.9 us (8%)
  matrix products  16.5 us (8%)
  other arithmetic  8.24 us (4%)
  local copies, waits for them, and re-layouts  7.46 us (4%)
  starting transfers between devices  3.05 us (2%)
    pallas_call x5, Pallas kernels, exchange(): pl.pallas_call(functools.partial(_exchange_kernel, n, axis), out_shape=ja...  148 us
    dot_general x1, matrix products, per_device(): jnp.einsum('kmn,kms->ksn', compensated, left_rows, preferred_element_type...  4.73 us
    gather x1, local copies, waits for them, and re-layouts, per_device(): jnp.take(weight_slots, slots, axis=0).astype(jnp.float32)  4.44 us
    dot_general x1, matrix products, per_device(): jnp.einsum('kms,ksn->kmn', left_block, right_new, preferred_element_type=...  4.05 us
  transfers between devices with their start and end apart: 2, of which 0 were waited for; matrix products, arithmetic and copies ran while one was open for 10% of the time, Pallas kernels for 74%

profile of v4, /device:TPU:1, one launch (start us, length us, event | category | flops | bytes accessed | tf_op | source)
XLA Modules:
  0.0 200.3 jit_solution(15552108585746097845)
XLA Ops:
  7.2 0.0 copy-start
  7.2 0.0 all-gather.3.cloned.1.call-start
  7.2 2.1 %subtract_convert_fusion.2 = bf16[1,1,48,3072]{3,2,1,0:T(8,128)(2,1)} fusion(f32[1,1,48,3072]{3,2,1,0:T(8,128)} %param.16, f32[1,1,48,3072]{3,2,1,0:T(8,128)} %param.15), kind=kLoop, calls=%fused_computation.10 | loop fusion | flops 442368 | bytes 1474560 | tf_op jit(solution)/shard_map/convert_element_type | solution.py:105
  9.4 0.0 all-gather.3.cloned.1.call-update
  9.4 0.0 copy-start.8
  9.4 3.2 %fusion.18 = f32[8,48,32]{2,1,0:T(8,128)S(1)} fusion(bf16[8,3072,32]{1,2,0:T(8,128)(2,1)S(1)} %copy-done, bf16[1,8,48,3072]{3,2,1,0:T(8,128)(2,1)} %param.11, bf16[1,8,48,3072]{3,2,1,0:T(8,128)(2,1)} %param.10), kind=kOutput, calls=%fused_computation.37 | convolution fusion | flops 80216064 | bytes 6340608 | tf_op jit(solution)/shard_map/kmn,knr->kmr/dot_general | solution.py:106
  12.6 0.1 reshape.144
  12.8 0.1 broadcast_in_dim.40.x_ref
  12.8 28.9 %shard_map.145 = f32[16,104,128]{2,1,0:T(8,128)S(1)} custom-call(f32[16,104,128]{2,1,0:T(8,128)S(1)} %broadcast_in_dim.40.x_ref), custom_call_target="tpu_custom_call" | custom-call | tf_op jit(solution)/shard_map/pallas_call | solution.py:59
  41.8 0.1 reshape.146
  41.9 0.5 convolution_convert_fusion
  42.4 3.0 %collective-permute-start = (bf16[8,48,32]{1,2,0:T(8,128)(2,1)S(1)}, bf16[8,48,32]{1,2,0:T(8,128)(2,1)S(1)}, u32[]{:S(2)}, u32[]{:S(2)}) collective-permute-start(bf16[8,48,32]{1,2,0:T(8,128)(2,1)S(1)} %convolution_convert_fusion), channel_id=1, source_target_pairs={{0,0},{1,16},{2,32},{3,48},{4,64},{5,80},{6,96},{7,112},{8,128},{9... | collective-permute-start | bytes 73736 | tf_op jit(solution)/shard_map/ppermute | solution.py:141
  45.4 4.7 %fusion.16 = f32[8,32,3072]{2,1,0:T(8,128)} fusion(bf16[8,48,32]{1,2,0:T(8,128)(2,1)S(1)} %convolution_convert_fusion, bf16[1,8,48,3072]{3,2,1,0:T(8,128)(2,1)} %param.11, bf16[1,8,48,3072]{3,2,1,0:T(8,128)(2,1)} %param.10), kind=kOutput, calls=%fused_computation.36 | convolution fusion | flops 80216064 | bytes 7888896 | tf_op jit(solution)/shard_map/kmn,kms->ksn/dot_general | solution.py:123
  50.2 68.3 %shard_map.146 = f32[16,16,3072]{2,1,0:T(8,128)S(1)} custom-call(f32[16,16,3072]{2,1,0:T(8,128)} %bitcast.50), custom_call_target="tpu_custom_call" | custom-call | tf_op jit(solution)/shard_map/pallas_call | solution.py:59
  118.4 1.7 copy-done.1
  120.1 2.1 %reduce_sum.37 = f32[16,3072]{1,0:T(8,128)S(1)} reduce(f32[16,16,3072]{2,1,0:T(8,128)} %copy-done.1, f32[]{:T(128)} %constant.12.clone.1), dimensions={0}, to_apply=%region_1.0 | reduce | flops 737280 | bytes 3342340 | tf_op jit(solution)/shard_map/reduce_sum | solution.py:127
  122.2 13.7 %shard_map.147 = f32[16,24,128]{2,1,0:T(8,128)S(1)} custom-call(f32[16,24,128]{2,1,0:T(8,128)S(1)} %bitcast.49), custom_call_target="tpu_custom_call" | custom-call | tf_op jit(solution)/shard_map/pallas_call | solution.py:59
  136.0 11.6 %shard_map.148 = f32[16,24,128]{2,1,0:T(8,128)S(1)} custom-call(f32[16,24,128]{2,1,0:T(8,128)S(1)} %broadcast_in_dim.41.x_ref), custom_call_target="tpu_custom_call" | custom-call | tf_op jit(solution)/shard_map/pallas_call | solution.py:59
  147.6 0.0 copy-start.6
  147.6 0.0 copy-start.7
  147.7 0.2 broadcast_in_dim.42.x_ref
  147.9 25.6 %shard_map.149 = bf16[16,16,3072]{2,1,0:T(8,128)(2,1)S(1)} custom-call(bf16[16,16,3072]{2,1,0:T(8,128)(2,1)S(1)} %broadcast_in_dim.42.x_ref), custom_call_target="tpu_custom_call" | custom-call | tf_op jit(solution)/shard_map/pallas_call | solution.py:59
  173.5 0.1 convert_reduce_fusion
  173.6 0.7 bitcast_reduce_fusion
  174.2 0.6 compare_and_fusion
  174.9 0.6 multiply_subtract_fusion
  175.5 2.3 %fusion = bf16[1,8,48,3072]{3,2,1,0:T(8,128)(2,1)} fusion(bf16[8,48,32]{1,2,0:T(8,128)(2,1)S(1)} %convolution_convert_fusion, bf16[8,32,3072]{2,1,0:T(8,128)(2,1)S(1)} %bitcast.46, bf16[1,8,48,3072]{3,2,1,0:T(8,128)(2,1)S(1)} %copy-done.2, bf16[1,8,48,3072]{3,2,1,0:T(8,128)(2,1)S(1)} %copy-done.3), kind=kOutput, calls=%fused_computation.4 | convolution fusion | flops 83755008 | bytes 8675328 | tf_op jit(solution)/shard_map/kms,ksn->kmn/dot_general | solution.py:142
  180.4 1.7 convolution_add_fusion
  182.2 0.8 copy-done.4
  183.0 1.9 fusion.2
  184.9 4.4 %gather_fusion = bf16[8,48,3072]{2,1,0:T(8,128)(2,1)} fusion(bf16[16,48,3072]{2,1,0:T(8,128)(2,1)} %bitcast.52, s32[1024]{0:T(1024)S(1)} %pad_clamp_fusion), kind=kCustom, calls=%fused_computation | custom fusion | bytes 4718624 | tf_op jit(solution)/shard_map/jit(_take)/gather | solution.py:156
  189.4 4.0 %subtract_convert_fusion = bf16[8,48,3072]{2,1,0:T(8,128)(2,1)} fusion(bf16[8,48,32]{1,2,0:T(8,128)(2,1)S(1)} %collective-permute-done, bf16[8,32,3072]{2,1,0:T(8,128)(2,1)S(1)} %bitcast.48, bf16[8,48,3072]{2,1,0:T(8,128)(2,1)} %gather_fusion, pred[8]{0:T(512)(128)(4,1)S(1)} %get-tuple-element.32), kind=kOutput, calls=%fused_computation.1 | convolution fusion | flops 81395712 | bytes 6316040 | tf_op jit(solution)/shard_map/kms,ksn->kmn/dot_general | solution.py:152
  (26 shorter events, 0.2 us)
Async XLA Ops:
  7.2 2.2 %copy-start = (bf16[8,3072,32]{1,2,0:T(8,128)(2,1)S(1)}, bf16[8,3072,32]{1,2,0:T(8,128)(2,1)}, u32[]{:S(2)}) copy-start(bf16[8,3072,32]{1,2,0:T(8,128)(2,1)} %param.12) | copy-start | bytes 4718596
  7.2 177.7 %all-gather.3.cloned.1.call-start = ((), (), s32[]{:S(2)}) async-start(), calls=%async_computation | async-start | bytes 5013504 | tf_op jit(solution)/shard_map/all_gather | solution.py:105
  9.4 3.3 %copy-start.8 = (f32[1,672]{1,0:T(1,128)S(1)}, f32[1,672]{1,0:T(1,128)}, u32[]{:S(2)}) copy-start(f32[1,672]{1,0:T(1,128)} %param.17) | copy-start | bytes 8068
  12.6 29.3 %copy-start.5 = (f32[8,32,32]{2,1,0:T(8,128)S(1)}, f32[8,32,32]{2,1,0:T(8,128)}, u32[]{:S(2)}) copy-start(f32[8,32,32]{2,1,0:T(8,128)} %param.13) | copy-start | bytes 98308
  42.4 138.0 %collective-permute-start = (bf16[8,48,32]{1,2,0:T(8,128)(2,1)S(1)}, bf16[8,48,32]{1,2,0:T(8,128)(2,1)S(1)}, u32[]{:S(2)}, u32[]{:S(2)}) collective-permute-start(bf16[8,48,32]{1,2,0:T(8,128)(2,1)S(1)} %convolution_convert_fusion), channel_id=1, source_target_pairs={{0,0},{1,16},{2,32},{3,48},{4,64},{5,80},{6,96},{7,112},{8,128},{9... | collective-permute-start | bytes 73736 | tf_op jit(solution)/shard_map/ppermute | solution.py:141
  118.4 1.7 copy-start.1
  147.6 25.8 %copy-start.9 = (s32[8]{0:T(128)S(1)}, s32[8]{0:T(128)}, u32[]{:S(2)}) copy-start(s32[8]{0:T(128)} %param.14) | copy-start | bytes 100
  147.6 27.2 %copy-start.6 = (f32[672]{0:T(1024)S(1)}, f32[672]{0:T(1024)}, u32[]{:S(2)}) copy-start(f32[672]{0:T(1024)} %param.19) | copy-start | bytes 8068
  147.6 27.2 %copy-start.7 = (f32[672]{0:T(1024)S(1)}, f32[672]{0:T(1024)}, u32[]{:S(2)}) copy-start(f32[672]{0:T(1024)} %param.18) | copy-start | bytes 8068
  147.7 27.8 %copy-start.2 = (bf16[1,8,48,3072]{3,2,1,0:T(8,128)(2,1)S(1)}, bf16[1,8,48,3072]{3,2,1,0:T(8,128)(2,1)}, u32[]{:S(2)}) copy-start(bf16[1,8,48,3072]{3,2,1,0:T(8,128)(2,1)} %param.11) | copy-start | bytes 7077892
  147.7 27.8 %copy-start.3 = (bf16[1,8,48,3072]{3,2,1,0:T(8,128)(2,1)S(1)}, bf16[1,8,48,3072]{3,2,1,0:T(8,128)(2,1)}, u32[]{:S(2)}) copy-start(bf16[1,8,48,3072]{3,2,1,0:T(8,128)(2,1)} %param.10) | copy-start | bytes 7077892
  182.2 0.8 copy-start.4
Sparse Core Ops, SparseCore 0:
  11.0 99.3 all-gather.2

commit v5 on v4

--- a/solution.py
+++ b/solution.py
@@ -124,7 +124,9 @@
         "kmn,kms->ksn", compensated, left_rows, preferred_element_type=jnp.float32
     )
     right_slots = right_terms.reshape(owners_count, -1, right_terms.shape[2])
-    right_part = jnp.sum(exchange(right_slots, "mp", 1), axis=0)
+    right_part = jnp.sum(
+        exchange(right_slots.astype(jnp.bfloat16), "mp", 1).astype(jnp.float32), axis=0
+    )
     part_shape = right_part.shape
     right_part = right_part.reshape(replicas, -1, lanes)
     right_chunk = jnp.sum(exchange(right_part, "replica", 2), axis=0)

time: 201 us -> 167 us (0.83)
  Pallas kernels: 148 us -> 120 us
    pallas_call x5, Pallas kernels: 148 us -> 120 us  [exchange(): pl.pallas_call(functools.partial(_exchange_kernel, n, axis), out_shape=ja...]
  transfers between devices with their start and end apart: 2 -> 2, of which waited for: 0 -> 0; matrix products, arithmetic and copies ran while one was open for 10% -> 9% of each run, Pallas kernels for 74% -> 72%
where the time goes in v5:
time: 167 us
  Pallas kernels  120 us (72%)
  between operations  16.9 us (10%)
  matrix products  14.9 us (9%)
  other arithmetic  6.41 us (4%)
  local copies, waits for them, and re-layouts  5.8 us (3%)
  starting transfers between devices  3.05 us (2%)
    pallas_call x5, Pallas kernels, exchange(): pl.pallas_call(functools.partial(_exchange_kernel, n, axis), out_shape=ja...  120 us
    gather x1, local copies, waits for them, and re-layouts, per_device(): jnp.take(weight_slots, slots, axis=0).astype(jnp.float32)  4.44 us
    dot_general x1, matrix products, per_device(): jnp.einsum('kms,ksn->kmn', left_block, right_new, preferred_element_type=...  4.05 us
  transfers between devices with their start and end apart: 2, of which 0 were waited for; matrix products, arithmetic and copies ran while one was open for 9% of the time, Pallas kernels for 72%

profile of v5, /device:TPU:1, one launch (start us, length us, event | category | flops | bytes accessed | tf_op | source)
XLA Modules:
  0.0 167.0 jit_solution(6468200929615310441)
XLA Ops:
  7.2 0.0 copy-start
  7.2 0.0 all-gather.3.cloned.1.call-start
  7.2 2.1 %subtract_convert_fusion.2 = bf16[1,1,48,3072]{3,2,1,0:T(8,128)(2,1)} fusion(f32[1,1,48,3072]{3,2,1,0:T(8,128)} %param.16, f32[1,1,48,3072]{3,2,1,0:T(8,128)} %param.15), kind=kLoop, calls=%fused_computation.12 | loop fusion | flops 442368 | bytes 1474560 | tf_op jit(solution)/shard_map/convert_element_type | solution.py:105
  9.4 0.0 all-gather.3.cloned.1.call-update
  9.4 0.0 copy-start.7
  9.4 3.2 %fusion.17 = f32[8,48,32]{2,1,0:T(8,128)S(1)} fusion(bf16[8,3072,32]{1,2,0:T(8,128)(2,1)S(1)} %copy-done, bf16[1,8,48,3072]{3,2,1,0:T(8,128)(2,1)} %param.11, bf16[1,8,48,3072]{3,2,1,0:T(8,128)(2,1)} %param.10), kind=kOutput, calls=%fused_computation.38 | convolution fusion | flops 80216064 | bytes 6340608 | tf_op jit(solution)/shard_map/kmn,knr->kmr/dot_general | solution.py:106
  12.6 0.1 reshape.143
  12.8 0.1 broadcast_in_dim.40.x_ref
  12.8 28.9 %shard_map.145 = f32[16,104,128]{2,1,0:T(8,128)S(1)} custom-call(f32[16,104,128]{2,1,0:T(8,128)S(1)} %broadcast_in_dim.40.x_ref), custom_call_target="tpu_custom_call" | custom-call | tf_op jit(solution)/shard_map/pallas_call | solution.py:59
  41.8 0.1 reshape.145
  41.9 0.5 convolution_convert_fusion.1
  42.4 3.0 %collective-permute-start = (bf16[8,48,32]{1,2,0:T(8,128)(2,1)S(1)}, bf16[8,48,32]{1,2,0:T(8,128)(2,1)S(1)}, u32[]{:S(2)}, u32[]{:S(2)}) collective-permute-start(bf16[8,48,32]{1,2,0:T(8,128)(2,1)S(1)} %convolution_convert_fusion.1), channel_id=1, source_target_pairs={{0,0},{1,16},{2,32},{3,48},{4,64},{5,80},{6,96},{7,112},{8,128},{9... | collective-permute-start | bytes 73736 | tf_op jit(solution)/shard_map/ppermute | solution.py:143
  45.4 3.1 %convolution_convert_fusion = bf16[8,32,3072]{2,1,0:T(8,128)(2,1)S(1)} fusion(bf16[8,48,32]{1,2,0:T(8,128)(2,1)S(1)} %convolution_convert_fusion.1, bf16[1,8,48,3072]{3,2,1,0:T(8,128)(2,1)} %param.11, bf16[1,8,48,3072]{3,2,1,0:T(8,128)(2,1)} %param.10), kind=kOutput, calls=%fused_computation.5 | convolution fusion | flops 81002496 | bytes 6316032 | tf_op jit(solution)/shard_map/kmn,kms->ksn/dot_general | solution.py:123
  48.5 41.3 %shard_map.146 = bf16[16,16,3072]{2,1,0:T(8,128)(2,1)S(1)} custom-call(bf16[16,16,3072]{2,1,0:T(8,128)(2,1)S(1)} %bitcast.49), custom_call_target="tpu_custom_call" | custom-call | tf_op jit(solution)/shard_map/pallas_call | solution.py:59
  89.8 0.2 convert_reduce_fusion
  90.1 13.0 %shard_map.147 = f32[16,24,128]{2,1,0:T(8,128)S(1)} custom-call(f32[16,24,128]{2,1,0:T(8,128)S(1)} %bitcast.50), custom_call_target="tpu_custom_call" | custom-call | tf_op jit(solution)/shard_map/pallas_call | solution.py:59
  103.1 10.5 %shard_map.148 = f32[16,24,128]{2,1,0:T(8,128)S(1)} custom-call(f32[16,24,128]{2,1,0:T(8,128)S(1)} %broadcast_in_dim.41.x_ref), custom_call_target="tpu_custom_call" | custom-call | tf_op jit(solution)/shard_map/pallas_call | solution.py:59
  113.7 0.0 copy-start.5
  113.7 0.0 copy-start.6
  113.7 0.2 broadcast_in_dim.42.x_ref
  113.9 26.3 %shard_map.149 = bf16[16,16,3072]{2,1,0:T(8,128)(2,1)S(1)} custom-call(bf16[16,16,3072]{2,1,0:T(8,128)(2,1)S(1)} %broadcast_in_dim.42.x_ref), custom_call_target="tpu_custom_call" | custom-call | tf_op jit(solution)/shard_map/pallas_call | solution.py:59
  140.2 0.1 convert_reduce_fusion.1
  140.3 0.7 bitcast_reduce_fusion
  141.0 0.6 compare_and_fusion
  141.6 0.6 multiply_subtract_fusion
  142.2 2.3 %fusion = bf16[1,8,48,3072]{3,2,1,0:T(8,128)(2,1)} fusion(bf16[8,48,32]{1,2,0:T(8,128)(2,1)S(1)} %convolution_convert_fusion.1, bf16[8,32,3072]{2,1,0:T(8,128)(2,1)S(1)} %bitcast.46, bf16[1,8,48,3072]{3,2,1,0:T(8,128)(2,1)S(1)} %copy-done.1, bf16[1,8,48,3072]{3,2,1,0:T(8,128)(2,1)S(1)} %copy-done.2), kind=kOutput, calls=%fused_computation.4 | convolution fusion | flops 83755008 | bytes 8675328 | tf_op jit(solution)/shard_map/kms,ksn->kmn/dot_general | solution.py:144
  147.2 1.7 %convolution_add_fusion = f32[48,3072]{1,0:T(8,128)S(1)} fusion(f32[1,1,48,3072]{3,2,1,0:T(8,128)} %param.15, bf16[8,32,3072]{2,1,0:T(8,128)(2,1)S(1)} %bitcast.47, s32[]{:T(128)} %bitcast.7, f32[]{:T(128)S(6)} %convert_element_type.118, bf16[8,48,32]{1,2,0:T(8,128)(2,1)S(1)} %collective-permute-done), kind=kOutput, calls=%fused_computation.6 | convolution fusion | flops 57117696 | bytes 1386496 | tf_op jit(solution)/shard_map/cmr,crn->cmn/dot_general | solution.py:151
  148.9 0.0 copy-start.3
  148.9 0.8 copy-done.3
  149.7 1.9 %fusion.2 = f32[1,1,48,3072]{3,2,1,0:T(8,128)} fusion(f32[1,1,48,3072]{3,2,1,0:T(8,128)} %param.16, f32[48,3072]{1,0:T(8,128)S(1)} %convolution_add_fusion), kind=kLoop, calls=%fused_computation.11 | loop fusion | flops 294912 | bytes 1769472 | tf_op jit(solution)/shard_map/broadcast_in_dim | solution.py:165
  151.7 4.4 %gather_fusion = bf16[8,48,3072]{2,1,0:T(8,128)(2,1)} fusion(bf16[16,48,3072]{2,1,0:T(8,128)(2,1)} %bitcast.52, s32[1024]{0:T(1024)S(1)} %pad_clamp_fusion), kind=kCustom, calls=%fused_computation | custom fusion | bytes 4718624 | tf_op jit(solution)/shard_map/jit(_take)/gather | solution.py:158
  156.1 4.0 %subtract_convert_fusion = bf16[8,48,3072]{2,1,0:T(8,128)(2,1)} fusion(bf16[8,48,32]{1,2,0:T(8,128)(2,1)S(1)} %collective-permute-done, bf16[8,32,3072]{2,1,0:T(8,128)(2,1)S(1)} %bitcast.48, bf16[8,48,3072]{2,1,0:T(8,128)(2,1)} %gather_fusion, pred[8]{0:T(512)(128)(4,1)S(1)} %get-tuple-element.32), kind=kOutput, calls=%fused_computation.1 | convolution fusion | flops 81395712 | bytes 6316040 | tf_op jit(solution)/shard_map/kms,ksn->kmn/dot_general | solution.py:154
  (24 shorter events, 0.2 us)
Async XLA Ops:
  7.2 2.2 %copy-start = (bf16[8,3072,32]{1,2,0:T(8,128)(2,1)S(1)}, bf16[8,3072,32]{1,2,0:T(8,128)(2,1)}, u32[]{:S(2)}) copy-start(bf16[8,3072,32]{1,2,0:T(8,128)(2,1)} %param.12) | copy-start | bytes 4718596
  7.2 144.5 %all-gather.3.cloned.1.call-start = ((), (), s32[]{:S(2)}) async-start(), calls=%async_computation | async-start | bytes 5013504 | tf_op jit(solution)/shard_map/all_gather | solution.py:105
  9.4 3.3 %copy-start.7 = (f32[1,672]{1,0:T(1,128)S(1)}, f32[1,672]{1,0:T(1,128)}, u32[]{:S(2)}) copy-start(f32[1,672]{1,0:T(1,128)} %param.17) | copy-start | bytes 8068
  12.6 29.3 %copy-start.4 = (f32[8,32,32]{2,1,0:T(8,128)S(1)}, f32[8,32,32]{2,1,0:T(8,128)}, u32[]{:S(2)}) copy-start(f32[8,32,32]{2,1,0:T(8,128)} %param.13) | copy-start | bytes 98308
  42.4 104.7 %collective-permute-start = (bf16[8,48,32]{1,2,0:T(8,128)(2,1)S(1)}, bf16[8,48,32]{1,2,0:T(8,128)(2,1)S(1)}, u32[]{:S(2)}, u32[]{:S(2)}) collective-permute-start(bf16[8,48,32]{1,2,0:T(8,128)(2,1)S(1)} %convolution_convert_fusion.1), channel_id=1, source_target_pairs={{0,0},{1,16},{2,32},{3,48},{4,64},{5,80},{6,96},{7,112},{8,128},{9... | collective-permute-start | bytes 73736 | tf_op jit(solution)/shard_map/ppermute | solution.py:143
  113.7 26.5 %copy-start.8 = (s32[8]{0:T(128)S(1)}, s32[8]{0:T(128)}, u32[]{:S(2)}) copy-start(s32[8]{0:T(128)} %param.14) | copy-start | bytes 100
  113.7 27.9 %copy-start.5 = (f32[672]{0:T(1024)S(1)}, f32[672]{0:T(1024)}, u32[]{:S(2)}) copy-start(f32[672]{0:T(1024)} %param.19) | copy-start | bytes 8068
  113.7 27.9 %copy-start.6 = (f32[672]{0:T(1024)S(1)}, f32[672]{0:T(1024)}, u32[]{:S(2)}) copy-start(f32[672]{0:T(1024)} %param.18) | copy-start | bytes 8068
  113.7 28.5 %copy-start.1 = (bf16[1,8,48,3072]{3,2,1,0:T(8,128)(2,1)S(1)}, bf16[1,8,48,3072]{3,2,1,0:T(8,128)(2,1)}, u32[]{:S(2)}) copy-start(bf16[1,8,48,3072]{3,2,1,0:T(8,128)(2,1)} %param.11) | copy-start | bytes 7077892
  113.7 28.5 %copy-start.2 = (bf16[1,8,48,3072]{3,2,1,0:T(8,128)(2,1)S(1)}, bf16[1,8,48,3072]{3,2,1,0:T(8,128)(2,1)}, u32[]{:S(2)}) copy-start(bf16[1,8,48,3072]{3,2,1,0:T(8,128)(2,1)} %param.10) | copy-start | bytes 7077892
  148.9 0.8 copy-start.3
Sparse Core Ops, SparseCore 0:
  11.0 81.8 all-gather.2

commit v6 on v5

--- a/solution.py
+++ b/solution.py
@@ -69,6 +69,70 @@
         compiler_params=pltpu.CompilerParams(
             collective_id=cid, has_side_effects=True, vmem_limit_bytes=48 * 1024 * 1024
         ),
+    )(x)
+
+
+def _allreduce_kernel(n, x_ref, o_ref, first, middle, second, send_sem, recv_sem):
+    me = lax.axis_index("replica")
+    mp = lax.axis_index("mp")
+    barrier = pltpu.get_barrier_semaphore()
+    for d in range(1, n):
+        peer = lax.rem(me + d, n)
+        pl.semaphore_signal(barrier, inc=1, device_id=(peer, mp), device_id_type=MESH_IDS)
+    pl.semaphore_wait(barrier, n - 1)
+
+    def round_trip(phase, source_of, landing):
+        copies = []
+        for d in range(1, n):
+            peer = lax.rem(me + d, n)
+            copy = pltpu.make_async_remote_copy(
+                src_ref=source_of(peer),
+                dst_ref=landing.at[me],
+                send_sem=send_sem.at[phase, d],
+                recv_sem=recv_sem.at[phase, me],
+                device_id=(peer, mp),
+                device_id_type=MESH_IDS,
+            )
+            copy.start()
+            copies.append(copy)
+        landing[me] = source_of(me)[...]
+        for d in range(1, n):
+            source = lax.rem(me + n - d, n)
+            pltpu.make_async_remote_copy(
+                src_ref=source_of(source),
+                dst_ref=landing.at[source],
+                send_sem=send_sem.at[phase, d],
+                recv_sem=recv_sem.at[phase, source],
+                device_id=(source, mp),
+                device_id_type=MESH_IDS,
+            ).wait_recv()
+        for copy in copies:
+            copy.wait_send()
+
+    round_trip(0, lambda peer: x_ref.at[peer], first)
+    total = first[0]
+    for s in range(1, n):
+        total = total + first[s]
+    middle[...] = total
+    round_trip(1, lambda peer: middle, second)
+    o_ref[...] = second[...]
+
+
+def allreduce_replica(x, cid):
+    n = x.shape[0]
+    return pl.pallas_call(
+        functools.partial(_allreduce_kernel, n),
+        out_shape=jax.ShapeDtypeStruct(x.shape, x.dtype),
+        in_specs=[pl.BlockSpec(memory_space=pltpu.VMEM)],
+        out_specs=pl.BlockSpec(memory_space=pltpu.VMEM),
+        scratch_shapes=[
+            pltpu.VMEM(x.shape, x.dtype),
+            pltpu.VMEM(x.shape[1:], x.dtype),
+            pltpu.VMEM(x.shape, x.dtype),
+            pltpu.SemaphoreType.DMA((2, n)),
+            pltpu.SemaphoreType.DMA((2, n)),
+        ],
+        compiler_params=pltpu.CompilerParams(collective_id=cid, has_side_effects=True),
     )(x)
 
 
@@ -110,10 +174,9 @@
     vector_len = vector_grads.shape[1]
     packed = jnp.concatenate([left_terms.reshape(-1), vector_grads[0]])
     lanes = 128
-    rows = -(-packed.shape[0] // (8 * lanes)) * 8
-    packed = jnp.pad(packed, (0, rows * lanes - packed.shape[0])).reshape(rows, lanes)
-    packed = jnp.sum(exchange(jnp.broadcast_to(packed, (replicas, rows, lanes)), "replica", 0), axis=0)
-    packed = packed.reshape(-1)
+    rows = -(-packed.shape[0] // (replicas * 8 * lanes)) * 8
+    packed = jnp.pad(packed, (0, replicas * rows * lanes - packed.shape[0]))
+    packed = allreduce_replica(packed.reshape(replicas, rows, lanes), 0).reshape(-1)
     left_sum = packed[: left_terms.size].reshape(left_terms.shape)
     vector_total = packed[left_terms.size : left_terms.size + vector_len]
     left_rows = jnp.einsum("kmr,krs->kms", left_sum, gram_root, precision=highest).astype(
@@ -129,8 +192,7 @@
     )
     part_shape = right_part.shape
     right_part = right_part.reshape(replicas, -1, lanes)
-    right_chunk = jnp.sum(exchange(right_part, "replica", 2), axis=0)
-    right_part = exchange(jnp.broadcast_to(right_chunk, right_part.shape), "replica", 3)
+    right_part = allreduce_replica(right_part, 2)
     right_part = right_part.reshape(part_shape).astype(jnp.bfloat16)
     right_new = exchange(
         jnp.broadcast_to(right_part, right_slots.shape), "mp", 4

time: 167 us -> 156 us (0.934)
  Pallas kernels: 120 us -> 104 us
  other arithmetic: 6.41 us -> 8.57 us
    pallas_call x5 -> x2, Pallas kernels: 120 us -> 65 us  [exchange(): pl.pallas_call(functools.partial(_exchange_kernel, n, axis), out_shape=ja...]
    pallas_call x0 -> x2, Pallas kernels: none -> 39.2 us  [allreduce_replica(): pl.pallas_call(functools.partial(_allreduce_kernel, n), out_shape=jax.Sha...]
  transfers between devices with their start and end apart: 2 -> 2, of which waited for: 0 -> 0; matrix products, arithmetic and copies ran while one was open for 9% -> 12% of each run, Pallas kernels for 72% -> 67%
where the time goes in v6:
time: 156 us; the launch traced here: 155 us
  Pallas kernels  104 us (67%)
  between operations  16.8 us (11%)
  matrix products  14.9 us (10%)
  other arithmetic  8.57 us (5%)
  local copies, waits for them, and re-layouts  7.2 us (5%)
  starting transfers between devices  3.44 us (2%)
    pallas_call x2, Pallas kernels, exchange(): pl.pallas_call(functools.partial(_exchange_kernel, n, axis), out_shape=ja...  65 us
    pallas_call x2, Pallas kernels, allreduce_replica(): pl.pallas_call(functools.partial(_allreduce_kernel, n), out_shape=jax.Sha...  39.2 us
    gather x1, local copies, waits for them, and re-layouts, per_device(): jnp.take(weight_slots, slots, axis=0).astype(jnp.float32)  4.44 us
    dot_general x1, matrix products, per_device(): jnp.einsum('kms,ksn->kmn', left_block, right_new, preferred_element_type=...  4.05 us
    ppermute x1, starting transfers between devices, per_device(): left_block = lax.ppermute(left_rows, ('replica', 'mp'), pairs)  3.4 us
    dot_general x1, matrix products, per_device(): jnp.einsum('kmn,knr->kmr', compensated, right_init, preferred_element_typ...  3.21 us
  transfers between devices with their start and end apart: 2, of which 0 were waited for; matrix products, arithmetic and copies ran while one was open for 12% of the time, Pallas kernels for 67%

profile of v6, /device:TPU:1, one launch (start us, length us, event | category | flops | bytes accessed | tf_op | source)
XLA Modules:
  0.0 155.1 jit_solution(10318379185092486894)
XLA Ops:
  7.2 0.0 copy-start
  7.2 0.0 all-gather.3.cloned.1.call-start
  7.2 2.1 %subtract_convert_fusion.2 = bf16[1,1,48,3072]{3,2,1,0:T(8,128)(2,1)} fusion(f32[1,1,48,3072]{3,2,1,0:T(8,128)} %param.16, f32[1,1,48,3072]{3,2,1,0:T(8,128)} %param.15), kind=kLoop, calls=%fused_computation.12 | loop fusion | flops 442368 | bytes 1474560 | tf_op jit(solution)/shard_map/convert_element_type | solution.py:169
  9.4 0.0 all-gather.3.cloned.1.call-update
  9.4 0.0 copy-start.7
  9.4 0.0 copy-start.4
  9.4 3.2 %fusion.17 = f32[8,48,32]{2,1,0:T(8,128)S(1)} fusion(bf16[8,3072,32]{1,2,0:T(8,128)(2,1)S(1)} %copy-done, bf16[1,8,48,3072]{3,2,1,0:T(8,128)(2,1)} %param.11, bf16[1,8,48,3072]{3,2,1,0:T(8,128)(2,1)} %param.10), kind=kOutput, calls=%fused_computation.38 | convolution fusion | flops 80216064 | bytes 6340608 | tf_op jit(solution)/shard_map/kmn,knr->kmr/dot_general | solution.py:170
  12.6 0.1 reshape.143
  12.8 0.6 fusion.8.x_ref
  13.4 21.0 %shard_map.145 = f32[16,8,128]{2,1,0:T(8,128)} custom-call(f32[16,8,128]{2,1,0:T(8,128)} %fusion.8.x_ref), custom_call_target="tpu_custom_call" | custom-call | tf_op jit(solution)/shard_map/pallas_call | solution.py:123
  34.4 0.8 slice.7
  35.2 0.1 reshape.145
  35.3 0.5 convolution_convert_fusion.1
  35.8 3.4 %collective-permute-start = (bf16[8,48,32]{1,2,0:T(8,128)(2,1)S(1)}, bf16[8,48,32]{1,2,0:T(8,128)(2,1)S(1)}, u32[]{:S(2)}, u32[]{:S(2)}) collective-permute-start(bf16[8,48,32]{1,2,0:T(8,128)(2,1)S(1)} %convolution_convert_fusion.1), channel_id=1, source_target_pairs={{0,0},{1,16},{2,32},{3,48},{4,64},{5,80},{6,96},{7,112},{8,128},{9... | collective-permute-start | bytes 73736 | tf_op jit(solution)/shard_map/ppermute | solution.py:205
  39.2 3.1 %convolution_convert_fusion = bf16[8,32,3072]{2,1,0:T(8,128)(2,1)S(1)} fusion(bf16[8,48,32]{1,2,0:T(8,128)(2,1)S(1)} %convolution_convert_fusion.1, bf16[1,8,48,3072]{3,2,1,0:T(8,128)(2,1)} %param.11, bf16[1,8,48,3072]{3,2,1,0:T(8,128)(2,1)} %param.10), kind=kOutput, calls=%fused_computation.5 | convolution fusion | flops 81002496 | bytes 6316032 | tf_op jit(solution)/shard_map/kmn,kms->ksn/dot_general | solution.py:186
  42.3 39.3 %shard_map.146 = bf16[16,16,3072]{2,1,0:T(8,128)(2,1)S(1)} custom-call(bf16[16,16,3072]{2,1,0:T(8,128)(2,1)S(1)} %bitcast.49), custom_call_target="tpu_custom_call" | custom-call | tf_op jit(solution)/shard_map/pallas_call | solution.py:59
  81.6 0.2 convert_reduce_fusion
  81.9 0.7 copy.30
  82.6 18.2 %shard_map.147 = f32[16,24,128]{2,1,0:T(8,128)} custom-call(f32[16,24,128]{2,1,0:T(8,128)} %bitcast.53), custom_call_target="tpu_custom_call" | custom-call | tf_op jit(solution)/shard_map/pallas_call | solution.py:123
  100.8 0.9 convert_element_type.113
  101.8 0.2 broadcast_in_dim.34.x_ref
  102.0 25.6 %shard_map.148 = bf16[16,16,3072]{2,1,0:T(8,128)(2,1)S(1)} custom-call(bf16[16,16,3072]{2,1,0:T(8,128)(2,1)S(1)} %broadcast_in_dim.34.x_ref), custom_call_target="tpu_custom_call" | custom-call | tf_op jit(solution)/shard_map/pallas_call | solution.py:59
  127.7 0.1 convert_reduce_fusion.1
  127.7 0.7 bitcast_reduce_fusion
  128.4 0.6 compare_and_fusion
  129.1 1.3 multiply_subtract_fusion
  130.3 2.3 %fusion = bf16[1,8,48,3072]{3,2,1,0:T(8,128)(2,1)} fusion(bf16[8,48,32]{1,2,0:T(8,128)(2,1)S(1)} %convolution_convert_fusion.1, bf16[8,32,3072]{2,1,0:T(8,128)(2,1)S(1)} %bitcast.46, bf16[1,8,48,3072]{3,2,1,0:T(8,128)(2,1)S(1)} %copy-done.1, bf16[1,8,48,3072]{3,2,1,0:T(8,128)(2,1)S(1)} %copy-done.2), kind=kOutput, calls=%fused_computation.4 | convolution fusion | flops 83755008 | bytes 8675328 | tf_op jit(solution)/shard_map/kms,ksn->kmn/dot_general | solution.py:206
  135.3 1.7 %convolution_add_fusion = f32[48,3072]{1,0:T(8,128)S(1)} fusion(f32[1,1,48,3072]{3,2,1,0:T(8,128)} %param.15, bf16[8,32,3072]{2,1,0:T(8,128)(2,1)S(1)} %bitcast.47, s32[]{:T(128)} %bitcast.7, f32[]{:T(128)S(6)} %convert_element_type.118, bf16[8,48,32]{1,2,0:T(8,128)(2,1)S(1)} %collective-permute-done), kind=kOutput, calls=%fused_computation.6 | convolution fusion | flops 57117696 | bytes 1386496 | tf_op jit(solution)/shard_map/cmr,crn->cmn/dot_general | solution.py:213
  137.0 0.8 copy-done.3
  137.8 1.9 %fusion.2 = f32[1,1,48,3072]{3,2,1,0:T(8,128)} fusion(f32[1,1,48,3072]{3,2,1,0:T(8,128)} %param.16, f32[48,3072]{1,0:T(8,128)S(1)} %convolution_add_fusion), kind=kLoop, calls=%fused_computation.11 | loop fusion | flops 294912 | bytes 1769472 | tf_op jit(solution)/shard_map/broadcast_in_dim | solution.py:227
  139.8 4.4 %gather_fusion = bf16[8,48,3072]{2,1,0:T(8,128)(2,1)} fusion(bf16[16,48,3072]{2,1,0:T(8,128)(2,1)} %bitcast.51, s32[1024]{0:T(1024)S(1)} %pad_clamp_fusion), kind=kCustom, calls=%fused_computation | custom fusion | bytes 4718624 | tf_op jit(solution)/shard_map/jit(_take)/gather | solution.py:220
  144.2 4.0 %subtract_convert_fusion = bf16[8,48,3072]{2,1,0:T(8,128)(2,1)} fusion(bf16[8,48,32]{1,2,0:T(8,128)(2,1)S(1)} %collective-permute-done, bf16[8,32,3072]{2,1,0:T(8,128)(2,1)S(1)} %bitcast.48, bf16[8,48,3072]{2,1,0:T(8,128)(2,1)} %gather_fusion, pred[8]{0:T(512)(128)(4,1)S(1)} %get-tuple-element.32), kind=kOutput, calls=%fused_computation.1 | convolution fusion | flops 81395712 | bytes 6316040 | tf_op jit(solution)/shard_map/kms,ksn->kmn/dot_general | solution.py:216
  (19 shorter events, 0.1 us)
Async XLA Ops:
  7.2 2.2 %copy-start = (bf16[8,3072,32]{1,2,0:T(8,128)(2,1)S(1)}, bf16[8,3072,32]{1,2,0:T(8,128)(2,1)}, u32[]{:S(2)}) copy-start(bf16[8,3072,32]{1,2,0:T(8,128)(2,1)} %param.12) | copy-start | bytes 4718596
  7.2 132.6 %all-gather.3.cloned.1.call-start = ((), (), s32[]{:S(2)}) async-start(), calls=%async_computation | async-start | bytes 5013504 | tf_op jit(solution)/shard_map/all_gather | solution.py:169
  9.4 3.4 %copy-start.7 = (f32[1,672]{1,0:T(1,128)S(1)}, f32[1,672]{1,0:T(1,128)}, u32[]{:S(2)}) copy-start(f32[1,672]{1,0:T(1,128)} %param.17) | copy-start | bytes 8068
  9.4 25.9 %copy-start.4 = (f32[8,32,32]{2,1,0:T(8,128)S(1)}, f32[8,32,32]{2,1,0:T(8,128)}, u32[]{:S(2)}) copy-start(f32[8,32,32]{2,1,0:T(8,128)} %param.13) | copy-start | bytes 98308
  35.8 99.5 %collective-permute-start = (bf16[8,48,32]{1,2,0:T(8,128)(2,1)S(1)}, bf16[8,48,32]{1,2,0:T(8,128)(2,1)S(1)}, u32[]{:S(2)}, u32[]{:S(2)}) collective-permute-start(bf16[8,48,32]{1,2,0:T(8,128)(2,1)S(1)} %convolution_convert_fusion.1), channel_id=1, source_target_pairs={{0,0},{1,16},{2,32},{3,48},{4,64},{5,80},{6,96},{7,112},{8,128},{9... | collective-permute-start | bytes 73736 | tf_op jit(solution)/shard_map/ppermute | solution.py:205
  101.8 25.9 %copy-start.8 = (s32[8]{0:T(128)S(1)}, s32[8]{0:T(128)}, u32[]{:S(2)}) copy-start(s32[8]{0:T(128)} %param.14) | copy-start | bytes 100
  101.8 27.3 %copy-start.5 = (f32[672]{0:T(1024)S(1)}, f32[672]{0:T(1024)}, u32[]{:S(2)}) copy-start(f32[672]{0:T(1024)} %param.19) | copy-start | bytes 8068
  101.8 27.2 %copy-start.6 = (f32[672]{0:T(1024)S(1)}, f32[672]{0:T(1024)}, u32[]{:S(2)}) copy-start(f32[672]{0:T(1024)} %param.18) | copy-start | bytes 8068
  101.8 28.5 %copy-start.1 = (bf16[1,8,48,3072]{3,2,1,0:T(8,128)(2,1)S(1)}, bf16[1,8,48,3072]{3,2,1,0:T(8,128)(2,1)}, u32[]{:S(2)}) copy-start(bf16[1,8,48,3072]{3,2,1,0:T(8,128)(2,1)} %param.11) | copy-start | bytes 7077892
  101.8 28.5 %copy-start.2 = (bf16[1,8,48,3072]{3,2,1,0:T(8,128)(2,1)S(1)}, bf16[1,8,48,3072]{3,2,1,0:T(8,128)(2,1)}, u32[]{:S(2)}) copy-start(bf16[1,8,48,3072]{3,2,1,0:T(8,128)(2,1)} %param.10) | copy-start | bytes 7077892
  137.0 0.8 copy-start.3
Sparse Core Ops, SparseCore 0:
  11.0 77.5 all-gather.2

commit v7 on v6

--- a/solution.py
+++ b/solution.py
@@ -136,6 +136,31 @@
     )(x)
 
 
+def _weights_kernel(slots_ref, base_ref, left_ref, right_ref, o_ref):
+    del slots_ref
+    approx = jnp.dot(left_ref[0], right_ref[0], preferred_element_type=jnp.float32)
+    o_ref[0] = (base_ref[0].astype(jnp.float32) - 0.1 * approx).astype(o_ref.dtype)
+
+
+def weights_of(slots, base, left, right):
+    matrices, rows, _ = left.shape
+    columns = right.shape[2]
+    return pl.pallas_call(
+        _weights_kernel,
+        out_shape=jax.ShapeDtypeStruct((matrices, rows, columns), base.dtype),
+        grid_spec=pltpu.PrefetchScalarGridSpec(
+            num_scalar_prefetch=1,
+            grid=(matrices,),
+            in_specs=[
+                pl.BlockSpec((1, rows, columns), lambda k, slot: (slot[k], 0, 0)),
+                pl.BlockSpec((1, rows, left.shape[2]), lambda k, slot: (k, 0, 0)),
+                pl.BlockSpec((1, right.shape[1], columns), lambda k, slot: (k, 0, 0)),
+            ],
+            out_specs=pl.BlockSpec((1, rows, columns), lambda k, slot: (k, 0, 0)),
+        ),
+    )(slots, base, left, right)
+
+
 def per_device(
     gradients,
     feedback,
@@ -213,12 +238,7 @@
     approx_slots = jnp.einsum("cmr,crn->cmn", left_chosen, right_chosen, precision=highest)
     new_momentum = 0.9 * momentum[0] + approx_slots
     new_master = master_weights[0] - 0.1 * new_momentum
-    block_approx = jnp.einsum(
-        "kms,ksn->kmn", left_block, right_new, preferred_element_type=jnp.float32
-    )
-    new_weights = (
-        jnp.take(weight_slots, slots, axis=0).astype(jnp.float32) - 0.1 * block_approx
-    ).astype(jnp.bfloat16)
+    new_weights = weights_of(slots, weight_slots, left_block, right_new)
     new_vector_momentum = 0.9 * vector_momentum + vector_total
     new_vector_params = vector_params - 0.1 * new_vector_momentum
     return (

time: 156 us -> 156 us (level)
  Pallas kernels: 104 us -> 113 us
  local copies, waits for them, and re-layouts: 7.2 us -> 2.89 us
  matrix products: 14.9 us -> 10.8 us
    pallas_call x0 -> x1, Pallas kernels: none -> 7.72 us  [weights_of(): pl.pallas_call(_weights_kernel, out_shape=jax.ShapeDtypeStruct((matrices,...]
    gather x1 -> x0, local copies, waits for them, and re-layouts: 4.44 us -> none  [per_device(): jnp.take(weight_slots, slots, axis=0).astype(jnp.float32)]
    dot_general x1 -> x0, matrix products: 4.05 us -> none  [per_device(): jnp.einsum('kms,ksn->kmn', left_block, right_new, preferred_element_type=...]
  transfers between devices with their start and end apart: 2 -> 2, of which waited for: 0 -> 0; matrix products, arithmetic and copies ran while one was open for 12% -> 12% of each run, Pallas kernels for 67% -> 68%
where the time goes in v7:
time: 156 us
  Pallas kernels  113 us (72%)
  between operations  16.7 us (11%)
  matrix products  10.8 us (7%)
  other arithmetic  8.74 us (6%)
  starting transfers between devices  3.44 us (2%)
  local copies, waits for them, and re-layouts  2.89 us (2%)
    pallas_call x2, Pallas kernels, exchange(): pl.pallas_call(functools.partial(_exchange_kernel, n, axis), out_shape=ja...  66.5 us
    pallas_call x2, Pallas kernels, allreduce_replica(): pl.pallas_call(functools.partial(_allreduce_kernel, n), out_shape=jax.Sha...  38.9 us
    pallas_call x1, Pallas kernels, weights_of(): pl.pallas_call(_weights_kernel, out_shape=jax.ShapeDtypeStruct((matrices,...  7.72 us
    ppermute x1, starting transfers between devices, per_device(): left_block = lax.ppermute(left_rows, ('replica', 'mp'), pairs)  3.4 us
    dot_general x1, matrix products, per_device(): jnp.einsum('kmn,knr->kmr', compensated, right_init, preferred_element_typ...  3.21 us
  transfers between devices with their start and end apart: 2, of which 0 were waited for; matrix products, arithmetic and copies ran while one was open for 12% of the time, Pallas kernels for 68%

profile of v7, /device:TPU:1, one launch (start us, length us, event | category | flops | bytes accessed | tf_op | source)
XLA Modules:
  0.0 155.7 jit_solution(11228128532120462509)
XLA Ops:
  7.2 0.0 copy-start
  7.2 0.0 all-gather.3.cloned.1.call-start
  7.2 2.1 %subtract_convert_fusion.1 = bf16[1,1,48,3072]{3,2,1,0:T(8,128)(2,1)} fusion(f32[1,1,48,3072]{3,2,1,0:T(8,128)} %param.16, f32[1,1,48,3072]{3,2,1,0:T(8,128)} %param.15), kind=kLoop, calls=%fused_computation.10 | loop fusion | flops 442368 | bytes 1474560 | tf_op jit(solution)/shard_map/convert_element_type | solution.py:194
  9.4 0.0 all-gather.3.cloned.1.call-update
  9.4 0.0 copy-start.10
  9.4 3.2 %fusion.17 = f32[8,48,32]{2,1,0:T(8,128)S(1)} fusion(bf16[8,3072,32]{1,2,0:T(8,128)(2,1)S(1)} %copy-done, bf16[1,8,48,3072]{3,2,1,0:T(8,128)(2,1)} %param.11, bf16[1,8,48,3072]{3,2,1,0:T(8,128)(2,1)} %param.10), kind=kOutput, calls=%fused_computation.33 | convolution fusion | flops 80216064 | bytes 6340608 | tf_op jit(solution)/shard_map/kmn,knr->kmr/dot_general | solution.py:195
  12.6 0.1 reshape.138
  12.8 0.6 fusion.8.x_ref
  13.4 21.0 %shard_map.145 = f32[16,8,128]{2,1,0:T(8,128)} custom-call(f32[16,8,128]{2,1,0:T(8,128)} %fusion.8.x_ref), custom_call_target="tpu_custom_call" | custom-call | tf_op jit(solution)/shard_map/pallas_call | solution.py:123
  34.4 0.8 slice.7
  35.2 0.1 reshape.140
  35.3 0.5 convolution_convert_fusion.1
  35.8 0.1 copy.46
  35.9 3.4 %collective-permute-start = (bf16[8,48,32]{2,1,0:T(8,128)(2,1)S(1)}, bf16[8,48,32]{2,1,0:T(8,128)(2,1)S(1)}, u32[]{:S(2)}, u32[]{:S(2)}) collective-permute-start(bf16[8,48,32]{2,1,0:T(8,128)(2,1)S(1)} %copy.46), channel_id=1, source_target_pairs={{0,0},{1,16},{2,32},{3,48},{4,64},{5,80},{6,96},{7,112},{8,128},{9... | collective-permute-start | bytes 73736 | tf_op jit(solution)/shard_map/ppermute | solution.py:230
  39.3 3.1 %convolution_convert_fusion = bf16[8,32,3072]{2,1,0:T(8,128)(2,1)S(1)} fusion(bf16[8,48,32]{1,2,0:T(8,128)(2,1)S(1)} %convolution_convert_fusion.1, bf16[1,8,48,3072]{3,2,1,0:T(8,128)(2,1)} %param.11, bf16[1,8,48,3072]{3,2,1,0:T(8,128)(2,1)} %param.10), kind=kOutput, calls=%fused_computation.3 | convolution fusion | flops 81002496 | bytes 6316032 | tf_op jit(solution)/shard_map/kmn,kms->ksn/dot_general | solution.py:211
  42.4 40.5 %shard_map.146 = bf16[16,16,3072]{2,1,0:T(8,128)(2,1)S(1)} custom-call(bf16[16,16,3072]{2,1,0:T(8,128)(2,1)S(1)} %bitcast.47), custom_call_target="tpu_custom_call" | custom-call | tf_op jit(solution)/shard_map/pallas_call | solution.py:59
  82.9 0.2 convert_reduce_fusion
  83.1 0.7 copy.50
  83.8 17.9 %shard_map.147 = f32[16,24,128]{2,1,0:T(8,128)} custom-call(f32[16,24,128]{2,1,0:T(8,128)} %bitcast.51), custom_call_target="tpu_custom_call" | custom-call | tf_op jit(solution)/shard_map/pallas_call | solution.py:123
  101.8 0.9 convert_element_type.107
  102.8 0.2 broadcast_in_dim.10.x_ref
  103.0 26.0 %shard_map.148 = bf16[16,16,3072]{2,1,0:T(8,128)(2,1)S(1)} custom-call(bf16[16,16,3072]{2,1,0:T(8,128)(2,1)S(1)} %broadcast_in_dim.10.x_ref), custom_call_target="tpu_custom_call" | custom-call | tf_op jit(solution)/shard_map/pallas_call | solution.py:59
  129.0 0.1 convert_reduce_fusion.1
  129.1 0.8 compare_reduce_fusion
  129.9 1.3 multiply_subtract_fusion
  131.2 2.3 %fusion = bf16[1,8,48,3072]{3,2,1,0:T(8,128)(2,1)} fusion(bf16[8,48,32]{1,2,0:T(8,128)(2,1)S(1)} %convolution_convert_fusion.1, bf16[8,32,3072]{2,1,0:T(8,128)(2,1)S(1)} %bitcast.44, bf16[1,8,48,3072]{3,2,1,0:T(8,128)(2,1)S(1)} %copy-done.2, bf16[1,8,48,3072]{3,2,1,0:T(8,128)(2,1)S(1)} %copy-done.3), kind=kOutput, calls=%fused_computation.2 | convolution fusion | flops 83755008 | bytes 8675328 | tf_op jit(solution)/shard_map/kms,ksn->kmn/dot_general | solution.py:231
  133.5 0.7 bitcast_reduce_fusion
  136.6 1.7 %convolution_add_fusion = f32[48,3072]{1,0:T(8,128)S(1)} fusion(f32[1,1,48,3072]{3,2,1,0:T(8,128)} %param.15, bf16[8,32,3072]{2,1,0:T(8,128)(2,1)S(1)} %bitcast.45, s32[]{:T(128)} %bitcast.7, f32[]{:T(128)S(6)} %convert_element_type.112, bf16[8,48,32]{2,1,0:T(8,128)(2,1)S(1)} %collective-permute-done.left_ref), kind=kOutput, calls=%fused_computation.4 | convolution fusion | flops 57117696 | bytes 1390592 | tf_op jit(solution)/shard_map/cmr,crn->cmn/dot_general | solution.py:238
  138.4 0.0 copy-start.4
  138.4 0.8 copy-done.4
  139.2 1.9 %fusion.2 = f32[1,1,48,3072]{3,2,1,0:T(8,128)} fusion(f32[1,1,48,3072]{3,2,1,0:T(8,128)} %param.16, f32[48,3072]{1,0:T(8,128)S(1)} %convolution_add_fusion), kind=kLoop, calls=%fused_computation.9 | loop fusion | flops 294912 | bytes 1769472 | tf_op jit(solution)/shard_map/broadcast_in_dim | solution.py:247
  141.1 7.7 %shard_map.149 = bf16[8,48,3072]{2,1,0:T(8,128)(2,1)} custom-call(s32[8]{0:T(128)} %copy-done.7, bf16[16,48,3072]{2,1,0:T(8,128)(2,1)} %bitcast.48, bf16[8,48,32]{2,1,0:T(8,128)(2,1)} %copy-done.6, bf16[8,32,3072]{2,1,0:T(8,128)(2,1)} %bitcast.46), custom_call_target="tpu_custom_call" | custom-call | tf_op jit(solution)/shard_map/pallas_call | solution.py:148
  (24 shorter events, 0.1 us)
Async XLA Ops:
  7.2 2.2 %copy-start = (bf16[8,3072,32]{1,2,0:T(8,128)(2,1)S(1)}, bf16[8,3072,32]{1,2,0:T(8,128)(2,1)}, u32[]{:S(2)}) copy-start(bf16[8,3072,32]{1,2,0:T(8,128)(2,1)} %param.12) | copy-start | bytes 4718596
  7.2 133.9 %all-gather.3.cloned.1.call-start = ((), (), s32[]{:S(2)}) async-start(), calls=%async_computation | async-start | bytes 5013504 | tf_op jit(solution)/shard_map/all_gather | solution.py:194
  9.4 3.4 %copy-start.10 = (f32[1,672]{1,0:T(1,128)S(1)}, f32[1,672]{1,0:T(1,128)}, u32[]{:S(2)}) copy-start(f32[1,672]{1,0:T(1,128)} %param.17) | copy-start | bytes 8068
  9.4 25.9 %copy-start.5 = (f32[8,32,32]{2,1,0:T(8,128)S(1)}, f32[8,32,32]{2,1,0:T(8,128)}, u32[]{:S(2)}) copy-start(f32[8,32,32]{2,1,0:T(8,128)} %param.13) | copy-start | bytes 98308
  35.9 100.7 %collective-permute-start = (bf16[8,48,32]{2,1,0:T(8,128)(2,1)S(1)}, bf16[8,48,32]{2,1,0:T(8,128)(2,1)S(1)}, u32[]{:S(2)}, u32[]{:S(2)}) collective-permute-start(bf16[8,48,32]{2,1,0:T(8,128)(2,1)S(1)} %copy.46), channel_id=1, source_target_pairs={{0,0},{1,16},{2,32},{3,48},{4,64},{5,80},{6,96},{7,112},{8,128},{9... | collective-permute-start | bytes 73736 | tf_op jit(solution)/shard_map/ppermute | solution.py:230
  102.8 26.3 %copy-start.11 = (s32[8]{0:T(128)S(1)}, s32[8]{0:T(128)}, u32[]{:S(2)}) copy-start(s32[8]{0:T(128)} %param.14) | copy-start | bytes 100
  102.8 27.2 %copy-start.8 = (f32[672]{0:T(1024)S(1)}, f32[672]{0:T(1024)}, u32[]{:S(2)}) copy-start(f32[672]{0:T(1024)} %param.19) | copy-start | bytes 8068
  102.8 27.2 %copy-start.9 = (f32[672]{0:T(1024)S(1)}, f32[672]{0:T(1024)}, u32[]{:S(2)}) copy-start(f32[672]{0:T(1024)} %param.18) | copy-start | bytes 8068
  102.8 28.4 %copy-start.2 = (bf16[1,8,48,3072]{3,2,1,0:T(8,128)(2,1)S(1)}, bf16[1,8,48,3072]{3,2,1,0:T(8,128)(2,1)}, u32[]{:S(2)}) copy-start(bf16[1,8,48,3072]{3,2,1,0:T(8,128)(2,1)} %param.11) | copy-start | bytes 7077892
  102.8 28.4 %copy-start.3 = (bf16[1,8,48,3072]{3,2,1,0:T(8,128)(2,1)S(1)}, bf16[1,8,48,3072]{3,2,1,0:T(8,128)(2,1)}, u32[]{:S(2)}) copy-start(bf16[1,8,48,3072]{3,2,1,0:T(8,128)(2,1)} %param.10) | copy-start | bytes 7077892
  129.0 7.6 %copy-start.1 = (bf16[16,16,3072]{2,1,0:T(8,128)(2,1)}, bf16[16,16,3072]{2,1,0:T(8,128)(2,1)S(1)}, u32[]{:S(2)}) copy-start(bf16[16,16,3072]{2,1,0:T(8,128)(2,1)S(1)} %shard_map.148) | copy-start | bytes 4718596
  129.9 3.6 %copy-start.7 = (s32[8]{0:T(128)}, s32[8]{0:T(128)S(1)}, u32[]{:S(2)}) copy-start(s32[8]{0:T(128)S(1)} %get-tuple-element.33.slots_ref) | copy-start | bytes 100
  136.6 4.5 %copy-start.6 = (bf16[8,48,32]{2,1,0:T(8,128)(2,1)}, bf16[8,48,32]{2,1,0:T(8,128)(2,1)S(1)}, u32[]{:S(2)}) copy-start(bf16[8,48,32]{2,1,0:T(8,128)(2,1)S(1)} %collective-permute-done.left_ref) | copy-start | bytes 73732
  138.4 0.8 copy-start.4
Sparse Core Ops, SparseCore 0:
  11.0 79.2 all-gather.2

commit v8 on v6

--- a/solution.py
+++ b/solution.py
@@ -10,14 +10,16 @@
 MESH_IDS = pl.DeviceIdType.MESH
 
 
-def _exchange_kernel(n, axis, x_ref, o_ref, recv, send_sem, recv_sem):
-    me = lax.axis_index(axis)
+def _exchange_kernel(n, axis, stride, x_ref, o_ref, recv, send_sem, recv_sem):
+    rank = lax.axis_index(axis)
+    me = lax.rem(lax.div(rank, stride), n)
+    first = rank - me * stride
     here = [lax.axis_index("replica"), lax.axis_index("mp")]
     where = 0 if axis == "replica" else 1
 
     def device(peer):
         ids = list(here)
-        ids[where] = peer
+        ids[where] = first + peer * stride
         return tuple(ids)
 
     barrier = pltpu.get_barrier_semaphore()
@@ -54,10 +56,10 @@
     o_ref[...] = recv[...]
 
 
-def exchange(x, axis, cid):
+def exchange(x, axis, cid, stride=1):
     n = x.shape[0]
     return pl.pallas_call(
-        functools.partial(_exchange_kernel, n, axis),
+        functools.partial(_exchange_kernel, n, axis, stride),
         out_shape=jax.ShapeDtypeStruct(x.shape, x.dtype),
         in_specs=[pl.BlockSpec(memory_space=pltpu.VMEM)],
         out_specs=pl.BlockSpec(memory_space=pltpu.VMEM),
@@ -72,13 +74,19 @@
     )(x)
 
 
-def _allreduce_kernel(n, x_ref, o_ref, first, middle, second, send_sem, recv_sem):
-    me = lax.axis_index("replica")
+def _allreduce_kernel(n, stride, x_ref, o_ref, first, middle, second, send_sem, recv_sem):
+    rank = lax.axis_index("replica")
+    me = lax.rem(lax.div(rank, stride), n)
+    base = rank - me * stride
     mp = lax.axis_index("mp")
+
+    def device(peer):
+        return (base + peer * stride, mp)
+
     barrier = pltpu.get_barrier_semaphore()
     for d in range(1, n):
         peer = lax.rem(me + d, n)
-        pl.semaphore_signal(barrier, inc=1, device_id=(peer, mp), device_id_type=MESH_IDS)
+        pl.semaphore_signal(barrier, inc=1, device_id=device(peer), device_id_type=MESH_IDS)
     pl.semaphore_wait(barrier, n - 1)
 
     def round_trip(phase, source_of, landing):
@@ -90,7 +98,7 @@
                 dst_ref=landing.at[me],
                 send_sem=send_sem.at[phase, d],
                 recv_sem=recv_sem.at[phase, me],
-                device_id=(peer, mp),
+                device_id=device(peer),
                 device_id_type=MESH_IDS,
             )
             copy.start()
@@ -103,7 +111,7 @@
                 dst_ref=landing.at[source],
                 send_sem=send_sem.at[phase, d],
                 recv_sem=recv_sem.at[phase, source],
-                device_id=(source, mp),
+                device_id=device(source),
                 device_id_type=MESH_IDS,
             ).wait_recv()
         for copy in copies:
@@ -118,10 +126,10 @@
     o_ref[...] = second[...]
 
 
-def allreduce_replica(x, cid):
+def allreduce_replica(x, cid, stride=1):
     n = x.shape[0]
     return pl.pallas_call(
-        functools.partial(_allreduce_kernel, n),
+        functools.partial(_allreduce_kernel, n, stride),
         out_shape=jax.ShapeDtypeStruct(x.shape, x.dtype),
         in_specs=[pl.BlockSpec(memory_space=pltpu.VMEM)],
         out_specs=pl.BlockSpec(memory_space=pltpu.VMEM),
@@ -183,20 +191,28 @@
         jnp.bfloat16
     )
     owners_count = lax.axis_size("mp")
+    cores = 2
+    chips = replicas // cores
+    pieces = owners_count // (matrices // cores)
+    width = compensated.shape[2] // pieces
     right_terms = jnp.einsum(
-        "kmn,kms->ksn", compensated, left_rows, preferred_element_type=jnp.float32
-    )
-    right_slots = right_terms.reshape(owners_count, -1, right_terms.shape[2])
+        "kmjn,kms->kjsn",
+        compensated.reshape(matrices, -1, pieces, width),
+        left_rows,
+        preferred_element_type=jnp.float32,
+    )
+    right_terms = right_terms.reshape(cores, owners_count, -1, width)
+    right_half = jnp.sum(exchange(right_terms, "replica", 1), axis=0)
     right_part = jnp.sum(
-        exchange(right_slots.astype(jnp.bfloat16), "mp", 1).astype(jnp.float32), axis=0
+        exchange(right_half.astype(jnp.bfloat16), "mp", 2).astype(jnp.float32), axis=0
     )
     part_shape = right_part.shape
-    right_part = right_part.reshape(replicas, -1, lanes)
-    right_part = allreduce_replica(right_part, 2)
+    right_part = allreduce_replica(right_part.reshape(chips, -1, lanes), 3, cores)
     right_part = right_part.reshape(part_shape).astype(jnp.bfloat16)
-    right_new = exchange(
-        jnp.broadcast_to(right_part, right_slots.shape), "mp", 4
-    ).reshape(right_terms.shape)
+    right_half = exchange(jnp.broadcast_to(right_part, right_half.shape), "mp", 4)
+    right_new = exchange(jnp.broadcast_to(right_half, right_terms.shape), "replica", 5)
+    right_new = right_new.reshape(matrices, pieces, -1, width).transpose(0, 2, 1, 3)
+    right_new = right_new.reshape(matrices, -1, compensated.shape[2])
     pairs = [
         (a * owners_count + b, b * owners_count + a)
         for a in range(replicas)

time: 156 us -> 147 us (0.942)
  Pallas kernels: 104 us -> 82.8 us
  local copies, waits for them, and re-layouts: 7.2 us -> 16.5 us
  other arithmetic: 8.57 us -> 13.9 us
  matrix products: 14.9 us -> 13.1 us
    pallas_call x4 -> x6, Pallas kernels: 104 us -> 82.8 us  [the longest x4 45.5 us: exchange(): pl.pallas_call(functools.partial(_exchange_kernel, n, axis, stride), out_...]
    convert_element_type x0 -> x2, local copies, waits for them, and re-layouts: none -> 5.61 us  [the longest x1 5.55 us: per_device(): (gradients[0].astype(jnp.float32) + feedback[0].astype(jnp.float32)).asty...]
    convert_element_type x0 -> x1, other arithmetic: none -> 3.32 us  [per_device(): (gradients[0].astype(jnp.float32) + feedback[0].astype(jnp.float32)).asty...]
    unnamed x20, local copies, waits for them, and re-layouts: 1.59 us -> 4.32 us
    dot_general x1, matrix products: 3.21 us -> 0.75 us  [per_device(): jnp.einsum('kmn,knr->kmr', compensated, right_init, preferred_element_typ...]
    reduce_sum x1 -> x2, other arithmetic: 0.22 us -> 2.31 us  [the longest x1 2.21 us: per_device(): right_half = jnp.sum(exchange(right_terms, 'replica', 1), axis=0)]
  transfers between devices with their start and end apart: 2 -> 2, of which waited for: 0 -> 0; matrix products, arithmetic and copies ran while one was open for 12% -> 19% of each run, Pallas kernels for 67% -> 56%
where the time goes in v8:
time: 147 us
  Pallas kernels  82.8 us (56%)
  between operations  16.9 us (11%)
  local copies, waits for them, and re-layouts  16.5 us (11%)
  other arithmetic  13.9 us (9%)
  matrix products  13.1 us (9%)
  starting transfers between devices  3.44 us (2%)
    pallas_call x4, Pallas kernels, exchange(): pl.pallas_call(functools.partial(_exchange_kernel, n, axis, stride), out_...  45.5 us
    pallas_call x2, Pallas kernels, allreduce_replica(): pl.pallas_call(functools.partial(_allreduce_kernel, n, stride), out_shape...  37.3 us
    convert_element_type x1, local copies, waits for them, and re-layouts, per_device(): (gradients[0].astype(jnp.float32) + feedback[0].astype(jnp.float32)).asty...  5.55 us
    gather x1, local copies, waits for them, and re-layouts, per_device(): jnp.take(weight_slots, slots, axis=0).astype(jnp.float32)  4.44 us
    unnamed x20, local copies, waits for them, and re-layouts  4.32 us
    dot_general x1, matrix products, per_device(): jnp.einsum('kms,ksn->kmn', left_block, right_new, preferred_element_type=...  4.05 us
    dot_general x1, matrix products, per_device(): jnp.einsum('kmjn,kms->kjsn', compensated.reshape(matrices, -1, pieces, wi...  3.88 us
    ppermute x1, starting transfers between devices, per_device(): left_block = lax.ppermute(left_rows, ('replica', 'mp'), pairs)  3.4 us
  transfers between devices with their start and end apart: 2, of which 0 were waited for; matrix products, arithmetic and copies ran while one was open for 19% of the time, Pallas kernels for 56%

profile of v8, /device:TPU:1, one launch (start us, length us, event | category | flops | bytes accessed | tf_op | source)
XLA Modules:
  0.0 146.6 jit_solution(8595562421618475932)
XLA Ops:
  7.2 2.1 %subtract_convert_fusion.2 = bf16[1,1,48,3072]{3,2,1,0:T(8,128)(2,1)} fusion(f32[1,1,48,3072]{3,2,1,0:T(8,128)} %param.16, f32[1,1,48,3072]{3,2,1,0:T(8,128)} %param.15), kind=kLoop, calls=%fused_computation.14 | loop fusion | flops 442368 | bytes 1474560 | tf_op jit(solution)/shard_map/convert_element_type | solution.py:177
  9.4 3.3 %add_convert_fusion = bf16[1,8,48,3072]{3,2,1,0:T(8,128)(2,1)S(1)} fusion(bf16[1,8,48,3072]{3,2,1,0:T(8,128)(2,1)} %param.11, bf16[1,8,48,3072]{3,2,1,0:T(8,128)(2,1)} %param.10), kind=kLoop, calls=%fused_computation.3 | loop fusion | flops 4718592 | bytes 7077888 | tf_op jit(solution)/shard_map/convert_element_type | solution.py:160
  12.7 1.4 copy-done.2
  14.1 0.7 fusion.1
  15.0 0.6 fusion.11.x_ref
  15.7 21.0 %shard_map.145 = f32[16,8,128]{2,1,0:T(8,128)} custom-call(f32[16,8,128]{2,1,0:T(8,128)} %fusion.11.x_ref), custom_call_target="tpu_custom_call" | custom-call | tf_op jit(solution)/shard_map/pallas_call | solution.py:131
  36.6 0.8 slice.7
  37.5 0.5 convolution_convert_fusion
  38.0 3.4 %collective-permute-start = (bf16[8,48,32]{1,2,0:T(8,128)(2,1)S(1)}, bf16[8,48,32]{1,2,0:T(8,128)(2,1)S(1)}, u32[]{:S(2)}, u32[]{:S(2)}) collective-permute-start(bf16[8,48,32]{1,2,0:T(8,128)(2,1)S(1)} %convolution_convert_fusion), channel_id=1, source_target_pairs={{0,0},{1,16},{2,32},{3,48},{4,64},{5,80},{6,96},{7,112},{8,128},{9... | collective-permute-start | bytes 73736 | tf_op jit(solution)/shard_map/ppermute | solution.py:221
  41.4 5.5 %convert_element_type.116 = bf16[8,48,4,768]{3,2,1,0:T(4,128)(2,1)} reshape(bf16[1,8,48,3072]{3,2,1,0:T(8,128)(2,1)} %copy-done.2) | data formatting | bytes 4718592 | tf_op jit(solution)/shard_map/convert_element_type | solution.py:160
  47.0 3.9 %fusion.3 = f32[8,32,4,768]{3,1,2,0:T(8,128)} fusion(bf16[8,48,4,768]{3,2,1,0:T(4,128)(2,1)} %convert_element_type.116, bf16[8,48,32]{1,2,0:T(8,128)(2,1)S(1)} %convolution_convert_fusion), kind=kOutput, calls=%fused_computation.8 | convolution fusion | flops 75497472 | bytes 5529600 | tf_op jit(solution)/shard_map/kmjn,kms->kjsn/dot_general | solution.py:198
  50.9 5.6 %shard_map.146 = f32[2,16,32,768]{3,2,1,0:T(8,128)S(1)} custom-call(f32[2,16,32,768]{3,2,1,0:T(8,128)} %bitcast.54), custom_call_target="tpu_custom_call" | custom-call | tf_op jit(solution)/shard_map/pallas_call | solution.py:61
  56.5 1.7 %copy-done.1 = f32[2,16,32,768]{3,2,1,0:T(8,128)} copy-done((f32[2,16,32,768]{3,2,1,0:T(8,128)}, f32[2,16,32,768]{3,2,1,0:T(8,128)S(1)}, u32[]{:S(2)}) %copy-start.1) | copy-done | bytes 3145752
  58.2 2.2 %reduce_sum.27.x_ref = bf16[16,32,768]{2,1,0:T(8,128)(2,1)S(1)} reduce(f32[2,16,32,768]{3,2,1,0:T(8,128)} %copy-done.1, f32[]{:T(128)} %constant.12.clone.1), dimensions={0}, to_apply=%region_0.0 | reduce | flops 393216 | bytes 3932164 | tf_op jit(solution)/shard_map/reduce_sum | solution.py:205
  60.4 21.6 %shard_map.147 = bf16[16,32,768]{2,1,0:T(8,128)(2,1)S(1)} custom-call(bf16[16,32,768]{2,1,0:T(8,128)(2,1)S(1)} %reduce_sum.27.x_ref), custom_call_target="tpu_custom_call" | custom-call | tf_op jit(solution)/shard_map/pallas_call | solution.py:61
  82.1 0.6 reshape.158.x_ref
  82.7 16.3 %shard_map.148 = f32[8,24,128]{2,1,0:T(8,128)} custom-call(f32[8,24,128]{2,1,0:T(8,128)} %reshape.158.x_ref), custom_call_target="tpu_custom_call" | custom-call | tf_op jit(solution)/shard_map/pallas_call | solution.py:131
  99.0 0.9 convert_element_type.119
  100.1 12.7 %shard_map.149 = bf16[16,32,768]{2,1,0:T(8,128)(2,1)S(1)} custom-call(bf16[16,32,768]{2,1,0:T(8,128)(2,1)S(1)} %broadcast_in_dim.37.x_ref), custom_call_target="tpu_custom_call" | custom-call | tf_op jit(solution)/shard_map/pallas_call | solution.py:61
  112.8 0.2 broadcast_in_dim.38.x_ref
  113.0 5.6 %shard_map.150 = bf16[2,16,32,768]{3,2,1,0:T(8,128)(2,1)S(1)} custom-call(bf16[2,16,32,768]{3,2,1,0:T(8,128)(2,1)S(1)} %broadcast_in_dim.38.x_ref), custom_call_target="tpu_custom_call" | custom-call | tf_op jit(solution)/shard_map/pallas_call | solution.py:61
  118.6 0.2 copy.39
  118.8 0.4 copy-done.9
  119.3 0.7 bitcast_reduce_fusion
  120.0 0.6 compare_and_fusion
  120.6 1.3 multiply_subtract_fusion
  121.9 2.2 %fusion = bf16[1,8,48,3072]{3,2,1,0:T(8,128)(2,1)} fusion(bf16[8,48,32]{1,2,0:T(8,128)(2,1)S(1)} %convolution_convert_fusion, bf16[8,32,3072]{2,1,0:T(8,128)(2,1)S(1)} %bitcast.51, bf16[1,8,48,3072]{3,2,1,0:T(8,128)(2,1)S(1)} %copy-done.3), kind=kOutput, calls=%fused_computation.4 | convolution fusion | flops 79036416 | bytes 6316032 | tf_op jit(solution)/shard_map/kms,ksn->kmn/dot_general | solution.py:222
  126.8 1.8 %convolution_add_fusion = f32[48,3072]{1,0:T(8,128)S(1)} fusion(f32[1,1,48,3072]{3,2,1,0:T(8,128)} %param.15, bf16[8,32,3072]{2,1,0:T(8,128)(2,1)S(1)} %bitcast.52, s32[]{:T(128)} %bitcast.11, f32[]{:T(128)S(6)} %convert_element_type.124, bf16[8,48,32]{1,2,0:T(8,128)(2,1)S(1)} %collective-permute-done), kind=kOutput, calls=%fused_computation.5 | convolution fusion | flops 57117696 | bytes 1386496 | tf_op jit(solution)/shard_map/cmr,crn->cmn/dot_general | solution.py:229
  128.5 0.8 copy-done.4
  129.3 1.9 %fusion.5 = f32[1,1,48,3072]{3,2,1,0:T(8,128)} fusion(f32[1,1,48,3072]{3,2,1,0:T(8,128)} %param.16, f32[48,3072]{1,0:T(8,128)S(1)} %convolution_add_fusion), kind=kLoop, calls=%fused_computation.13 | loop fusion | flops 294912 | bytes 1769472 | tf_op jit(solution)/shard_map/broadcast_in_dim | solution.py:243
  131.3 4.4 %gather_fusion = bf16[8,48,3072]{2,1,0:T(8,128)(2,1)} fusion(bf16[16,48,3072]{2,1,0:T(8,128)(2,1)} %bitcast.56, s32[1024]{0:T(1024)S(1)} %pad_clamp_fusion), kind=kCustom, calls=%fused_computation | custom fusion | bytes 4718624 | tf_op jit(solution)/shard_map/jit(_take)/gather | solution.py:236
  135.7 4.0 %subtract_convert_fusion = bf16[8,48,3072]{2,1,0:T(8,128)(2,1)} fusion(bf16[8,48,32]{1,2,0:T(8,128)(2,1)S(1)} %collective-permute-done, bf16[8,32,3072]{2,1,0:T(8,128)(2,1)S(1)} %bitcast.53, bf16[8,48,3072]{2,1,0:T(8,128)(2,1)} %gather_fusion, pred[8]{0:T(512)(128)(4,1)S(1)} %get-tuple-element.32), kind=kOutput, calls=%fused_computation.1 | convolution fusion | flops 81395712 | bytes 6316040 | tf_op jit(solution)/shard_map/kms,ksn->kmn/dot_general | solution.py:232
  (28 shorter events, 0.7 us)
Async XLA Ops:
  7.2 6.9 %copy-start = (bf16[8,3072,32]{1,2,0:T(8,128)(2,1)S(1)}, bf16[8,3072,32]{1,2,0:T(8,128)(2,1)}, u32[]{:S(2)}) copy-start(bf16[8,3072,32]{1,2,0:T(8,128)(2,1)} %param.12) | copy-start | bytes 4718596
  7.2 124.1 %all-gather.3.cloned.1.call-start = ((), (), s32[]{:S(2)}) async-start(), calls=%async_computation | async-start | bytes 5013504 | tf_op jit(solution)/shard_map/all_gather | solution.py:177
  12.7 1.4 copy-start.2
  14.1 0.9 copy-start.8
  14.1 23.4 %copy-start.5 = (f32[8,32,32]{2,1,0:T(8,128)S(1)}, f32[8,32,32]{2,1,0:T(8,128)}, u32[]{:S(2)}) copy-start(f32[8,32,32]{2,1,0:T(8,128)} %param.13) | copy-start | bytes 98308
  38.0 88.7 %collective-permute-start = (bf16[8,48,32]{1,2,0:T(8,128)(2,1)S(1)}, bf16[8,48,32]{1,2,0:T(8,128)(2,1)S(1)}, u32[]{:S(2)}, u32[]{:S(2)}) collective-permute-start(bf16[8,48,32]{1,2,0:T(8,128)(2,1)S(1)} %convolution_convert_fusion), channel_id=1, source_target_pairs={{0,0},{1,16},{2,32},{3,48},{4,64},{5,80},{6,96},{7,112},{8,128},{9... | collective-permute-start | bytes 73736 | tf_op jit(solution)/shard_map/ppermute | solution.py:221
  56.5 1.7 %copy-start.1 = (f32[2,16,32,768]{3,2,1,0:T(8,128)}, f32[2,16,32,768]{3,2,1,0:T(8,128)S(1)}, u32[]{:S(2)}) copy-start(f32[2,16,32,768]{3,2,1,0:T(8,128)S(1)} %shard_map.146) | copy-start | bytes 9437188
  118.6 0.7 copy-start.9
  118.6 2.0 %copy-start.6 = (f32[672]{0:T(1024)S(1)}, f32[672]{0:T(1024)}, u32[]{:S(2)}) copy-start(f32[672]{0:T(1024)} %param.19) | copy-start | bytes 8068
  118.6 2.0 %copy-start.7 = (f32[672]{0:T(1024)S(1)}, f32[672]{0:T(1024)}, u32[]{:S(2)}) copy-start(f32[672]{0:T(1024)} %param.18) | copy-start | bytes 8068
  118.6 3.3 %copy-start.3 = (bf16[1,8,48,3072]{3,2,1,0:T(8,128)(2,1)S(1)}, bf16[1,8,48,3072]{3,2,1,0:T(8,128)(2,1)}, u32[]{:S(2)}) copy-start(bf16[1,8,48,3072]{3,2,1,0:T(8,128)(2,1)} %copy-done.2) | copy-start | bytes 7077892
  128.5 0.8 copy-start.4
Sparse Core Ops, SparseCore 0:
  10.4 71.2 all-gather.2

commit v9 on v8

--- a/solution.py
+++ b/solution.py
@@ -196,13 +196,11 @@
     pieces = owners_count // (matrices // cores)
     width = compensated.shape[2] // pieces
     right_terms = jnp.einsum(
-        "kmjn,kms->kjsn",
-        compensated.reshape(matrices, -1, pieces, width),
-        left_rows,
-        preferred_element_type=jnp.float32,
-    )
-    right_terms = right_terms.reshape(cores, owners_count, -1, width)
-    right_half = jnp.sum(exchange(right_terms, "replica", 1), axis=0)
+        "kmn,kms->ksn", compensated, left_rows, preferred_element_type=jnp.float32
+    )
+    right_terms = right_terms.reshape(matrices, -1, pieces, width).transpose(0, 2, 1, 3)
+    right_terms = right_terms.astype(jnp.bfloat16).reshape(cores, owners_count, -1, width)
+    right_half = jnp.sum(exchange(right_terms, "replica", 1).astype(jnp.float32), axis=0)
     right_part = jnp.sum(
         exchange(right_half.astype(jnp.bfloat16), "mp", 2).astype(jnp.float32), axis=0
     )

time: 147 us -> 135 us (0.918)
  local copies, waits for them, and re-layouts: 16.5 us -> 9.18 us
  other arithmetic: 13.9 us -> 9.78 us
  Pallas kernels: 82.8 us -> 80 us
  matrix products: 13.1 us -> 14.9 us
    convert_element_type x1, local copies, waits for them, and re-layouts: 5.55 us -> 0.18 us  [per_device(): right_terms.astype(jnp.bfloat16).reshape(cores, owners_count, -1, width)]
    convert_element_type x1 -> x0, other arithmetic: 3.32 us -> none  [per_device(): (gradients[0].astype(jnp.float32) + feedback[0].astype(jnp.float32)).asty...]
    pallas_call x4, Pallas kernels: 45.5 us -> 43 us  [exchange(): pl.pallas_call(functools.partial(_exchange_kernel, n, axis, stride), out_...]
    dot_general x1, matrix products: 0.75 us -> 3.21 us  [per_device(): jnp.einsum('kmn,knr->kmr', compensated, right_init, preferred_element_typ...]
    unnamed x20, local copies, waits for them, and re-layouts: 4.32 us -> 2.41 us
  transfers between devices with their start and end apart: 2 -> 2, of which waited for: 0 -> 0; matrix products, arithmetic and copies ran while one was open for 19% -> 16% of each run, Pallas kernels for 56% -> 60%
where the time goes in v9:
time: 135 us; the launch traced here: 134 us
  Pallas kernels  80 us (59%)
  between operations  16.9 us (13%)
  matrix products  14.9 us (11%)
  other arithmetic  9.78 us (7%)
  local copies, waits for them, and re-layouts  9.18 us (7%)
  starting transfers between devices  3.44 us (3%)
    pallas_call x4, Pallas kernels, exchange(): pl.pallas_call(functools.partial(_exchange_kernel, n, axis, stride), out_...  43 us
    pallas_call x2, Pallas kernels, allreduce_replica(): pl.pallas_call(functools.partial(_allreduce_kernel, n, stride), out_shape...  37 us
    gather x1, local copies, waits for them, and re-layouts, per_device(): jnp.take(weight_slots, slots, axis=0).astype(jnp.float32)  4.44 us
    dot_general x1, matrix products, per_device(): jnp.einsum('kms,ksn->kmn', left_block, right_new, preferred_element_type=...  4.05 us
    ppermute x1, starting transfers between devices, per_device(): left_block = lax.ppermute(left_rows, ('replica', 'mp'), pairs)  3.4 us
    dot_general x1, matrix products, per_device(): jnp.einsum('kmn,knr->kmr', compensated, right_init, preferred_element_typ...  3.21 us
    dot_general x1, matrix products, per_device(): jnp.einsum('kmn,kms->ksn', compensated, left_rows, preferred_element_type...  3.09 us
  transfers between devices with their start and end apart: 2, of which 0 were waited for; matrix products, arithmetic and copies ran while one was open for 16% of the time, Pallas kernels for 60%

profile of v9, /device:TPU:1, one launch (start us, length us, event | category | flops | bytes accessed | tf_op | source)
XLA Modules:
  0.0 134.2 jit_solution(727291822588005703)
XLA Ops:
  7.2 2.1 %subtract_convert_fusion.2 = bf16[1,1,48,3072]{3,2,1,0:T(8,128)(2,1)} fusion(f32[1,1,48,3072]{3,2,1,0:T(8,128)} %param.16, f32[1,1,48,3072]{3,2,1,0:T(8,128)} %param.15), kind=kLoop, calls=%fused_computation.13 | loop fusion | flops 442368 | bytes 1474560 | tf_op jit(solution)/shard_map/convert_element_type | solution.py:177
  9.4 3.2 %fusion.17 = f32[8,48,32]{2,1,0:T(8,128)S(1)} fusion(bf16[8,3072,32]{1,2,0:T(8,128)(2,1)S(1)} %copy-done, bf16[1,8,48,3072]{3,2,1,0:T(8,128)(2,1)} %param.11, bf16[1,8,48,3072]{3,2,1,0:T(8,128)(2,1)} %param.10), kind=kOutput, calls=%fused_computation.38 | convolution fusion | flops 80216064 | bytes 6340608 | tf_op jit(solution)/shard_map/kmn,knr->kmr/dot_general | solution.py:178
  12.6 0.1 reshape.149
  12.8 0.6 fusion.8.x_ref
  13.4 21.0 %shard_map.145 = f32[16,8,128]{2,1,0:T(8,128)} custom-call(f32[16,8,128]{2,1,0:T(8,128)} %fusion.8.x_ref), custom_call_target="tpu_custom_call" | custom-call | tf_op jit(solution)/shard_map/pallas_call | solution.py:131
  34.4 0.8 slice.7
  35.3 0.5 convolution_convert_fusion.1
  35.8 3.4 %collective-permute-start = (bf16[8,48,32]{1,2,0:T(8,128)(2,1)S(1)}, bf16[8,48,32]{1,2,0:T(8,128)(2,1)S(1)}, u32[]{:S(2)}, u32[]{:S(2)}) collective-permute-start(bf16[8,48,32]{1,2,0:T(8,128)(2,1)S(1)} %convolution_convert_fusion.1), channel_id=1, source_target_pairs={{0,0},{1,16},{2,32},{3,48},{4,64},{5,80},{6,96},{7,112},{8,128},{9... | collective-permute-start | bytes 73736 | tf_op jit(solution)/shard_map/ppermute | solution.py:219
  39.2 3.1 %convolution_convert_fusion = bf16[8,32,3072]{2,1,0:T(8,128)(2,1)S(1)} fusion(bf16[8,48,32]{1,2,0:T(8,128)(2,1)S(1)} %convolution_convert_fusion.1, bf16[1,8,48,3072]{3,2,1,0:T(8,128)(2,1)} %param.11, bf16[1,8,48,3072]{3,2,1,0:T(8,128)(2,1)} %param.10), kind=kOutput, calls=%fused_computation.5 | convolution fusion | flops 81002496 | bytes 6316032 | tf_op jit(solution)/shard_map/kmn,kms->ksn/dot_general | solution.py:198
  42.3 0.2 copy.41
  42.5 2.6 %shard_map.146 = bf16[2,16,32,768]{3,2,1,0:T(8,128)(2,1)S(1)} custom-call(bf16[2,16,32,768]{3,2,1,0:T(8,128)(2,1)S(1)} %bitcast.50), custom_call_target="tpu_custom_call" | custom-call | tf_op jit(solution)/shard_map/pallas_call | solution.py:61
  45.1 1.4 %reduce_sum.30.x_ref = bf16[16,32,768]{2,1,0:T(8,128)(2,1)} reduce(bf16[2,16,32,768]{3,2,1,0:T(8,128)(2,1)S(1)} %shard_map.146, bf16[]{:T(256)} %constant.12.clone.1), dimensions={0}, to_apply=%region_0.0 | reduce | flops 393216 | bytes 2359298 | tf_op jit(solution)/shard_map/reduce_sum | solution.py:203
  46.4 1.1 copy-done.1
  47.6 20.1 %shard_map.147 = bf16[16,32,768]{2,1,0:T(8,128)(2,1)S(1)} custom-call(bf16[16,32,768]{2,1,0:T(8,128)(2,1)S(1)} %copy-done.1), custom_call_target="tpu_custom_call" | custom-call | tf_op jit(solution)/shard_map/pallas_call | solution.py:61
  67.7 0.1 convert_reduce_fusion
  67.8 0.6 reshape.153.x_ref
  68.5 16.1 %shard_map.148 = f32[8,24,128]{2,1,0:T(8,128)} custom-call(f32[8,24,128]{2,1,0:T(8,128)} %reshape.153.x_ref), custom_call_target="tpu_custom_call" | custom-call | tf_op jit(solution)/shard_map/pallas_call | solution.py:131
  84.6 0.9 convert_element_type.120
  85.6 11.9 %shard_map.149 = bf16[16,32,768]{2,1,0:T(8,128)(2,1)S(1)} custom-call(bf16[16,32,768]{2,1,0:T(8,128)(2,1)S(1)} %broadcast_in_dim.37.x_ref), custom_call_target="tpu_custom_call" | custom-call | tf_op jit(solution)/shard_map/pallas_call | solution.py:61
  97.5 0.2 broadcast_in_dim.38.x_ref
  97.7 8.4 %shard_map.150 = bf16[2,16,32,768]{3,2,1,0:T(8,128)(2,1)S(1)} custom-call(bf16[2,16,32,768]{3,2,1,0:T(8,128)(2,1)S(1)} %broadcast_in_dim.38.x_ref), custom_call_target="tpu_custom_call" | custom-call | tf_op jit(solution)/shard_map/pallas_call | solution.py:61
  106.1 0.2 copy.39
  106.3 0.4 copy-done.9
  106.8 0.7 bitcast_reduce_fusion
  107.5 0.6 compare_and_fusion
  108.1 1.3 multiply_subtract_fusion
  109.4 2.3 %fusion = bf16[1,8,48,3072]{3,2,1,0:T(8,128)(2,1)} fusion(bf16[8,48,32]{1,2,0:T(8,128)(2,1)S(1)} %convolution_convert_fusion.1, bf16[8,32,3072]{2,1,0:T(8,128)(2,1)S(1)} %bitcast.52, bf16[1,8,48,3072]{3,2,1,0:T(8,128)(2,1)S(1)} %copy-done.2, bf16[1,8,48,3072]{3,2,1,0:T(8,128)(2,1)S(1)} %copy-done.3), kind=kOutput, calls=%fused_computation.4 | convolution fusion | flops 83755008 | bytes 8675328 | tf_op jit(solution)/shard_map/kms,ksn->kmn/dot_general | solution.py:220
  114.3 1.8 %convolution_add_fusion = f32[48,3072]{1,0:T(8,128)S(1)} fusion(f32[1,1,48,3072]{3,2,1,0:T(8,128)} %param.15, bf16[8,32,3072]{2,1,0:T(8,128)(2,1)S(1)} %bitcast.53, s32[]{:T(128)} %bitcast.9, f32[]{:T(128)S(6)} %convert_element_type.125, bf16[8,48,32]{1,2,0:T(8,128)(2,1)S(1)} %collective-permute-done), kind=kOutput, calls=%fused_computation.6 | convolution fusion | flops 57117696 | bytes 1386496 | tf_op jit(solution)/shard_map/cmr,crn->cmn/dot_general | solution.py:227
  116.1 0.8 copy-done.4
  116.9 1.9 %fusion.2 = f32[1,1,48,3072]{3,2,1,0:T(8,128)} fusion(f32[1,1,48,3072]{3,2,1,0:T(8,128)} %param.16, f32[48,3072]{1,0:T(8,128)S(1)} %convolution_add_fusion), kind=kLoop, calls=%fused_computation.12 | loop fusion | flops 294912 | bytes 1769472 | tf_op jit(solution)/shard_map/broadcast_in_dim | solution.py:241
  118.8 4.4 %gather_fusion = bf16[8,48,3072]{2,1,0:T(8,128)(2,1)} fusion(bf16[16,48,3072]{2,1,0:T(8,128)(2,1)} %bitcast.57, s32[1024]{0:T(1024)S(1)} %pad_clamp_fusion), kind=kCustom, calls=%fused_computation | custom fusion | bytes 4718624 | tf_op jit(solution)/shard_map/jit(_take)/gather | solution.py:234
  123.3 4.0 %subtract_convert_fusion = bf16[8,48,3072]{2,1,0:T(8,128)(2,1)} fusion(bf16[8,48,32]{1,2,0:T(8,128)(2,1)S(1)} %collective-permute-done, bf16[8,32,3072]{2,1,0:T(8,128)(2,1)S(1)} %bitcast.54, bf16[8,48,3072]{2,1,0:T(8,128)(2,1)} %gather_fusion, pred[8]{0:T(512)(128)(4,1)S(1)} %get-tuple-element.32), kind=kOutput, calls=%fused_computation.1 | convolution fusion | flops 81395712 | bytes 6316040 | tf_op jit(solution)/shard_map/kms,ksn->kmn/dot_general | solution.py:230
  (27 shorter events, 0.5 us)
Async XLA Ops:
  7.2 2.2 %copy-start = (bf16[8,3072,32]{1,2,0:T(8,128)(2,1)S(1)}, bf16[8,3072,32]{1,2,0:T(8,128)(2,1)}, u32[]{:S(2)}) copy-start(bf16[8,3072,32]{1,2,0:T(8,128)(2,1)} %param.12) | copy-start | bytes 4718596
  7.2 111.7 %all-gather.3.cloned.1.call-start = ((), (), s32[]{:S(2)}) async-start(), calls=%async_computation | async-start | bytes 5013504 | tf_op jit(solution)/shard_map/all_gather | solution.py:177
  9.4 3.4 %copy-start.8 = (f32[1,672]{1,0:T(1,128)S(1)}, f32[1,672]{1,0:T(1,128)}, u32[]{:S(2)}) copy-start(f32[1,672]{1,0:T(1,128)} %param.17) | copy-start | bytes 8068
  9.4 25.9 %copy-start.5 = (f32[8,32,32]{2,1,0:T(8,128)S(1)}, f32[8,32,32]{2,1,0:T(8,128)}, u32[]{:S(2)}) copy-start(f32[8,32,32]{2,1,0:T(8,128)} %param.13) | copy-start | bytes 98308
  35.8 78.5 %collective-permute-start = (bf16[8,48,32]{1,2,0:T(8,128)(2,1)S(1)}, bf16[8,48,32]{1,2,0:T(8,128)(2,1)S(1)}, u32[]{:S(2)}, u32[]{:S(2)}) collective-permute-start(bf16[8,48,32]{1,2,0:T(8,128)(2,1)S(1)} %convolution_convert_fusion.1), channel_id=1, source_target_pairs={{0,0},{1,16},{2,32},{3,48},{4,64},{5,80},{6,96},{7,112},{8,128},{9... | collective-permute-start | bytes 73736 | tf_op jit(solution)/shard_map/ppermute | solution.py:219
  46.4 1.1 copy-start.1
  97.7 11.7 %copy-start.3 = (bf16[1,8,48,3072]{3,2,1,0:T(8,128)(2,1)S(1)}, bf16[1,8,48,3072]{3,2,1,0:T(8,128)(2,1)}, u32[]{:S(2)}) copy-start(bf16[1,8,48,3072]{3,2,1,0:T(8,128)(2,1)} %param.10) | copy-start | bytes 7077892
  106.1 0.7 copy-start.9
  106.1 2.0 %copy-start.6 = (f32[672]{0:T(1024)S(1)}, f32[672]{0:T(1024)}, u32[]{:S(2)}) copy-start(f32[672]{0:T(1024)} %param.19) | copy-start | bytes 8068
  106.1 2.0 %copy-start.7 = (f32[672]{0:T(1024)S(1)}, f32[672]{0:T(1024)}, u32[]{:S(2)}) copy-start(f32[672]{0:T(1024)} %param.18) | copy-start | bytes 8068
  106.1 3.3 %copy-start.2 = (bf16[1,8,48,3072]{3,2,1,0:T(8,128)(2,1)S(1)}, bf16[1,8,48,3072]{3,2,1,0:T(8,128)(2,1)}, u32[]{:S(2)}) copy-start(bf16[1,8,48,3072]{3,2,1,0:T(8,128)(2,1)} %param.11) | copy-start | bytes 7077892
  116.1 0.8 copy-start.4
Sparse Core Ops, SparseCore 0:
  10.4 72.1 all-gather.2

commit v10 on v9

--- a/solution.py
+++ b/solution.py
@@ -10,7 +10,7 @@
 MESH_IDS = pl.DeviceIdType.MESH
 
 
-def _exchange_kernel(n, axis, stride, x_ref, o_ref, recv, send_sem, recv_sem):
+def _exchange_kernel(n, axis, stride, total, x_ref, o_ref, recv, send_sem, recv_sem):
     rank = lax.axis_index(axis)
     me = lax.rem(lax.div(rank, stride), n)
     first = rank - me * stride
@@ -53,14 +53,23 @@
         ).wait_recv()
     for copy in copies:
         copy.wait_send()
-    o_ref[...] = recv[...]
-
-
-def exchange(x, axis, cid, stride=1):
+    if total is None:
+        o_ref[...] = recv[...]
+    else:
+        acc = recv[0].astype(jnp.float32)
+        for s in range(1, n):
+            acc = acc + recv[s].astype(jnp.float32)
+        o_ref[...] = acc.astype(o_ref.dtype)
+
+
+def exchange(x, axis, cid, stride=1, total=None):
     n = x.shape[0]
+    out = jax.ShapeDtypeStruct(x.shape, x.dtype) if total is None else jax.ShapeDtypeStruct(
+        x.shape[1:], total
+    )
     return pl.pallas_call(
-        functools.partial(_exchange_kernel, n, axis, stride),
-        out_shape=jax.ShapeDtypeStruct(x.shape, x.dtype),
+        functools.partial(_exchange_kernel, n, axis, stride, total),
+        out_shape=out,
         in_specs=[pl.BlockSpec(memory_space=pltpu.VMEM)],
         out_specs=pl.BlockSpec(memory_space=pltpu.VMEM),
         scratch_shapes=[
@@ -200,10 +209,8 @@
     )
     right_terms = right_terms.reshape(matrices, -1, pieces, width).transpose(0, 2, 1, 3)
     right_terms = right_terms.astype(jnp.bfloat16).reshape(cores, owners_count, -1, width)
-    right_half = jnp.sum(exchange(right_terms, "replica", 1).astype(jnp.float32), axis=0)
-    right_part = jnp.sum(
-        exchange(right_half.astype(jnp.bfloat16), "mp", 2).astype(jnp.float32), axis=0
-    )
+    right_half = exchange(right_terms, "replica", 1, total=jnp.bfloat16)
+    right_part = exchange(right_half, "mp", 2, total=jnp.float32)
     part_shape = right_part.shape
     right_part = allreduce_replica(right_part.reshape(chips, -1, lanes), 3, cores)
     right_part = right_part.reshape(part_shape).astype(jnp.bfloat16)

time: 135 us -> 130 us (0.963)
  Pallas kernels: 80 us -> 77.6 us
  other arithmetic: 9.78 us -> 8.31 us
    pallas_call x4, Pallas kernels: 43 us -> 39.7 us  [exchange(): pl.pallas_call(functools.partial(_exchange_kernel, n, axis, stride, total...]
    reduce_sum x2 -> x0, other arithmetic: 1.49 us -> none  [the longest x1 1.38 us: per_device(): jnp.sum(exchange(right_terms, 'replica', 1).astype(jnp.float32), axis=0)]
  transfers between devices with their start and end apart: 2 -> 2, of which waited for: 0 -> 0; matrix products, arithmetic and copies ran while one was open for 16% -> 15% of each run, Pallas kernels for 60% -> 60%
where the time goes in v10:
time: 130 us; the launch traced here: 129 us
  Pallas kernels  77.6 us (60%)
  between operations  16.9 us (13%)
  matrix products  14.9 us (11%)
  other arithmetic  8.31 us (6%)
  local copies, waits for them, and re-layouts  8.05 us (6%)
  starting transfers between devices  3.44 us (3%)
    pallas_call x4, Pallas kernels, exchange(): pl.pallas_call(functools.partial(_exchange_kernel, n, axis, stride, total...  39.7 us
    pallas_call x2, Pallas kernels, allreduce_replica(): pl.pallas_call(functools.partial(_allreduce_kernel, n, stride), out_shape...  37.9 us
    gather x1, local copies, waits for them, and re-layouts, per_device(): jnp.take(weight_slots, slots, axis=0).astype(jnp.float32)  4.44 us
    dot_general x1, matrix products, per_device(): jnp.einsum('kms,ksn->kmn', left_block, right_new, preferred_element_type=...  4.04 us
    ppermute x1, starting transfers between devices, per_device(): left_block = lax.ppermute(left_rows, ('replica', 'mp'), pairs)  3.4 us
    dot_general x1, matrix products, per_device(): jnp.einsum('kmn,knr->kmr', compensated, right_init, preferred_element_typ...  3.21 us
    dot_general x1, matrix products, per_device(): jnp.einsum('kmn,kms->ksn', compensated, left_rows, preferred_element_type...  3.09 us
  transfers between devices with their start and end apart: 2, of which 0 were waited for; matrix products, arithmetic and copies ran while one was open for 15% of the time, Pallas kernels for 60%

profile of v10, /device:TPU:1, one launch (start us, length us, event | category | flops | bytes accessed | tf_op | source)
XLA Modules:
  0.0 129.2 jit_solution(5025036391548081437)
XLA Ops:
  7.2 2.1 %subtract_convert_fusion.2 = bf16[1,1,48,3072]{3,2,1,0:T(8,128)(2,1)} fusion(f32[1,1,48,3072]{3,2,1,0:T(8,128)} %param.16, f32[1,1,48,3072]{3,2,1,0:T(8,128)} %param.15), kind=kLoop, calls=%fused_computation.12 | loop fusion | flops 442368 | bytes 1474560 | tf_op jit(solution)/shard_map/convert_element_type | solution.py:186
  9.4 3.2 %fusion.17 = f32[8,48,32]{2,1,0:T(8,128)S(1)} fusion(bf16[8,3072,32]{1,2,0:T(8,128)(2,1)S(1)} %copy-done, bf16[1,8,48,3072]{3,2,1,0:T(8,128)(2,1)} %param.11, bf16[1,8,48,3072]{3,2,1,0:T(8,128)(2,1)} %param.10), kind=kOutput, calls=%fused_computation.37 | convolution fusion | flops 80216064 | bytes 6340608 | tf_op jit(solution)/shard_map/kmn,knr->kmr/dot_general | solution.py:187
  12.6 0.1 reshape.149
  12.8 0.6 fusion.8.x_ref
  13.4 21.0 %shard_map.145 = f32[16,8,128]{2,1,0:T(8,128)} custom-call(f32[16,8,128]{2,1,0:T(8,128)} %fusion.8.x_ref), custom_call_target="tpu_custom_call" | custom-call | tf_op jit(solution)/shard_map/pallas_call | solution.py:140
  34.4 0.8 slice.7
  35.2 0.1 reshape.151
  35.3 0.5 convolution_convert_fusion.1
  35.8 3.4 %collective-permute-start = (bf16[8,48,32]{1,2,0:T(8,128)(2,1)S(1)}, bf16[8,48,32]{1,2,0:T(8,128)(2,1)S(1)}, u32[]{:S(2)}, u32[]{:S(2)}) collective-permute-start(bf16[8,48,32]{1,2,0:T(8,128)(2,1)S(1)} %convolution_convert_fusion.1), channel_id=1, source_target_pairs={{0,0},{1,16},{2,32},{3,48},{4,64},{5,80},{6,96},{7,112},{8,128},{9... | collective-permute-start | bytes 73736 | tf_op jit(solution)/shard_map/ppermute | solution.py:226
  39.2 3.1 %convolution_convert_fusion = bf16[8,32,3072]{2,1,0:T(8,128)(2,1)S(1)} fusion(bf16[8,48,32]{1,2,0:T(8,128)(2,1)S(1)} %convolution_convert_fusion.1, bf16[1,8,48,3072]{3,2,1,0:T(8,128)(2,1)} %param.11, bf16[1,8,48,3072]{3,2,1,0:T(8,128)(2,1)} %param.10), kind=kOutput, calls=%fused_computation.5 | convolution fusion | flops 81002496 | bytes 6316032 | tf_op jit(solution)/shard_map/kmn,kms->ksn/dot_general | solution.py:207
  42.3 0.2 copy.41
  42.5 2.7 %shard_map.146.x_ref = bf16[16,32,768]{2,1,0:T(8,128)(2,1)S(1)} custom-call(bf16[2,16,32,768]{3,2,1,0:T(8,128)(2,1)S(1)} %bitcast.50), custom_call_target="tpu_custom_call" | custom-call | tf_op jit(solution)/shard_map/pallas_call | solution.py:70
  45.1 17.8 %shard_map.147 = f32[32,768]{1,0:T(8,128)S(1)} custom-call(bf16[16,32,768]{2,1,0:T(8,128)(2,1)S(1)} %shard_map.146.x_ref), custom_call_target="tpu_custom_call" | custom-call | tf_op jit(solution)/shard_map/pallas_call | solution.py:70
  63.0 0.6 reshape.153.x_ref
  63.6 17.0 %shard_map.148 = f32[8,24,128]{2,1,0:T(8,128)} custom-call(f32[8,24,128]{2,1,0:T(8,128)} %reshape.153.x_ref), custom_call_target="tpu_custom_call" | custom-call | tf_op jit(solution)/shard_map/pallas_call | solution.py:140
  80.6 0.9 convert_element_type.114
  81.6 0.1 broadcast_in_dim.37.x_ref
  81.6 10.8 %shard_map.149 = bf16[16,32,768]{2,1,0:T(8,128)(2,1)S(1)} custom-call(bf16[16,32,768]{2,1,0:T(8,128)(2,1)S(1)} %broadcast_in_dim.37.x_ref), custom_call_target="tpu_custom_call" | custom-call | tf_op jit(solution)/shard_map/pallas_call | solution.py:70
  92.5 0.2 broadcast_in_dim.38.x_ref
  92.7 8.4 %shard_map.150 = bf16[2,16,32,768]{3,2,1,0:T(8,128)(2,1)S(1)} custom-call(bf16[2,16,32,768]{3,2,1,0:T(8,128)(2,1)S(1)} %broadcast_in_dim.38.x_ref), custom_call_target="tpu_custom_call" | custom-call | tf_op jit(solution)/shard_map/pallas_call | solution.py:70
  101.1 0.2 copy.39
  101.3 0.4 copy-done.8
  101.7 0.1 convert_reduce_fusion
  101.8 0.7 bitcast_reduce_fusion
  102.5 0.6 compare_and_fusion
  103.1 1.3 multiply_subtract_fusion
  104.4 2.3 %fusion = bf16[1,8,48,3072]{3,2,1,0:T(8,128)(2,1)} fusion(bf16[8,48,32]{1,2,0:T(8,128)(2,1)S(1)} %convolution_convert_fusion.1, bf16[8,32,3072]{2,1,0:T(8,128)(2,1)S(1)} %bitcast.52, bf16[1,8,48,3072]{3,2,1,0:T(8,128)(2,1)S(1)} %copy-done.1, bf16[1,8,48,3072]{3,2,1,0:T(8,128)(2,1)S(1)} %copy-done.2), kind=kOutput, calls=%fused_computation.4 | convolution fusion | flops 83755008 | bytes 8675328 | tf_op jit(solution)/shard_map/kms,ksn->kmn/dot_general | solution.py:227
  109.3 1.7 %convolution_add_fusion = f32[48,3072]{1,0:T(8,128)S(1)} fusion(f32[1,1,48,3072]{3,2,1,0:T(8,128)} %param.15, bf16[8,32,3072]{2,1,0:T(8,128)(2,1)S(1)} %bitcast.53, s32[]{:T(128)} %bitcast.9, f32[]{:T(128)S(6)} %convert_element_type.119, bf16[8,48,32]{1,2,0:T(8,128)(2,1)S(1)} %collective-permute-done), kind=kOutput, calls=%fused_computation.6 | convolution fusion | flops 57117696 | bytes 1386496 | tf_op jit(solution)/shard_map/cmr,crn->cmn/dot_general | solution.py:234
  111.1 0.8 copy-done.3
  111.9 1.9 %fusion.2 = f32[1,1,48,3072]{3,2,1,0:T(8,128)} fusion(f32[1,1,48,3072]{3,2,1,0:T(8,128)} %param.16, f32[48,3072]{1,0:T(8,128)S(1)} %convolution_add_fusion), kind=kLoop, calls=%fused_computation.11 | loop fusion | flops 294912 | bytes 1769472 | tf_op jit(solution)/shard_map/broadcast_in_dim | solution.py:248
  113.8 4.4 %gather_fusion = bf16[8,48,3072]{2,1,0:T(8,128)(2,1)} fusion(bf16[16,48,3072]{2,1,0:T(8,128)(2,1)} %bitcast.57, s32[1024]{0:T(1024)S(1)} %pad_clamp_fusion), kind=kCustom, calls=%fused_computation | custom fusion | bytes 4718624 | tf_op jit(solution)/shard_map/jit(_take)/gather | solution.py:241
  118.3 4.0 %subtract_convert_fusion = bf16[8,48,3072]{2,1,0:T(8,128)(2,1)} fusion(bf16[8,48,32]{1,2,0:T(8,128)(2,1)S(1)} %collective-permute-done, bf16[8,32,3072]{2,1,0:T(8,128)(2,1)S(1)} %bitcast.54, bf16[8,48,3072]{2,1,0:T(8,128)(2,1)} %gather_fusion, pred[8]{0:T(512)(128)(4,1)S(1)} %get-tuple-element.32), kind=kOutput, calls=%fused_computation.1 | convolution fusion | flops 81395712 | bytes 6316040 | tf_op jit(solution)/shard_map/kms,ksn->kmn/dot_general | solution.py:237
  (23 shorter events, 0.2 us)
Async XLA Ops:
  7.2 2.2 %copy-start = (bf16[8,3072,32]{1,2,0:T(8,128)(2,1)S(1)}, bf16[8,3072,32]{1,2,0:T(8,128)(2,1)}, u32[]{:S(2)}) copy-start(bf16[8,3072,32]{1,2,0:T(8,128)(2,1)} %param.12) | copy-start | bytes 4718596
  7.2 106.7 %all-gather.3.cloned.1.call-start = ((), (), s32[]{:S(2)}) async-start(), calls=%async_computation | async-start | bytes 5013504 | tf_op jit(solution)/shard_map/all_gather | solution.py:186
  9.4 3.4 %copy-start.7 = (f32[1,672]{1,0:T(1,128)S(1)}, f32[1,672]{1,0:T(1,128)}, u32[]{:S(2)}) copy-start(f32[1,672]{1,0:T(1,128)} %param.17) | copy-start | bytes 8068
  9.4 25.9 %copy-start.4 = (f32[8,32,32]{2,1,0:T(8,128)S(1)}, f32[8,32,32]{2,1,0:T(8,128)}, u32[]{:S(2)}) copy-start(f32[8,32,32]{2,1,0:T(8,128)} %param.13) | copy-start | bytes 98308
  35.8 73.5 %collective-permute-start = (bf16[8,48,32]{1,2,0:T(8,128)(2,1)S(1)}, bf16[8,48,32]{1,2,0:T(8,128)(2,1)S(1)}, u32[]{:S(2)}, u32[]{:S(2)}) collective-permute-start(bf16[8,48,32]{1,2,0:T(8,128)(2,1)S(1)} %convolution_convert_fusion.1), channel_id=1, source_target_pairs={{0,0},{1,16},{2,32},{3,48},{4,64},{5,80},{6,96},{7,112},{8,128},{9... | collective-permute-start | bytes 73736 | tf_op jit(solution)/shard_map/ppermute | solution.py:226
  92.6 11.8 %copy-start.2 = (bf16[1,8,48,3072]{3,2,1,0:T(8,128)(2,1)S(1)}, bf16[1,8,48,3072]{3,2,1,0:T(8,128)(2,1)}, u32[]{:S(2)}) copy-start(bf16[1,8,48,3072]{3,2,1,0:T(8,128)(2,1)} %param.10) | copy-start | bytes 7077892
  101.1 0.7 copy-start.8
  101.1 2.0 %copy-start.5 = (f32[672]{0:T(1024)S(1)}, f32[672]{0:T(1024)}, u32[]{:S(2)}) copy-start(f32[672]{0:T(1024)} %param.19) | copy-start | bytes 8068
  101.1 2.0 %copy-start.6 = (f32[672]{0:T(1024)S(1)}, f32[672]{0:T(1024)}, u32[]{:S(2)}) copy-start(f32[672]{0:T(1024)} %param.18) | copy-start | bytes 8068
  101.1 3.3 %copy-start.1 = (bf16[1,8,48,3072]{3,2,1,0:T(8,128)(2,1)S(1)}, bf16[1,8,48,3072]{3,2,1,0:T(8,128)(2,1)}, u32[]{:S(2)}) copy-start(bf16[1,8,48,3072]{3,2,1,0:T(8,128)(2,1)} %param.11) | copy-start | bytes 7077892
  111.1 0.8 copy-start.3
Sparse Core Ops, SparseCore 0:
  11.0 69.6 all-gather.2

commit v11 on v10

--- a/solution.py
+++ b/solution.py
@@ -153,6 +153,40 @@
     )(x)
 
 
+def _weights_kernel(slots_ref, base_hbm, left_ref, right_ref, o_ref, bases, sems):
+    matrices = left_ref.shape[0]
+    copies = []
+    for k in range(matrices):
+        copy = pltpu.make_async_copy(base_hbm.at[slots_ref[k]], bases.at[k], sems.at[k])
+        copy.start()
+        copies.append(copy)
+    for k in range(matrices):
+        copies[k].wait()
+        approx = jnp.dot(left_ref[k], right_ref[k], preferred_element_type=jnp.float32)
+        o_ref[k] = (bases[k].astype(jnp.float32) - 0.1 * approx).astype(o_ref.dtype)
+
+
+def weights_of(slots, base, left, right):
+    matrices, rows, _ = left.shape
+    shape = (matrices, rows, right.shape[2])
+    return pl.pallas_call(
+        _weights_kernel,
+        out_shape=jax.ShapeDtypeStruct(shape, base.dtype),
+        in_specs=[
+            pl.BlockSpec(memory_space=pltpu.SMEM),
+            pl.BlockSpec(memory_space=pl.ANY),
+            pl.BlockSpec(memory_space=pltpu.VMEM),
+            pl.BlockSpec(memory_space=pltpu.VMEM),
+        ],
+        out_specs=pl.BlockSpec(memory_space=pltpu.VMEM),
+        scratch_shapes=[
+            pltpu.VMEM(shape, base.dtype),
+            pltpu.SemaphoreType.DMA((matrices,)),
+        ],
+        compiler_params=pltpu.CompilerParams(vmem_limit_bytes=32 * 1024 * 1024),
+    )(slots, base, left, right)
+
+
 def per_device(
     gradients,
     feedback,
@@ -234,12 +268,7 @@
     approx_slots = jnp.einsum("cmr,crn->cmn", left_chosen, right_chosen, precision=highest)
     new_momentum = 0.9 * momentum[0] + approx_slots
     new_master = master_weights[0] - 0.1 * new_momentum
-    block_approx = jnp.einsum(
-        "kms,ksn->kmn", left_block, right_new, preferred_element_type=jnp.float32
-    )
-    new_weights = (
-        jnp.take(weight_slots, slots, axis=0).astype(jnp.float32) - 0.1 * block_approx
-    ).astype(jnp.bfloat16)
+    new_weights = weights_of(slots, weight_slots, left_block, right_new)
     new_vector_momentum = 0.9 * vector_momentum + vector_total
     new_vector_params = vector_params - 0.1 * new_vector_momentum
     return (

time: 130 us -> 135 us (1.038)
  Pallas kernels: 77.6 us -> 81.3 us
  local copies, waits for them, and re-layouts: 8.05 us -> 10.9 us
  matrix products: 14.9 us -> 13.2 us
    pallas_call x2, Pallas kernels: 37.9 us -> 32.8 us  [allreduce_replica(): pl.pallas_call(functools.partial(_allreduce_kernel, n, stride), out_shape...]
    pallas_call x4, Pallas kernels: 39.7 us -> 44.2 us  [exchange(): pl.pallas_call(functools.partial(_exchange_kernel, n, axis, stride, total...]
    gather x1 -> x0, local copies, waits for them, and re-layouts: 4.44 us -> none  [per_device(): jnp.take(weight_slots, slots, axis=0).astype(jnp.float32)]
    pallas_call x0 -> x1, Pallas kernels: none -> 4.27 us  [weights_of(): pl.pallas_call(_weights_kernel, out_shape=jax.ShapeDtypeStruct(shape, bas...]
    dot_general x1 -> x0, matrix products: 4.04 us -> none  [per_device(): jnp.einsum('kms,ksn->kmn', left_block, right_new, preferred_element_type=...]
    reshape x1, local copies, waits for them, and re-layouts: 0.19 us -> 3.12 us  [per_device(): right_new = right_new.reshape(matrices, -1, compensated.shape[2])]
    dot_general x1, matrix products: 2.32 us -> 4.69 us  [per_device(): jnp.einsum('kms,ksn->kmn', left_rows, right_new, preferred_element_type=j...]
    reshape x0 -> x1, local copies, waits for them, and re-layouts: none -> 2.36 us  [per_device(): right_new.reshape(matrices, pieces, -1, width).transpose(0, 2, 1, 3)]
  transfers between devices with their start and end apart: 2 -> 2, of which waited for: 0 -> 0; matrix products, arithmetic and copies ran while one was open for 15% -> 20% of each run, Pallas kernels for 60% -> 57%
where the time goes in v11:
time: 135 us; the launch traced here: 134 us
  Pallas kernels  81.3 us (60%)
  between operations  16.9 us (13%)
  matrix products  13.2 us (10%)
  local copies, waits for them, and re-layouts  10.9 us (8%)
  other arithmetic  8.29 us (6%)
  starting transfers between devices  3.44 us (3%)
    pallas_call x4, Pallas kernels, exchange(): pl.pallas_call(functools.partial(_exchange_kernel, n, axis, stride, total...  44.2 us
    pallas_call x2, Pallas kernels, allreduce_replica(): pl.pallas_call(functools.partial(_allreduce_kernel, n, stride), out_shape...  32.8 us
    dot_general x1, matrix products, per_device(): jnp.einsum('kms,ksn->kmn', left_rows, right_new, preferred_element_type=j...  4.69 us
    pallas_call x1, Pallas kernels, weights_of(): pl.pallas_call(_weights_kernel, out_shape=jax.ShapeDtypeStruct(shape, bas...  4.27 us
    ppermute x1, starting transfers between devices, per_device(): left_block = lax.ppermute(left_rows, ('replica', 'mp'), pairs)  3.4 us
    dot_general x1, matrix products, per_device(): jnp.einsum('kmn,knr->kmr', compensated, right_init, preferred_element_typ...  3.21 us
    unnamed x16, local copies, waits for them, and re-layouts  3.18 us
    reshape x1, local copies, waits for them, and re-layouts, per_device(): right_new = right_new.reshape(matrices, -1, compensated.shape[2])  3.12 us
  transfers between devices with their start and end apart: 2, of which 0 were waited for; matrix products, arithmetic and copies ran while one was open for 20% of the time, Pallas kernels for 57%

profile of v11, /device:TPU:1, one launch (start us, length us, event | category | flops | bytes accessed | tf_op | source)
XLA Modules:
  0.0 134.0 jit_solution(587123186503653225)
XLA Ops:
  7.2 2.1 %subtract_convert_fusion.1 = bf16[1,1,48,3072]{3,2,1,0:T(8,128)(2,1)} fusion(f32[1,1,48,3072]{3,2,1,0:T(8,128)} %param.16, f32[1,1,48,3072]{3,2,1,0:T(8,128)} %param.15), kind=kLoop, calls=%fused_computation.11 | loop fusion | flops 442368 | bytes 1474560 | tf_op jit(solution)/shard_map/convert_element_type | solution.py:220
  9.4 3.2 %fusion.17 = f32[8,48,32]{2,1,0:T(8,128)S(1)} fusion(bf16[8,3072,32]{1,2,0:T(8,128)(2,1)S(1)} %copy-done, bf16[1,8,48,3072]{3,2,1,0:T(8,128)(2,1)} %param.11, bf16[1,8,48,3072]{3,2,1,0:T(8,128)(2,1)} %param.10), kind=kOutput, calls=%fused_computation.33 | convolution fusion | flops 80216064 | bytes 6340608 | tf_op jit(solution)/shard_map/kmn,knr->kmr/dot_general | solution.py:221
  12.6 0.1 reshape.144
  12.8 0.6 fusion.8.x_ref
  13.4 21.0 %shard_map.145 = f32[16,8,128]{2,1,0:T(8,128)} custom-call(f32[16,8,128]{2,1,0:T(8,128)} %fusion.8.x_ref), custom_call_target="tpu_custom_call" | custom-call | tf_op jit(solution)/shard_map/pallas_call | solution.py:140
  34.4 0.8 slice.7
  35.2 0.1 reshape.146
  35.3 0.5 convolution_convert_fusion.1
  35.8 0.1 copy.56
  35.9 3.4 %collective-permute-start = (bf16[8,48,32]{2,1,0:T(8,128)(2,1)S(1)}, bf16[8,48,32]{2,1,0:T(8,128)(2,1)S(1)}, u32[]{:S(2)}, u32[]{:S(2)}) collective-permute-start(bf16[8,48,32]{2,1,0:T(8,128)(2,1)S(1)} %copy.56), channel_id=1, source_target_pairs={{0,0},{1,16},{2,32},{3,48},{4,64},{5,80},{6,96},{7,112},{8,128},{9... | collective-permute-start | bytes 73736 | tf_op jit(solution)/shard_map/ppermute | solution.py:260
  39.3 3.1 %convolution_convert_fusion = bf16[8,32,3072]{2,1,0:T(8,128)(2,1)S(1)} fusion(bf16[8,48,32]{1,2,0:T(8,128)(2,1)S(1)} %convolution_convert_fusion.1, bf16[1,8,48,3072]{3,2,1,0:T(8,128)(2,1)} %param.11, bf16[1,8,48,3072]{3,2,1,0:T(8,128)(2,1)} %param.10), kind=kOutput, calls=%fused_computation.3 | convolution fusion | flops 81002496 | bytes 6316032 | tf_op jit(solution)/shard_map/kmn,kms->ksn/dot_general | solution.py:241
  42.4 0.2 copy.63
  42.6 2.7 %shard_map.146.x_ref = bf16[16,32,768]{2,1,0:T(8,128)(2,1)S(1)} custom-call(bf16[2,16,32,768]{3,2,1,0:T(8,128)(2,1)S(1)} %bitcast.47), custom_call_target="tpu_custom_call" | custom-call | tf_op jit(solution)/shard_map/pallas_call | solution.py:70
  45.3 21.0 %shard_map.147 = f32[32,768]{1,0:T(8,128)S(1)} custom-call(bf16[16,32,768]{2,1,0:T(8,128)(2,1)S(1)} %shard_map.146.x_ref), custom_call_target="tpu_custom_call" | custom-call | tf_op jit(solution)/shard_map/pallas_call | solution.py:70
  66.3 0.6 reshape.148.x_ref
  66.9 11.9 %shard_map.148 = f32[8,24,128]{2,1,0:T(8,128)} custom-call(f32[8,24,128]{2,1,0:T(8,128)} %reshape.148.x_ref), custom_call_target="tpu_custom_call" | custom-call | tf_op jit(solution)/shard_map/pallas_call | solution.py:140
  78.8 0.9 convert_element_type.108
  79.9 11.7 %shard_map.149 = bf16[16,32,768]{2,1,0:T(8,128)(2,1)S(1)} custom-call(bf16[16,32,768]{2,1,0:T(8,128)(2,1)S(1)} %broadcast_in_dim.12.x_ref), custom_call_target="tpu_custom_call" | custom-call | tf_op jit(solution)/shard_map/pallas_call | solution.py:70
  91.6 0.2 broadcast_in_dim.26.x_ref
  91.8 8.8 %shard_map.150 = bf16[2,16,32,768]{3,2,1,0:T(8,128)(2,1)S(1)} custom-call(bf16[2,16,32,768]{3,2,1,0:T(8,128)(2,1)S(1)} %broadcast_in_dim.26.x_ref), custom_call_target="tpu_custom_call" | custom-call | tf_op jit(solution)/shard_map/pallas_call | solution.py:70
  100.6 2.4 %copy.64 = bf16[8,4,32,768]{3,1,2,0:T(4,128)(2,1)} copy(bf16[8,4,32,768]{3,2,1,0:T(8,128)(2,1)S(1)} %bitcast.48) | data formatting | bytes 3145728 | tf_op jit(solution)/shard_map/reshape | solution.py:253
  102.9 3.1 %reshape.150.right_ref = bf16[8,32,3072]{2,1,0:T(8,128)(2,1)S(1)} reshape(bf16[8,32,4,768]{3,2,1,0:T(4,128)(2,1)} %bitcast.50) | data formatting | bytes 3145728 | tf_op jit(solution)/shard_map/reshape | solution.py:254
  106.1 0.1 convert_reduce_fusion
  106.2 0.6 compare_reduce_fusion
  106.8 1.3 multiply_subtract_fusion
  108.1 4.7 %fusion = bf16[1,8,48,3072]{3,2,1,0:T(8,128)(2,1)} fusion(bf16[8,48,32]{1,2,0:T(8,128)(2,1)S(1)} %convolution_convert_fusion.1, bf16[8,32,3072]{2,1,0:T(8,128)(2,1)S(1)} %reshape.150.right_ref, bf16[1,8,48,3072]{3,2,1,0:T(8,128)(2,1)} %param.11, bf16[1,8,48,3072]{3,2,1,0:T(8,128)(2,1)} %param.10), kind=kOutput, calls=%fused_computation.2 | convolution fusion | flops 83755008 | bytes 8675328 | tf_op jit(solution)/shard_map/kms,ksn->kmn/dot_general | solution.py:261
  112.8 0.7 bitcast_reduce_fusion
  116.0 1.7 %convolution_add_fusion = f32[48,3072]{1,0:T(8,128)S(1)} fusion(f32[1,1,48,3072]{3,2,1,0:T(8,128)} %param.15, bf16[8,32,3072]{2,1,0:T(8,128)(2,1)S(1)} %reshape.150.right_ref, s32[]{:T(128)} %bitcast.9, f32[]{:T(128)S(6)} %convert_element_type.113, bf16[8,48,32]{2,1,0:T(8,128)(2,1)S(1)} %collective-permute-done.left_ref), kind=kOutput, calls=%fused_computation.4 | convolution fusion | flops 57117696 | bytes 1390592 | tf_op jit(solution)/shard_map/cmr,crn->cmn/dot_general | solution.py:268
  117.8 0.8 copy-done.2
  118.6 1.9 %fusion.2 = f32[1,1,48,3072]{3,2,1,0:T(8,128)} fusion(f32[1,1,48,3072]{3,2,1,0:T(8,128)} %param.16, f32[48,3072]{1,0:T(8,128)S(1)} %convolution_add_fusion), kind=kLoop, calls=%fused_computation.10 | loop fusion | flops 294912 | bytes 1769472 | tf_op jit(solution)/shard_map/broadcast_in_dim | solution.py:277
  120.5 2.3 %copy-done.1 = bf16[16,1,48,3072]{3,2,1,0:T(8,128)(2,1)S(1)} copy-done((bf16[16,1,48,3072]{3,2,1,0:T(8,128)(2,1)S(1)}, bf16[16,1,48,3072]{3,2,1,0:T(8,128)(2,1)}, u32[]{:S(2)}) %copy-start.1) | copy-done | bytes 4718616
  122.9 4.3 %shard_map.151 = bf16[8,48,3072]{2,1,0:T(8,128)(2,1)} custom-call(s32[8]{0:T(128)S(1)} %get-tuple-element.33.slots_ref, bf16[16,48,3072]{2,1,0:T(8,128)(2,1)S(1)} %bitcast.49, bf16[8,48,32]{2,1,0:T(8,128)(2,1)S(1)} %collective-permute-done.left_ref, bf16[8,32,3072]{2,1,0:T(8,128)(2,1)S(1)} %reshape.150.right_ref), custom_call_target="tpu_custom_call" | custom-call | tf_op jit(solution)/shard_map/pallas_call | solution.py:172
  (21 shorter events, 0.3 us)
Async XLA Ops:
  7.2 2.2 %copy-start = (bf16[8,3072,32]{1,2,0:T(8,128)(2,1)S(1)}, bf16[8,3072,32]{1,2,0:T(8,128)(2,1)}, u32[]{:S(2)}) copy-start(bf16[8,3072,32]{1,2,0:T(8,128)(2,1)} %param.12) | copy-start | bytes 4718596
  7.2 113.3 %all-gather.3.cloned.1.call-start = ((), (), s32[]{:S(2)}) async-start(), calls=%async_computation | async-start | bytes 5013504 | tf_op jit(solution)/shard_map/all_gather | solution.py:220
  9.4 3.4 %copy-start.6 = (f32[1,672]{1,0:T(1,128)S(1)}, f32[1,672]{1,0:T(1,128)}, u32[]{:S(2)}) copy-start(f32[1,672]{1,0:T(1,128)} %param.17) | copy-start | bytes 8068
  9.4 25.9 %copy-start.3 = (f32[8,32,32]{2,1,0:T(8,128)S(1)}, f32[8,32,32]{2,1,0:T(8,128)}, u32[]{:S(2)}) copy-start(f32[8,32,32]{2,1,0:T(8,128)} %param.13) | copy-start | bytes 98308
  35.9 80.1 %collective-permute-start = (bf16[8,48,32]{2,1,0:T(8,128)(2,1)S(1)}, bf16[8,48,32]{2,1,0:T(8,128)(2,1)S(1)}, u32[]{:S(2)}, u32[]{:S(2)}) collective-permute-start(bf16[8,48,32]{2,1,0:T(8,128)(2,1)S(1)} %copy.56), channel_id=1, source_target_pairs={{0,0},{1,16},{2,32},{3,48},{4,64},{5,80},{6,96},{7,112},{8,128},{9... | collective-permute-start | bytes 73736 | tf_op jit(solution)/shard_map/ppermute | solution.py:260
  102.9 3.1 %copy-start.7 = (s32[8]{0:T(128)S(1)}, s32[8]{0:T(128)}, u32[]{:S(2)}) copy-start(s32[8]{0:T(128)} %param.14) | copy-start | bytes 100
  102.9 3.9 %copy-start.4 = (f32[672]{0:T(1024)S(1)}, f32[672]{0:T(1024)}, u32[]{:S(2)}) copy-start(f32[672]{0:T(1024)} %param.19) | copy-start | bytes 8068
  102.9 3.9 %copy-start.5 = (f32[672]{0:T(1024)S(1)}, f32[672]{0:T(1024)}, u32[]{:S(2)}) copy-start(f32[672]{0:T(1024)} %param.18) | copy-start | bytes 8068
  117.8 0.8 copy-start.2
  120.5 2.3 %copy-start.1 = (bf16[16,1,48,3072]{3,2,1,0:T(8,128)(2,1)S(1)}, bf16[16,1,48,3072]{3,2,1,0:T(8,128)(2,1)}, u32[]{:S(2)}) copy-start(bf16[16,1,48,3072]{3,2,1,0:T(8,128)(2,1)} %all-gather.3.cloned.1.call-done) | copy-start | bytes 14155780
Sparse Core Ops, SparseCore 0:
  10.4 71.0 all-gather.2

commit v12 on v10

--- a/solution.py
+++ b/solution.py
@@ -238,7 +238,13 @@
         "kms,ksn->kmn", left_block, right_new, preferred_element_type=jnp.float32
     )
     new_weights = (
-        jnp.take(weight_slots, slots, axis=0).astype(jnp.float32) - 0.1 * block_approx
+        jnp.stack(
+            [
+                lax.dynamic_index_in_dim(weight_slots, slots[k], 0, keepdims=False)
+                for k in range(matrices)
+            ]
+        ).astype(jnp.float32)
+        - 0.1 * block_approx
     ).astype(jnp.bfloat16)
     new_vector_momentum = 0.9 * vector_momentum + vector_total
     new_vector_params = vector_params - 0.1 * new_vector_momentum

time: 130 us -> 147 us (1.13)
  between operations: 16.9 us -> 31.7 us
  local copies, waits for them, and re-layouts: 8.05 us -> 12.2 us
  matrix products: 14.9 us -> 13.2 us
    unnamed x18 -> x25, local copies, waits for them, and re-layouts: 1.27 us -> 8.19 us
    gather x1 -> x0, local copies, waits for them, and re-layouts: 4.44 us -> none  [per_device(): jnp.take(weight_slots, slots, axis=0).astype(jnp.float32)]
    dot_general x1, matrix products: 4.04 us -> 2.22 us  [per_device(): jnp.einsum('kms,ksn->kmn', left_block, right_new, preferred_element_type=...]
  transfers between devices with their start and end apart: 2 -> 2, of which waited for: 0 -> 0; matrix products, arithmetic and copies ran while one was open for 15% -> 14% of each run, Pallas kernels for 60% -> 53%
where the time goes in v12:
time: 147 us; the launch traced here: 146 us
  Pallas kernels  77.6 us (53%)
  between operations  31.7 us (22%)
  matrix products  13.2 us (9%)
  local copies, waits for them, and re-layouts  12.2 us (8%)
  other arithmetic  8.3 us (6%)
  starting transfers between devices  3.44 us (2%)
    pallas_call x4, Pallas kernels, exchange(): pl.pallas_call(functools.partial(_exchange_kernel, n, axis, stride, total...  39.7 us
    pallas_call x2, Pallas kernels, allreduce_replica(): pl.pallas_call(functools.partial(_allreduce_kernel, n, stride), out_shape...  37.9 us
    unnamed x25, local copies, waits for them, and re-layouts  8.19 us
    ppermute x1, starting transfers between devices, per_device(): left_block = lax.ppermute(left_rows, ('replica', 'mp'), pairs)  3.4 us
    dot_general x1, matrix products, per_device(): jnp.einsum('kmn,knr->kmr', compensated, right_init, preferred_element_typ...  3.21 us
    dot_general x1, matrix products, per_device(): jnp.einsum('kmn,kms->ksn', compensated, left_rows, preferred_element_type...  3.09 us
  transfers between devices with their start and end apart: 2, of which 0 were waited for; matrix products, arithmetic and copies ran while one was open for 14% of the time, Pallas kernels for 53%

profile of v12, /device:TPU:1, one launch (start us, length us, event | category | flops | bytes accessed | tf_op | source)
XLA Modules:
  0.0 146.4 jit_solution(9082756321104947255)
XLA Ops:
  7.2 2.1 %subtract_convert_fusion.2 = bf16[1,1,48,3072]{3,2,1,0:T(8,128)(2,1)} fusion(f32[1,1,48,3072]{3,2,1,0:T(8,128)} %param.16, f32[1,1,48,3072]{3,2,1,0:T(8,128)} %param.15), kind=kLoop, calls=%fused_computation.11 | loop fusion | flops 442368 | bytes 1474560 | tf_op jit(solution)/shard_map/convert_element_type | solution.py:186
  9.4 3.2 %fusion.17 = f32[8,48,32]{2,1,0:T(8,128)S(1)} fusion(bf16[8,3072,32]{1,2,0:T(8,128)(2,1)S(1)} %copy-done, bf16[1,8,48,3072]{3,2,1,0:T(8,128)(2,1)} %param.11, bf16[1,8,48,3072]{3,2,1,0:T(8,128)(2,1)} %param.10), kind=kOutput, calls=%fused_computation.41 | convolution fusion | flops 80216064 | bytes 6340608 | tf_op jit(solution)/shard_map/kmn,knr->kmr/dot_general | solution.py:187
  12.8 0.6 fusion.8.x_ref
  13.4 21.0 %shard_map.145 = f32[16,8,128]{2,1,0:T(8,128)} custom-call(f32[16,8,128]{2,1,0:T(8,128)} %fusion.8.x_ref), custom_call_target="tpu_custom_call" | custom-call | tf_op jit(solution)/shard_map/pallas_call | solution.py:140
  34.4 0.8 slice.31
  35.3 0.5 convolution_convert_fusion.1
  35.8 3.4 %collective-permute-start = (bf16[8,48,32]{1,2,0:T(8,128)(2,1)S(1)}, bf16[8,48,32]{1,2,0:T(8,128)(2,1)S(1)}, u32[]{:S(2)}, u32[]{:S(2)}) collective-permute-start(bf16[8,48,32]{1,2,0:T(8,128)(2,1)S(1)} %convolution_convert_fusion.1), channel_id=1, source_target_pairs={{0,0},{1,16},{2,32},{3,48},{4,64},{5,80},{6,96},{7,112},{8,128},{9... | collective-permute-start | bytes 73736 | tf_op jit(solution)/shard_map/ppermute | solution.py:226
  39.2 3.1 %convolution_convert_fusion = bf16[8,32,3072]{2,1,0:T(8,128)(2,1)S(1)} fusion(bf16[8,48,32]{1,2,0:T(8,128)(2,1)S(1)} %convolution_convert_fusion.1, bf16[1,8,48,3072]{3,2,1,0:T(8,128)(2,1)} %param.11, bf16[1,8,48,3072]{3,2,1,0:T(8,128)(2,1)} %param.10), kind=kOutput, calls=%fused_computation.4 | convolution fusion | flops 81002496 | bytes 6316032 | tf_op jit(solution)/shard_map/kmn,kms->ksn/dot_general | solution.py:207
  42.5 2.7 %shard_map.146.x_ref = bf16[16,32,768]{2,1,0:T(8,128)(2,1)S(1)} custom-call(bf16[2,16,32,768]{3,2,1,0:T(8,128)(2,1)S(1)} %bitcast.73), custom_call_target="tpu_custom_call" | custom-call | tf_op jit(solution)/shard_map/pallas_call | solution.py:70
  45.1 17.8 %shard_map.147 = f32[32,768]{1,0:T(8,128)S(1)} custom-call(bf16[16,32,768]{2,1,0:T(8,128)(2,1)S(1)} %shard_map.146.x_ref), custom_call_target="tpu_custom_call" | custom-call | tf_op jit(solution)/shard_map/pallas_call | solution.py:70
  63.0 0.6 reshape.148.x_ref
  63.6 17.0 %shard_map.148 = f32[8,24,128]{2,1,0:T(8,128)} custom-call(f32[8,24,128]{2,1,0:T(8,128)} %reshape.148.x_ref), custom_call_target="tpu_custom_call" | custom-call | tf_op jit(solution)/shard_map/pallas_call | solution.py:140
  80.6 0.9 convert_element_type.114
  81.6 10.8 %shard_map.149 = bf16[16,32,768]{2,1,0:T(8,128)(2,1)S(1)} custom-call(bf16[16,32,768]{2,1,0:T(8,128)(2,1)S(1)} %broadcast_in_dim.12.x_ref), custom_call_target="tpu_custom_call" | custom-call | tf_op jit(solution)/shard_map/pallas_call | solution.py:70
  92.7 8.4 %shard_map.150 = bf16[2,16,32,768]{3,2,1,0:T(8,128)(2,1)S(1)} custom-call(bf16[2,16,32,768]{3,2,1,0:T(8,128)(2,1)S(1)} %broadcast_in_dim.26.x_ref), custom_call_target="tpu_custom_call" | custom-call | tf_op jit(solution)/shard_map/pallas_call | solution.py:70
  101.8 0.6 compare_reduce_fusion
  102.4 0.7 bitcast_reduce_fusion
  103.1 1.3 multiply_subtract_fusion
  104.4 2.4 %fusion = bf16[1,8,48,3072]{3,2,1,0:T(8,128)(2,1)} fusion(bf16[8,48,32]{1,2,0:T(8,128)(2,1)S(1)} %convolution_convert_fusion.1, bf16[8,32,3072]{2,1,0:T(8,128)(2,1)S(1)} %bitcast.75, bf16[1,8,48,3072]{3,2,1,0:T(8,128)(2,1)S(1)} %copy-done.1, bf16[1,8,48,3072]{3,2,1,0:T(8,128)(2,1)S(1)} %copy-done.2), kind=kOutput, calls=%fused_computation.3 | convolution fusion | flops 83755008 | bytes 8675328 | tf_op jit(solution)/shard_map/kms,ksn->kmn/dot_general | solution.py:227
  106.8 0.7 fusion.19
  124.9 1.7 %convolution_add_fusion = f32[48,3072]{1,0:T(8,128)S(1)} fusion(f32[1,1,48,3072]{3,2,1,0:T(8,128)} %param.15, bf16[8,32,3072]{2,1,0:T(8,128)(2,1)S(1)} %bitcast.76, s32[]{:T(128)} %bitcast.9, f32[]{:T(128)S(6)} %convert_element_type.119, bf16[8,48,32]{1,2,0:T(8,128)(2,1)S(1)} %collective-permute-done), kind=kOutput, calls=%fused_computation.5 | convolution fusion | flops 57117696 | bytes 1386496 | tf_op jit(solution)/shard_map/cmr,crn->cmn/dot_general | solution.py:234
  126.6 0.8 copy-done.3
  127.4 1.9 %fusion.2 = f32[1,1,48,3072]{3,2,1,0:T(8,128)} fusion(f32[1,1,48,3072]{3,2,1,0:T(8,128)} %param.16, f32[48,3072]{1,0:T(8,128)S(1)} %convolution_add_fusion), kind=kLoop, calls=%fused_computation.10 | loop fusion | flops 294912 | bytes 1769472 | tf_op jit(solution)/shard_map/broadcast_in_dim | solution.py:254
  129.4 1.0 bitcast_dynamic-update-slice_fusion.7
  130.4 1.0 bitcast_dynamic-update-slice_fusion.6
  131.4 1.0 bitcast_dynamic-update-slice_fusion.5
  132.4 1.0 bitcast_dynamic-update-slice_fusion.4
  133.4 1.0 bitcast_dynamic-update-slice_fusion.3
  134.3 1.0 bitcast_dynamic-update-slice_fusion.2
  135.3 1.0 bitcast_dynamic-update-slice_fusion.1
  136.3 1.0 bitcast_dynamic-update-slice_fusion
  137.3 2.2 %subtract_convert_fusion = bf16[8,48,3072]{2,1,0:T(8,128)(2,1)} fusion(bf16[8,48,3072]{2,1,0:T(8,128)(2,1)S(1)} %bitcast_dynamic-update-slice_fusion, bf16[8,48,32]{1,2,0:T(8,128)(2,1)S(1)} %collective-permute-done, bf16[8,32,3072]{2,1,0:T(8,128)(2,1)S(1)} %bitcast.77), kind=kOutput, calls=%fused_computation | convolution fusion | flops 80216064 | bytes 6316032 | tf_op jit(solution)/shard_map/kms,ksn->kmn/dot_general | solution.py:237
  (30 shorter events, 1.5 us)
Async XLA Ops:
  7.2 2.2 %copy-start = (bf16[8,3072,32]{1,2,0:T(8,128)(2,1)S(1)}, bf16[8,3072,32]{1,2,0:T(8,128)(2,1)}, u32[]{:S(2)}) copy-start(bf16[8,3072,32]{1,2,0:T(8,128)(2,1)} %param.12) | copy-start | bytes 4718596
  7.2 122.2 %all-gather.3.cloned.1.call-start = ((), (), s32[]{:S(2)}) async-start(), calls=%async_computation | async-start | bytes 5013504 | tf_op jit(solution)/shard_map/all_gather | solution.py:186
  9.4 3.4 %copy-start.7 = (f32[1,672]{1,0:T(1,128)S(1)}, f32[1,672]{1,0:T(1,128)}, u32[]{:S(2)}) copy-start(f32[1,672]{1,0:T(1,128)} %param.17) | copy-start | bytes 8068
  9.4 25.9 %copy-start.4 = (f32[8,32,32]{2,1,0:T(8,128)S(1)}, f32[8,32,32]{2,1,0:T(8,128)}, u32[]{:S(2)}) copy-start(f32[8,32,32]{2,1,0:T(8,128)} %param.13) | copy-start | bytes 98308
  35.8 89.1 %collective-permute-start = (bf16[8,48,32]{1,2,0:T(8,128)(2,1)S(1)}, bf16[8,48,32]{1,2,0:T(8,128)(2,1)S(1)}, u32[]{:S(2)}, u32[]{:S(2)}) collective-permute-start(bf16[8,48,32]{1,2,0:T(8,128)(2,1)S(1)} %convolution_convert_fusion.1), channel_id=1, source_target_pairs={{0,0},{1,16},{2,32},{3,48},{4,64},{5,80},{6,96},{7,112},{8,128},{9... | collective-permute-start | bytes 73736 | tf_op jit(solution)/shard_map/ppermute | solution.py:226
  92.6 11.8 %copy-start.2 = (bf16[1,8,48,3072]{3,2,1,0:T(8,128)(2,1)S(1)}, bf16[1,8,48,3072]{3,2,1,0:T(8,128)(2,1)}, u32[]{:S(2)}) copy-start(bf16[1,8,48,3072]{3,2,1,0:T(8,128)(2,1)} %param.10) | copy-start | bytes 7077892
  101.1 0.7 copy-start.8
  101.1 2.0 %copy-start.5 = (f32[672]{0:T(1024)S(1)}, f32[672]{0:T(1024)}, u32[]{:S(2)}) copy-start(f32[672]{0:T(1024)} %param.19) | copy-start | bytes 8068
  101.1 2.0 %copy-start.6 = (f32[672]{0:T(1024)S(1)}, f32[672]{0:T(1024)}, u32[]{:S(2)}) copy-start(f32[672]{0:T(1024)} %param.18) | copy-start | bytes 8068
  101.1 3.3 %copy-start.1 = (bf16[1,8,48,3072]{3,2,1,0:T(8,128)(2,1)S(1)}, bf16[1,8,48,3072]{3,2,1,0:T(8,128)(2,1)}, u32[]{:S(2)}) copy-start(bf16[1,8,48,3072]{3,2,1,0:T(8,128)(2,1)} %param.11) | copy-start | bytes 7077892
  126.6 0.8 copy-start.3
Sparse Core Ops, SparseCore 0:
  11.0 69.6 all-gather.2

commit v13 on v10

--- a/solution.py
+++ b/solution.py
@@ -153,6 +153,120 @@
     )(x)
 
 
+def _reduce_kernel(n, chips, x_ref, o_ref, recv, acc, first, middle, second, mp_sem, z_sem):
+    rank = lax.axis_index("replica")
+    me = lax.axis_index("mp")
+    spot = lax.rem(lax.div(rank, 2), chips)
+    base = rank - spot * 2
+    rows, cols = first.shape[1], first.shape[2]
+
+    def chip(peer):
+        return (base + peer * 2, me)
+
+    def piece(p):
+        r = pl.multiple_of(lax.div(p, 2) * rows, rows)
+        c = pl.multiple_of(lax.rem(p, 2) * cols, cols)
+        return acc.at[pl.ds(r, rows), pl.ds(c, cols)]
+
+    barrier = pltpu.get_barrier_semaphore()
+    for d in range(1, n):
+        peer = lax.rem(me + d, n)
+        pl.semaphore_signal(barrier, inc=1, device_id=(rank, peer), device_id_type=MESH_IDS)
+    for d in range(1, chips):
+        peer = lax.rem(spot + d, chips)
+        pl.semaphore_signal(barrier, inc=1, device_id=chip(peer), device_id_type=MESH_IDS)
+    pl.semaphore_wait(barrier, n - 1 + chips - 1)
+    copies = []
+    for d in range(1, n):
+        peer = lax.rem(me + d, n)
+        copy = pltpu.make_async_remote_copy(
+            src_ref=x_ref.at[peer],
+            dst_ref=recv.at[me],
+            send_sem=mp_sem.at[0, d],
+            recv_sem=mp_sem.at[1, me],
+            device_id=(rank, peer),
+            device_id_type=MESH_IDS,
+        )
+        copy.start()
+        copies.append(copy)
+    recv[me] = x_ref[me]
+    for d in range(1, n):
+        source = lax.rem(me + n - d, n)
+        pltpu.make_async_remote_copy(
+            src_ref=x_ref.at[source],
+            dst_ref=recv.at[source],
+            send_sem=mp_sem.at[0, d],
+            recv_sem=mp_sem.at[1, source],
+            device_id=(rank, source),
+            device_id_type=MESH_IDS,
+        ).wait_recv()
+    for copy in copies:
+        copy.wait_send()
+    total = recv[0].astype(jnp.float32)
+    for s in range(1, n):
+        total = total + recv[s].astype(jnp.float32)
+    acc[...] = total
+
+    def round_trip(phase, source_of, landing):
+        sent = []
+        for d in range(1, chips):
+            peer = lax.rem(spot + d, chips)
+            copy = pltpu.make_async_remote_copy(
+                src_ref=source_of(peer),
+                dst_ref=landing.at[spot],
+                send_sem=z_sem.at[phase, 0, d],
+                recv_sem=z_sem.at[phase, 1, spot],
+                device_id=chip(peer),
+                device_id_type=MESH_IDS,
+            )
+            copy.start()
+            sent.append(copy)
+        landing[spot] = source_of(spot)[...]
+        for d in range(1, chips):
+            source = lax.rem(spot + chips - d, chips)
+            pltpu.make_async_remote_copy(
+                src_ref=source_of(source),
+                dst_ref=landing.at[source],
+                send_sem=z_sem.at[phase, 0, d],
+                recv_sem=z_sem.at[phase, 1, source],
+                device_id=chip(source),
+                device_id_type=MESH_IDS,
+            ).wait_recv()
+        for copy in sent:
+            copy.wait_send()
+
+    round_trip(0, piece, first)
+    part = first[0]
+    for s in range(1, chips):
+        part = part + first[s]
+    middle[...] = part
+    round_trip(1, lambda peer: middle, second)
+    o_ref[...] = second[...]
+
+
+def reduce_right(x, chips, cid):
+    n = x.shape[0]
+    rows, cols = x.shape[1] // (chips // 2), x.shape[2] // 2
+    return pl.pallas_call(
+        functools.partial(_reduce_kernel, n, chips),
+        out_shape=jax.ShapeDtypeStruct((chips, rows, cols), jnp.float32),
+        in_specs=[pl.BlockSpec(memory_space=pltpu.VMEM)],
+        out_specs=pl.BlockSpec(memory_space=pltpu.VMEM),
+        scratch_shapes=[
+            pltpu.VMEM(x.shape, x.dtype),
+            pltpu.VMEM(x.shape[1:], jnp.float32),
+            pltpu.VMEM((chips, rows, cols), jnp.float32),
+            pltpu.VMEM((rows, cols), jnp.float32),
+            pltpu.VMEM((chips, rows, cols), jnp.float32),
+            pltpu.SemaphoreType.DMA((2, n)),
+            pltpu.SemaphoreType.DMA((2, 2, chips)),
+        ],
+        compiler_params=pltpu.CompilerParams(
+            collective_id=cid, has_side_effects=True, vmem_limit_bytes=48 * 1024 * 1024
+        ),
+    )(x)
+
+
 def per_device(
     gradients,
     feedback,
@@ -210,10 +324,9 @@
     right_terms = right_terms.reshape(matrices, -1, pieces, width).transpose(0, 2, 1, 3)
     right_terms = right_terms.astype(jnp.bfloat16).reshape(cores, owners_count, -1, width)
     right_half = exchange(right_terms, "replica", 1, total=jnp.bfloat16)
-    right_part = exchange(right_half, "mp", 2, total=jnp.float32)
-    part_shape = right_part.shape
-    right_part = allreduce_replica(right_part.reshape(chips, -1, lanes), 3, cores)
-    right_part = right_part.reshape(part_shape).astype(jnp.bfloat16)
+    right_part = reduce_right(right_half, chips, 2)
+    right_part = right_part.reshape(chips // 2, 2, *right_part.shape[1:]).transpose(0, 2, 1, 3)
+    right_part = right_part.reshape(right_half.shape[1:]).astype(jnp.bfloat16)
     right_half = exchange(jnp.broadcast_to(right_part, right_half.shape), "mp", 4)
     right_new = exchange(jnp.broadcast_to(right_half, right_terms.shape), "replica", 5)
     right_new = right_new.reshape(matrices, pieces, -1, width).transpose(0, 2, 1, 3)

time: 130 us -> 129 us (level)
    pallas_call x0 -> x1, Pallas kernels: none -> 34.4 us  [reduce_right(): pl.pallas_call(functools.partial(_reduce_kernel, n, chips), out_shape=jax...]
    pallas_call x2 -> x1, Pallas kernels: 37.9 us -> 21 us  [allreduce_replica(): pl.pallas_call(functools.partial(_allreduce_kernel, n, stride), out_shape...]
    pallas_call x4 -> x3, Pallas kernels: 39.7 us -> 23 us  [exchange(): pl.pallas_call(functools.partial(_exchange_kernel, n, axis, stride, total...]
  transfers between devices with their start and end apart: 2 -> 2, of which waited for: 0 -> 0; matrix products, arithmetic and copies ran while one was open for 15% -> 14% of each run, Pallas kernels for 60% -> 61%
where the time goes in v13:
time: 129 us; the launch traced here: 128 us
  Pallas kernels  78.3 us (61%)
  between operations  16.9 us (13%)
  matrix products  14.9 us (12%)
  other arithmetic  7.41 us (6%)
  local copies, waits for them, and re-layouts  7.34 us (6%)
  starting transfers between devices  3.44 us (3%)
    pallas_call x1, Pallas kernels, reduce_right(): pl.pallas_call(functools.partial(_reduce_kernel, n, chips), out_shape=jax...  34.4 us
    pallas_call x3, Pallas kernels, exchange(): pl.pallas_call(functools.partial(_exchange_kernel, n, axis, stride, total...  23 us
    pallas_call x1, Pallas kernels, allreduce_replica(): pl.pallas_call(functools.partial(_allreduce_kernel, n, stride), out_shape...  21 us
    gather x1, local copies, waits for them, and re-layouts, per_device(): jnp.take(weight_slots, slots, axis=0).astype(jnp.float32)  4.44 us
    dot_general x1, matrix products, per_device(): jnp.einsum('kms,ksn->kmn', left_block, right_new, preferred_element_type=...  4.05 us
    ppermute x1, starting transfers between devices, per_device(): left_block = lax.ppermute(left_rows, ('replica', 'mp'), pairs)  3.4 us
    dot_general x1, matrix products, per_device(): jnp.einsum('kmn,knr->kmr', compensated, right_init, preferred_element_typ...  3.21 us
    dot_general x1, matrix products, per_device(): jnp.einsum('kmn,kms->ksn', compensated, left_rows, preferred_element_type...  3.09 us
  transfers between devices with their start and end apart: 2, of which 0 were waited for; matrix products, arithmetic and copies ran while one was open for 14% of the time, Pallas kernels for 61%

profile of v13, /device:TPU:1, one launch (start us, length us, event | category | flops | bytes accessed | tf_op | source)
XLA Modules:
  0.0 128.3 jit_solution(12451708528815662399)
XLA Ops:
  7.2 0.0 copy-start
  7.2 0.0 all-gather.3.cloned.1.call-start
  7.2 2.1 %subtract_convert_fusion.2 = bf16[1,1,48,3072]{3,2,1,0:T(8,128)(2,1)} fusion(f32[1,1,48,3072]{3,2,1,0:T(8,128)} %param.16, f32[1,1,48,3072]{3,2,1,0:T(8,128)} %param.15), kind=kLoop, calls=%fused_computation.12 | loop fusion | flops 442368 | bytes 1474560 | tf_op jit(solution)/shard_map/convert_element_type | solution.py:300
  9.4 0.0 all-gather.3.cloned.1.call-update
  9.4 3.2 %fusion.17 = f32[8,48,32]{2,1,0:T(8,128)S(1)} fusion(bf16[8,3072,32]{1,2,0:T(8,128)(2,1)S(1)} %copy-done, bf16[1,8,48,3072]{3,2,1,0:T(8,128)(2,1)} %param.11, bf16[1,8,48,3072]{3,2,1,0:T(8,128)(2,1)} %param.10), kind=kOutput, calls=%fused_computation.37 | convolution fusion | flops 80216064 | bytes 6340608 | tf_op jit(solution)/shard_map/kmn,knr->kmr/dot_general | solution.py:301
  12.6 0.1 reshape.148
  12.8 0.6 fusion.8.x_ref
  13.4 21.0 %shard_map.145 = f32[16,8,128]{2,1,0:T(8,128)} custom-call(f32[16,8,128]{2,1,0:T(8,128)} %fusion.8.x_ref), custom_call_target="tpu_custom_call" | custom-call | tf_op jit(solution)/shard_map/pallas_call | solution.py:140
  34.4 0.8 slice.7
  35.2 0.1 reshape.150
  35.3 0.5 convolution_convert_fusion.1
  35.8 3.4 %collective-permute-start = (bf16[8,48,32]{1,2,0:T(8,128)(2,1)S(1)}, bf16[8,48,32]{1,2,0:T(8,128)(2,1)S(1)}, u32[]{:S(2)}, u32[]{:S(2)}) collective-permute-start(bf16[8,48,32]{1,2,0:T(8,128)(2,1)S(1)} %convolution_convert_fusion.1), channel_id=1, source_target_pairs={{0,0},{1,16},{2,32},{3,48},{4,64},{5,80},{6,96},{7,112},{8,128},{9... | collective-permute-start | bytes 73736 | tf_op jit(solution)/shard_map/ppermute | solution.py:339
  39.2 3.1 %convolution_convert_fusion = bf16[8,32,3072]{2,1,0:T(8,128)(2,1)S(1)} fusion(bf16[8,48,32]{1,2,0:T(8,128)(2,1)S(1)} %convolution_convert_fusion.1, bf16[1,8,48,3072]{3,2,1,0:T(8,128)(2,1)} %param.11, bf16[1,8,48,3072]{3,2,1,0:T(8,128)(2,1)} %param.10), kind=kOutput, calls=%fused_computation.5 | convolution fusion | flops 81002496 | bytes 6316032 | tf_op jit(solution)/shard_map/kmn,kms->ksn/dot_general | solution.py:321
  42.3 0.2 copy.41
  42.5 2.7 %shard_map.146.x_ref = bf16[16,32,768]{2,1,0:T(8,128)(2,1)S(1)} custom-call(bf16[2,16,32,768]{3,2,1,0:T(8,128)(2,1)S(1)} %bitcast.55), custom_call_target="tpu_custom_call" | custom-call | tf_op jit(solution)/shard_map/pallas_call | solution.py:70
  45.1 34.4 %shard_map.147 = f32[8,8,384]{2,1,0:T(8,128)S(1)} custom-call(bf16[16,32,768]{2,1,0:T(8,128)(2,1)S(1)} %shard_map.146.x_ref), custom_call_target="tpu_custom_call" | custom-call | tf_op jit(solution)/shard_map/pallas_call | solution.py:250
  79.5 0.1 broadcast_in_dim.37.x_ref
  79.6 13.1 %shard_map.148 = bf16[16,32,768]{2,1,0:T(8,128)(2,1)S(1)} custom-call(bf16[16,32,768]{2,1,0:T(8,128)(2,1)S(1)} %broadcast_in_dim.37.x_ref), custom_call_target="tpu_custom_call" | custom-call | tf_op jit(solution)/shard_map/pallas_call | solution.py:70
  92.7 0.2 broadcast_in_dim.38.x_ref
  92.9 7.2 %shard_map.149 = bf16[2,16,32,768]{3,2,1,0:T(8,128)(2,1)S(1)} custom-call(bf16[2,16,32,768]{3,2,1,0:T(8,128)(2,1)S(1)} %broadcast_in_dim.38.x_ref), custom_call_target="tpu_custom_call" | custom-call | tf_op jit(solution)/shard_map/pallas_call | solution.py:70
  100.2 0.2 copy.39
  100.4 0.4 copy-done.8
  100.8 0.1 convert_reduce_fusion
  100.9 0.7 bitcast_reduce_fusion
  101.6 0.6 compare_and_fusion
  102.2 1.3 multiply_subtract_fusion
  103.5 2.3 %fusion = bf16[1,8,48,3072]{3,2,1,0:T(8,128)(2,1)} fusion(bf16[8,48,32]{1,2,0:T(8,128)(2,1)S(1)} %convolution_convert_fusion.1, bf16[8,32,3072]{2,1,0:T(8,128)(2,1)S(1)} %bitcast.57, bf16[1,8,48,3072]{3,2,1,0:T(8,128)(2,1)S(1)} %copy-done.1, bf16[1,8,48,3072]{3,2,1,0:T(8,128)(2,1)S(1)} %copy-done.2), kind=kOutput, calls=%fused_computation.4 | convolution fusion | flops 83755008 | bytes 8675328 | tf_op jit(solution)/shard_map/kms,ksn->kmn/dot_general | solution.py:340
  108.4 1.7 %convolution_add_fusion = f32[48,3072]{1,0:T(8,128)S(1)} fusion(f32[1,1,48,3072]{3,2,1,0:T(8,128)} %param.15, bf16[8,32,3072]{2,1,0:T(8,128)(2,1)S(1)} %bitcast.58, s32[]{:T(128)} %bitcast.12, f32[]{:T(128)S(6)} %convert_element_type.127, bf16[8,48,32]{1,2,0:T(8,128)(2,1)S(1)} %collective-permute-done), kind=kOutput, calls=%fused_computation.6 | convolution fusion | flops 57117696 | bytes 1386496 | tf_op jit(solution)/shard_map/cmr,crn->cmn/dot_general | solution.py:347
  110.2 0.8 copy-done.3
  111.0 1.9 %fusion.2 = f32[1,1,48,3072]{3,2,1,0:T(8,128)} fusion(f32[1,1,48,3072]{3,2,1,0:T(8,128)} %param.16, f32[48,3072]{1,0:T(8,128)S(1)} %convolution_add_fusion), kind=kLoop, calls=%fused_computation.11 | loop fusion | flops 294912 | bytes 1769472 | tf_op jit(solution)/shard_map/broadcast_in_dim | solution.py:361
  112.9 4.4 %gather_fusion = bf16[8,48,3072]{2,1,0:T(8,128)(2,1)} fusion(bf16[16,48,3072]{2,1,0:T(8,128)(2,1)} %bitcast.62, s32[1024]{0:T(1024)S(1)} %pad_clamp_fusion), kind=kCustom, calls=%fused_computation | custom fusion | bytes 4718624 | tf_op jit(solution)/shard_map/jit(_take)/gather | solution.py:354
  117.4 4.0 %subtract_convert_fusion = bf16[8,48,3072]{2,1,0:T(8,128)(2,1)} fusion(bf16[8,48,32]{1,2,0:T(8,128)(2,1)S(1)} %collective-permute-done, bf16[8,32,3072]{2,1,0:T(8,128)(2,1)S(1)} %bitcast.59, bf16[8,48,3072]{2,1,0:T(8,128)(2,1)} %gather_fusion, pred[8]{0:T(512)(128)(4,1)S(1)} %get-tuple-element.32), kind=kOutput, calls=%fused_computation.1 | convolution fusion | flops 81395712 | bytes 6316040 | tf_op jit(solution)/shard_map/kms,ksn->kmn/dot_general | solution.py:350
  (20 shorter events, 0.1 us)
Async XLA Ops:
  7.2 2.2 %copy-start = (bf16[8,3072,32]{1,2,0:T(8,128)(2,1)S(1)}, bf16[8,3072,32]{1,2,0:T(8,128)(2,1)}, u32[]{:S(2)}) copy-start(bf16[8,3072,32]{1,2,0:T(8,128)(2,1)} %param.12) | copy-start | bytes 4718596
  7.2 105.7 %all-gather.3.cloned.1.call-start = ((), (), s32[]{:S(2)}) async-start(), calls=%async_computation | async-start | bytes 5013504 | tf_op jit(solution)/shard_map/all_gather | solution.py:300
  9.4 3.4 %copy-start.7 = (f32[1,672]{1,0:T(1,128)S(1)}, f32[1,672]{1,0:T(1,128)}, u32[]{:S(2)}) copy-start(f32[1,672]{1,0:T(1,128)} %param.17) | copy-start | bytes 8068
  9.4 25.9 %copy-start.4 = (f32[8,32,32]{2,1,0:T(8,128)S(1)}, f32[8,32,32]{2,1,0:T(8,128)}, u32[]{:S(2)}) copy-start(f32[8,32,32]{2,1,0:T(8,128)} %param.13) | copy-start | bytes 98308
  35.8 72.6 %collective-permute-start = (bf16[8,48,32]{1,2,0:T(8,128)(2,1)S(1)}, bf16[8,48,32]{1,2,0:T(8,128)(2,1)S(1)}, u32[]{:S(2)}, u32[]{:S(2)}) collective-permute-start(bf16[8,48,32]{1,2,0:T(8,128)(2,1)S(1)} %convolution_convert_fusion.1), channel_id=1, source_target_pairs={{0,0},{1,16},{2,32},{3,48},{4,64},{5,80},{6,96},{7,112},{8,128},{9... | collective-permute-start | bytes 73736 | tf_op jit(solution)/shard_map/ppermute | solution.py:339
  92.9 10.6 %copy-start.2 = (bf16[1,8,48,3072]{3,2,1,0:T(8,128)(2,1)S(1)}, bf16[1,8,48,3072]{3,2,1,0:T(8,128)(2,1)}, u32[]{:S(2)}) copy-start(bf16[1,8,48,3072]{3,2,1,0:T(8,128)(2,1)} %param.10) | copy-start | bytes 7077892
  100.1 0.7 copy-start.8
  100.1 2.0 %copy-start.5 = (f32[672]{0:T(1024)S(1)}, f32[672]{0:T(1024)}, u32[]{:S(2)}) copy-start(f32[672]{0:T(1024)} %param.19) | copy-start | bytes 8068
  100.2 2.0 %copy-start.6 = (f32[672]{0:T(1024)S(1)}, f32[672]{0:T(1024)}, u32[]{:S(2)}) copy-start(f32[672]{0:T(1024)} %param.18) | copy-start | bytes 8068
  100.2 3.3 %copy-start.1 = (bf16[1,8,48,3072]{3,2,1,0:T(8,128)(2,1)S(1)}, bf16[1,8,48,3072]{3,2,1,0:T(8,128)(2,1)}, u32[]{:S(2)}) copy-start(bf16[1,8,48,3072]{3,2,1,0:T(8,128)(2,1)} %param.11) | copy-start | bytes 7077892
  110.2 0.8 copy-start.3
Sparse Core Ops, SparseCore 0:
  11.0 71.8 all-gather.2

commit v14 on v13

--- a/solution.py
+++ b/solution.py
@@ -267,6 +267,74 @@
     )(x)
 
 
+def _gather_kernel(n, x_ref, o_ref, half, full, sems):
+    rank = lax.axis_index("replica")
+    me = lax.axis_index("mp")
+    core = lax.rem(rank, 2)
+    partner = rank + 1 - 2 * core
+    barrier = pltpu.get_barrier_semaphore()
+    for d in range(1, n):
+        peer = lax.rem(me + d, n)
+        pl.semaphore_signal(barrier, inc=1, device_id=(rank, peer), device_id_type=MESH_IDS)
+    pl.semaphore_signal(barrier, inc=1, device_id=(partner, me), device_id_type=MESH_IDS)
+    pl.semaphore_wait(barrier, n)
+    copies = []
+    for d in range(1, n):
+        peer = lax.rem(me + d, n)
+        copy = pltpu.make_async_remote_copy(
+            src_ref=x_ref,
+            dst_ref=half.at[me],
+            send_sem=sems.at[0, d],
+            recv_sem=sems.at[1, me],
+            device_id=(rank, peer),
+            device_id_type=MESH_IDS,
+        )
+        copy.start()
+        copies.append(copy)
+    half[me] = x_ref[...]
+    for d in range(1, n):
+        source = lax.rem(me + n - d, n)
+        pltpu.make_async_remote_copy(
+            src_ref=x_ref,
+            dst_ref=half.at[source],
+            send_sem=sems.at[0, d],
+            recv_sem=sems.at[1, source],
+            device_id=(rank, source),
+            device_id_type=MESH_IDS,
+        ).wait_recv()
+    for copy in copies:
+        copy.wait_send()
+    swap = pltpu.make_async_remote_copy(
+        src_ref=half,
+        dst_ref=full.at[core],
+        send_sem=sems.at[2, 0],
+        recv_sem=sems.at[2, 1],
+        device_id=(partner, me),
+        device_id_type=MESH_IDS,
+    )
+    swap.start()
+    full[core] = half[...]
+    swap.wait()
+    o_ref[...] = full[...]
+
+
+def gather_right(x, n, cid):
+    return pl.pallas_call(
+        functools.partial(_gather_kernel, n),
+        out_shape=jax.ShapeDtypeStruct((2, n) + x.shape, x.dtype),
+        in_specs=[pl.BlockSpec(memory_space=pltpu.VMEM)],
+        out_specs=pl.BlockSpec(memory_space=pltpu.VMEM),
+        scratch_shapes=[
+            pltpu.VMEM((n,) + x.shape, x.dtype),
+            pltpu.VMEM((2, n) + x.shape, x.dtype),
+            pltpu.SemaphoreType.DMA((3, n)),
+        ],
+        compiler_params=pltpu.CompilerParams(
+            collective_id=cid, has_side_effects=True, vmem_limit_bytes=48 * 1024 * 1024
+        ),
+    )(x)
+
+
 def per_device(
     gradients,
     feedback,
@@ -327,8 +395,7 @@
     right_part = reduce_right(right_half, chips, 2)
     right_part = right_part.reshape(chips // 2, 2, *right_part.shape[1:]).transpose(0, 2, 1, 3)
     right_part = right_part.reshape(right_half.shape[1:]).astype(jnp.bfloat16)
-    right_half = exchange(jnp.broadcast_to(right_part, right_half.shape), "mp", 4)
-    right_new = exchange(jnp.broadcast_to(right_half, right_terms.shape), "replica", 5)
+    right_new = gather_right(right_part, owners_count, 4)
     right_new = right_new.reshape(matrices, pieces, -1, width).transpose(0, 2, 1, 3)
     right_new = right_new.reshape(matrices, -1, compensated.shape[2])
     pairs = [

time: 129 us -> 128 us (level)
    pallas_call x3 -> x1, Pallas kernels: 23 us -> 2.66 us  [exchange(): pl.pallas_call(functools.partial(_exchange_kernel, n, axis, stride, total...]
    pallas_call x0 -> x1, Pallas kernels: none -> 20.1 us  [gather_right(): pl.pallas_call(functools.partial(_gather_kernel, n), out_shape=jax.ShapeD...]
where the time goes in v14:
time: 128 us; the launch traced here: 127 us
  Pallas kernels  78 us (61%)
  between operations  16.9 us (13%)
  matrix products  14.9 us (12%)
  other arithmetic  7.41 us (6%)
  local copies, waits for them, and re-layouts  6.67 us (5%)
  starting transfers between devices  3.44 us (3%)
    pallas_call x1, Pallas kernels, reduce_right(): pl.pallas_call(functools.partial(_reduce_kernel, n, chips), out_shape=jax...  34.4 us
    pallas_call x1, Pallas kernels, allreduce_replica(): pl.pallas_call(functools.partial(_allreduce_kernel, n, stride), out_shape...  21 us
    pallas_call x1, Pallas kernels, gather_right(): pl.pallas_call(functools.partial(_gather_kernel, n), out_shape=jax.ShapeD...  20.1 us
    gather x1, local copies, waits for them, and re-layouts, per_device(): jnp.take(weight_slots, slots, axis=0).astype(jnp.float32)  4.44 us
    dot_general x1, matrix products, per_device(): jnp.einsum('kms,ksn->kmn', left_block, right_new, preferred_element_type=...  4.04 us
    ppermute x1, starting transfers between devices, per_device(): left_block = lax.ppermute(left_rows, ('replica', 'mp'), pairs)  3.4 us
    dot_general x1, matrix products, per_device(): jnp.einsum('kmn,knr->kmr', compensated, right_init, preferred_element_typ...  3.21 us
    dot_general x1, matrix products, per_device(): jnp.einsum('kmn,kms->ksn', compensated, left_rows, preferred_element_type...  3.09 us
  transfers between devices with their start and end apart: 2, of which 0 were waited for; matrix products, arithmetic and copies ran while one was open for 14% of the time, Pallas kernels for 61%

profile of v14, /device:TPU:1, one launch (start us, length us, event | category | flops | bytes accessed | tf_op | source)
XLA Modules:
  0.0 127.3 jit_solution(15358227712404915617)
XLA Ops:
  7.2 0.0 copy-start
  7.2 0.0 all-gather.3.cloned.1.call-start
  7.2 2.1 %subtract_convert_fusion.2 = bf16[1,1,48,3072]{3,2,1,0:T(8,128)(2,1)} fusion(f32[1,1,48,3072]{3,2,1,0:T(8,128)} %param.16, f32[1,1,48,3072]{3,2,1,0:T(8,128)} %param.15), kind=kLoop, calls=%fused_computation.12 | loop fusion | flops 442368 | bytes 1474560 | tf_op jit(solution)/shard_map/convert_element_type | solution.py:368
  9.4 0.0 all-gather.3.cloned.1.call-update
  9.4 0.0 copy-start.7
  9.4 0.0 copy-start.4
  9.4 3.2 %fusion.17 = f32[8,48,32]{2,1,0:T(8,128)S(1)} fusion(bf16[8,3072,32]{1,2,0:T(8,128)(2,1)S(1)} %copy-done, bf16[1,8,48,3072]{3,2,1,0:T(8,128)(2,1)} %param.11, bf16[1,8,48,3072]{3,2,1,0:T(8,128)(2,1)} %param.10), kind=kOutput, calls=%fused_computation.37 | convolution fusion | flops 80216064 | bytes 6340608 | tf_op jit(solution)/shard_map/kmn,knr->kmr/dot_general | solution.py:369
  12.6 0.1 reshape.148
  12.8 0.6 fusion.8.x_ref
  13.4 21.0 %shard_map.145 = f32[16,8,128]{2,1,0:T(8,128)} custom-call(f32[16,8,128]{2,1,0:T(8,128)} %fusion.8.x_ref), custom_call_target="tpu_custom_call" | custom-call | tf_op jit(solution)/shard_map/pallas_call | solution.py:140
  34.4 0.8 slice.7
  35.2 0.1 reshape.150
  35.3 0.5 convolution_convert_fusion.1
  35.8 3.4 %collective-permute-start = (bf16[8,48,32]{1,2,0:T(8,128)(2,1)S(1)}, bf16[8,48,32]{1,2,0:T(8,128)(2,1)S(1)}, u32[]{:S(2)}, u32[]{:S(2)}) collective-permute-start(bf16[8,48,32]{1,2,0:T(8,128)(2,1)S(1)} %convolution_convert_fusion.1), channel_id=1, source_target_pairs={{0,0},{1,16},{2,32},{3,48},{4,64},{5,80},{6,96},{7,112},{8,128},{9... | collective-permute-start | bytes 73736 | tf_op jit(solution)/shard_map/ppermute | solution.py:406
  39.2 3.1 %convolution_convert_fusion = bf16[8,32,3072]{2,1,0:T(8,128)(2,1)S(1)} fusion(bf16[8,48,32]{1,2,0:T(8,128)(2,1)S(1)} %convolution_convert_fusion.1, bf16[1,8,48,3072]{3,2,1,0:T(8,128)(2,1)} %param.11, bf16[1,8,48,3072]{3,2,1,0:T(8,128)(2,1)} %param.10), kind=kOutput, calls=%fused_computation.5 | convolution fusion | flops 81002496 | bytes 6316032 | tf_op jit(solution)/shard_map/kmn,kms->ksn/dot_general | solution.py:389
  42.3 0.2 copy.41
  42.5 2.7 %shard_map.146.x_ref = bf16[16,32,768]{2,1,0:T(8,128)(2,1)S(1)} custom-call(bf16[2,16,32,768]{3,2,1,0:T(8,128)(2,1)S(1)} %bitcast.55), custom_call_target="tpu_custom_call" | custom-call | tf_op jit(solution)/shard_map/pallas_call | solution.py:70
  45.1 34.4 %shard_map.147 = f32[8,8,384]{2,1,0:T(8,128)S(1)} custom-call(bf16[16,32,768]{2,1,0:T(8,128)(2,1)S(1)} %shard_map.146.x_ref), custom_call_target="tpu_custom_call" | custom-call | tf_op jit(solution)/shard_map/pallas_call | solution.py:250
  79.5 0.0 copy-start.5
  79.5 0.0 copy-start.6
  79.6 20.1 %shard_map.148 = bf16[2,16,32,768]{3,2,1,0:T(8,128)(2,1)S(1)} custom-call(bf16[32,768]{1,0:T(8,128)(2,1)S(1)} %bitcast.57), custom_call_target="tpu_custom_call" | custom-call | tf_op jit(solution)/shard_map/pallas_call | solution.py:322
  99.7 0.2 copy.39
  99.9 0.1 convert_reduce_fusion
  100.0 0.7 bitcast_reduce_fusion
  100.6 0.6 compare_and_fusion
  101.3 1.3 %multiply_subtract_fusion = (f32[672]{0:T(1024)}, f32[672]{0:T(1024)}) fusion(f32[672]{0:T(1024)S(1)} %copy-done.5, f32[16384]{0:T(1024)} %bitcast.64, f32[672]{0:T(1024)S(1)} %copy-done.6), kind=kLoop, calls=%fused_computation.28 | loop fusion | flops 2688 | bytes 13440 | tf_op jit(solution)/shard_map/sub | solution.py:424
  102.6 2.3 %fusion = bf16[1,8,48,3072]{3,2,1,0:T(8,128)(2,1)} fusion(bf16[8,48,32]{1,2,0:T(8,128)(2,1)S(1)} %convolution_convert_fusion.1, bf16[8,32,3072]{2,1,0:T(8,128)(2,1)S(1)} %bitcast.58, bf16[1,8,48,3072]{3,2,1,0:T(8,128)(2,1)S(1)} %copy-done.1, bf16[1,8,48,3072]{3,2,1,0:T(8,128)(2,1)S(1)} %copy-done.2), kind=kOutput, calls=%fused_computation.4 | convolution fusion | flops 83755008 | bytes 8675328 | tf_op jit(solution)/shard_map/kms,ksn->kmn/dot_general | solution.py:407
  107.5 1.7 %convolution_add_fusion = f32[48,3072]{1,0:T(8,128)S(1)} fusion(f32[1,1,48,3072]{3,2,1,0:T(8,128)} %param.15, bf16[8,32,3072]{2,1,0:T(8,128)(2,1)S(1)} %bitcast.59, s32[]{:T(128)} %bitcast.12, f32[]{:T(128)S(6)} %convert_element_type.124, bf16[8,48,32]{1,2,0:T(8,128)(2,1)S(1)} %collective-permute-done), kind=kOutput, calls=%fused_computation.6 | convolution fusion | flops 57117696 | bytes 1386496 | tf_op jit(solution)/shard_map/cmr,crn->cmn/dot_general | solution.py:414
  109.2 0.8 copy-done.3
  110.1 1.9 %fusion.2 = f32[1,1,48,3072]{3,2,1,0:T(8,128)} fusion(f32[1,1,48,3072]{3,2,1,0:T(8,128)} %param.16, f32[48,3072]{1,0:T(8,128)S(1)} %convolution_add_fusion), kind=kLoop, calls=%fused_computation.11 | loop fusion | flops 294912 | bytes 1769472 | tf_op jit(solution)/shard_map/broadcast_in_dim | solution.py:428
  112.0 4.4 %gather_fusion = bf16[8,48,3072]{2,1,0:T(8,128)(2,1)} fusion(bf16[16,48,3072]{2,1,0:T(8,128)(2,1)} %bitcast.63, s32[1024]{0:T(1024)S(1)} %pad_clamp_fusion), kind=kCustom, calls=%fused_computation | custom fusion | bytes 4718624 | tf_op jit(solution)/shard_map/jit(_take)/gather | solution.py:421
  116.4 4.0 %subtract_convert_fusion = bf16[8,48,3072]{2,1,0:T(8,128)(2,1)} fusion(bf16[8,48,32]{1,2,0:T(8,128)(2,1)S(1)} %collective-permute-done, bf16[8,32,3072]{2,1,0:T(8,128)(2,1)S(1)} %bitcast.60, bf16[8,48,3072]{2,1,0:T(8,128)(2,1)} %gather_fusion, pred[8]{0:T(512)(128)(4,1)S(1)} %get-tuple-element.32), kind=kOutput, calls=%fused_computation.1 | convolution fusion | flops 81395712 | bytes 6316040 | tf_op jit(solution)/shard_map/kms,ksn->kmn/dot_general | solution.py:417
  (17 shorter events, 0.1 us)
Async XLA Ops:
  7.2 2.2 %copy-start = (bf16[8,3072,32]{1,2,0:T(8,128)(2,1)S(1)}, bf16[8,3072,32]{1,2,0:T(8,128)(2,1)}, u32[]{:S(2)}) copy-start(bf16[8,3072,32]{1,2,0:T(8,128)(2,1)} %param.12) | copy-start | bytes 4718596
  7.2 104.8 %all-gather.3.cloned.1.call-start = ((), (), s32[]{:S(2)}) async-start(), calls=%async_computation | async-start | bytes 5013504 | tf_op jit(solution)/shard_map/all_gather | solution.py:368
  9.4 3.4 %copy-start.7 = (f32[1,672]{1,0:T(1,128)S(1)}, f32[1,672]{1,0:T(1,128)}, u32[]{:S(2)}) copy-start(f32[1,672]{1,0:T(1,128)} %param.17) | copy-start | bytes 8068
  9.4 25.9 %copy-start.4 = (f32[8,32,32]{2,1,0:T(8,128)S(1)}, f32[8,32,32]{2,1,0:T(8,128)}, u32[]{:S(2)}) copy-start(f32[8,32,32]{2,1,0:T(8,128)} %param.13) | copy-start | bytes 98308
  35.8 71.7 %collective-permute-start = (bf16[8,48,32]{1,2,0:T(8,128)(2,1)S(1)}, bf16[8,48,32]{1,2,0:T(8,128)(2,1)S(1)}, u32[]{:S(2)}, u32[]{:S(2)}) collective-permute-start(bf16[8,48,32]{1,2,0:T(8,128)(2,1)S(1)} %convolution_convert_fusion.1), channel_id=1, source_target_pairs={{0,0},{1,16},{2,32},{3,48},{4,64},{5,80},{6,96},{7,112},{8,128},{9... | collective-permute-start | bytes 73736 | tf_op jit(solution)/shard_map/ppermute | solution.py:406
  79.5 20.3 %copy-start.8 = (s32[8]{0:T(128)S(1)}, s32[8]{0:T(128)}, u32[]{:S(2)}) copy-start(s32[8]{0:T(128)} %param.14) | copy-start | bytes 100
  79.5 21.7 %copy-start.5 = (f32[672]{0:T(1024)S(1)}, f32[672]{0:T(1024)}, u32[]{:S(2)}) copy-start(f32[672]{0:T(1024)} %param.19) | copy-start | bytes 8068
  79.5 21.7 %copy-start.6 = (f32[672]{0:T(1024)S(1)}, f32[672]{0:T(1024)}, u32[]{:S(2)}) copy-start(f32[672]{0:T(1024)} %param.18) | copy-start | bytes 8068
  79.6 23.0 %copy-start.1 = (bf16[1,8,48,3072]{3,2,1,0:T(8,128)(2,1)S(1)}, bf16[1,8,48,3072]{3,2,1,0:T(8,128)(2,1)}, u32[]{:S(2)}) copy-start(bf16[1,8,48,3072]{3,2,1,0:T(8,128)(2,1)} %param.11) | copy-start | bytes 7077892
  79.6 23.0 %copy-start.2 = (bf16[1,8,48,3072]{3,2,1,0:T(8,128)(2,1)S(1)}, bf16[1,8,48,3072]{3,2,1,0:T(8,128)(2,1)}, u32[]{:S(2)}) copy-start(bf16[1,8,48,3072]{3,2,1,0:T(8,128)(2,1)} %param.10) | copy-start | bytes 7077892
  109.2 0.8 copy-start.3
Sparse Core Ops, SparseCore 0:
  11.0 71.8 all-gather.2

commit v15 on v14

--- a/solution.py
+++ b/solution.py
@@ -153,9 +153,13 @@
     )(x)
 
 
-def _reduce_kernel(n, chips, x_ref, o_ref, recv, acc, first, middle, second, mp_sem, z_sem):
+def _reduce_kernel(
+    n, chips, x_ref, o_ref, pair, mine, recv, acc, first, middle, second, mp_sem, z_sem
+):
     rank = lax.axis_index("replica")
     me = lax.axis_index("mp")
+    core = lax.rem(rank, 2)
+    partner = rank + 1 - 2 * core
     spot = lax.rem(lax.div(rank, 2), chips)
     base = rank - spot * 2
     rows, cols = first.shape[1], first.shape[2]
@@ -175,12 +179,26 @@
     for d in range(1, chips):
         peer = lax.rem(spot + d, chips)
         pl.semaphore_signal(barrier, inc=1, device_id=chip(peer), device_id_type=MESH_IDS)
-    pl.semaphore_wait(barrier, n - 1 + chips - 1)
+    pl.semaphore_signal(barrier, inc=1, device_id=(partner, me), device_id_type=MESH_IDS)
+    pl.semaphore_wait(barrier, n - 1 + chips - 1 + 1)
+    swap = pltpu.make_async_remote_copy(
+        src_ref=x_ref.at[1 - core],
+        dst_ref=pair,
+        send_sem=z_sem.at[2, 0, 0],
+        recv_sem=z_sem.at[2, 1, 0],
+        device_id=(partner, me),
+        device_id_type=MESH_IDS,
+    )
+    swap.start()
+    swap.wait()
+    mine[...] = (x_ref[core].astype(jnp.float32) + pair[...].astype(jnp.float32)).astype(
+        mine.dtype
+    )
     copies = []
     for d in range(1, n):
         peer = lax.rem(me + d, n)
         copy = pltpu.make_async_remote_copy(
-            src_ref=x_ref.at[peer],
+            src_ref=mine.at[peer],
             dst_ref=recv.at[me],
             send_sem=mp_sem.at[0, d],
             recv_sem=mp_sem.at[1, me],
@@ -189,11 +207,11 @@
         )
         copy.start()
         copies.append(copy)
-    recv[me] = x_ref[me]
+    recv[me] = mine[me]
     for d in range(1, n):
         source = lax.rem(me + n - d, n)
         pltpu.make_async_remote_copy(
-            src_ref=x_ref.at[source],
+            src_ref=mine.at[source],
             dst_ref=recv.at[source],
             send_sem=mp_sem.at[0, d],
             recv_sem=mp_sem.at[1, source],
@@ -245,21 +263,23 @@
 
 
 def reduce_right(x, chips, cid):
-    n = x.shape[0]
-    rows, cols = x.shape[1] // (chips // 2), x.shape[2] // 2
+    n = x.shape[1]
+    rows, cols = x.shape[2] // (chips // 2), x.shape[3] // 2
     return pl.pallas_call(
         functools.partial(_reduce_kernel, n, chips),
         out_shape=jax.ShapeDtypeStruct((chips, rows, cols), jnp.float32),
         in_specs=[pl.BlockSpec(memory_space=pltpu.VMEM)],
         out_specs=pl.BlockSpec(memory_space=pltpu.VMEM),
         scratch_shapes=[
-            pltpu.VMEM(x.shape, x.dtype),
-            pltpu.VMEM(x.shape[1:], jnp.float32),
+            pltpu.VMEM(x.shape[1:], x.dtype),
+            pltpu.VMEM(x.shape[1:], x.dtype),
+            pltpu.VMEM(x.shape[1:], x.dtype),
+            pltpu.VMEM(x.shape[2:], jnp.float32),
             pltpu.VMEM((chips, rows, cols), jnp.float32),
             pltpu.VMEM((rows, cols), jnp.float32),
             pltpu.VMEM((chips, rows, cols), jnp.float32),
             pltpu.SemaphoreType.DMA((2, n)),
-            pltpu.SemaphoreType.DMA((2, 2, chips)),
+            pltpu.SemaphoreType.DMA((3, 2, chips)),
         ],
         compiler_params=pltpu.CompilerParams(
             collective_id=cid, has_side_effects=True, vmem_limit_bytes=48 * 1024 * 1024
@@ -391,10 +411,9 @@
     )
     right_terms = right_terms.reshape(matrices, -1, pieces, width).transpose(0, 2, 1, 3)
     right_terms = right_terms.astype(jnp.bfloat16).reshape(cores, owners_count, -1, width)
-    right_half = exchange(right_terms, "replica", 1, total=jnp.bfloat16)
-    right_part = reduce_right(right_half, chips, 2)
+    right_part = reduce_right(right_terms, chips, 2)
     right_part = right_part.reshape(chips // 2, 2, *right_part.shape[1:]).transpose(0, 2, 1, 3)
-    right_part = right_part.reshape(right_half.shape[1:]).astype(jnp.bfloat16)
+    right_part = right_part.reshape(right_terms.shape[2:]).astype(jnp.bfloat16)
     right_new = gather_right(right_part, owners_count, 4)
     right_new = right_new.reshape(matrices, pieces, -1, width).transpose(0, 2, 1, 3)
     right_new = right_new.reshape(matrices, -1, compensated.shape[2])

time: 128 us -> 127 us (level)
    pallas_call x1, Pallas kernels: 34.4 us -> 37 us  [reduce_right(): pl.pallas_call(functools.partial(_reduce_kernel, n, chips), out_shape=jax...]
    pallas_call x1 -> x0, Pallas kernels: 2.66 us -> none  [exchange(): pl.pallas_call(functools.partial(_exchange_kernel, n, axis, stride, total...]
where the time goes in v15:
time: 127 us
  Pallas kernels  77.7 us (61%)
  between operations  16.8 us (13%)
  matrix products  14.9 us (12%)
  other arithmetic  7.41 us (6%)
  local copies, waits for them, and re-layouts  6.67 us (5%)
  starting transfers between devices  3.44 us (3%)
    pallas_call x1, Pallas kernels, reduce_right(): pl.pallas_call(functools.partial(_reduce_kernel, n, chips), out_shape=jax...  37 us
    pallas_call x1, Pallas kernels, allreduce_replica(): pl.pallas_call(functools.partial(_allreduce_kernel, n, stride), out_shape...  21 us
    pallas_call x1, Pallas kernels, gather_right(): pl.pallas_call(functools.partial(_gather_kernel, n), out_shape=jax.ShapeD...  19.7 us
    gather x1, local copies, waits for them, and re-layouts, per_device(): jnp.take(weight_slots, slots, axis=0).astype(jnp.float32)  4.44 us
    dot_general x1, matrix products, per_device(): jnp.einsum('kms,ksn->kmn', left_block, right_new, preferred_element_type=...  4.05 us
    ppermute x1, starting transfers between devices, per_device(): left_block = lax.ppermute(left_rows, ('replica', 'mp'), pairs)  3.4 us
    dot_general x1, matrix products, per_device(): jnp.einsum('kmn,knr->kmr', compensated, right_init, preferred_element_typ...  3.21 us
    dot_general x1, matrix products, per_device(): jnp.einsum('kmn,kms->ksn', compensated, left_rows, preferred_element_type...  3.09 us
  transfers between devices with their start and end apart: 2, of which 0 were waited for; matrix products, arithmetic and copies ran while one was open for 14% of the time, Pallas kernels for 61%

profile of v15, /device:TPU:1, one launch (start us, length us, event | category | flops | bytes accessed | tf_op | source)
XLA Modules:
  0.0 127.0 jit_solution(414013695071496386)
XLA Ops:
  7.2 0.0 copy-start
  7.2 0.0 all-gather.3.cloned.1.call-start
  7.2 2.1 %subtract_convert_fusion.2 = bf16[1,1,48,3072]{3,2,1,0:T(8,128)(2,1)} fusion(f32[1,1,48,3072]{3,2,1,0:T(8,128)} %param.16, f32[1,1,48,3072]{3,2,1,0:T(8,128)} %param.15), kind=kLoop, calls=%fused_computation.12 | loop fusion | flops 442368 | bytes 1474560 | tf_op jit(solution)/shard_map/convert_element_type | solution.py:388
  9.4 0.0 all-gather.3.cloned.1.call-update
  9.4 0.0 copy-start.7
  9.4 0.0 copy-start.4
  9.4 3.2 %fusion.17 = f32[8,48,32]{2,1,0:T(8,128)S(1)} fusion(bf16[8,3072,32]{1,2,0:T(8,128)(2,1)S(1)} %copy-done, bf16[1,8,48,3072]{3,2,1,0:T(8,128)(2,1)} %param.11, bf16[1,8,48,3072]{3,2,1,0:T(8,128)(2,1)} %param.10), kind=kOutput, calls=%fused_computation.37 | convolution fusion | flops 80216064 | bytes 6340608 | tf_op jit(solution)/shard_map/kmn,knr->kmr/dot_general | solution.py:389
  12.6 0.1 reshape.148
  12.8 0.6 fusion.8.x_ref
  13.4 21.0 %shard_map.145 = f32[16,8,128]{2,1,0:T(8,128)} custom-call(f32[16,8,128]{2,1,0:T(8,128)} %fusion.8.x_ref), custom_call_target="tpu_custom_call" | custom-call | tf_op jit(solution)/shard_map/pallas_call | solution.py:140
  34.4 0.8 slice.7
  35.2 0.1 reshape.150
  35.3 0.5 convolution_convert_fusion.1
  35.8 3.4 %collective-permute-start = (bf16[8,48,32]{1,2,0:T(8,128)(2,1)S(1)}, bf16[8,48,32]{1,2,0:T(8,128)(2,1)S(1)}, u32[]{:S(2)}, u32[]{:S(2)}) collective-permute-start(bf16[8,48,32]{1,2,0:T(8,128)(2,1)S(1)} %convolution_convert_fusion.1), channel_id=1, source_target_pairs={{0,0},{1,16},{2,32},{3,48},{4,64},{5,80},{6,96},{7,112},{8,128},{9... | collective-permute-start | bytes 73736 | tf_op jit(solution)/shard_map/ppermute | solution.py:425
  39.2 3.1 %convolution_convert_fusion = bf16[8,32,3072]{2,1,0:T(8,128)(2,1)S(1)} fusion(bf16[8,48,32]{1,2,0:T(8,128)(2,1)S(1)} %convolution_convert_fusion.1, bf16[1,8,48,3072]{3,2,1,0:T(8,128)(2,1)} %param.11, bf16[1,8,48,3072]{3,2,1,0:T(8,128)(2,1)} %param.10), kind=kOutput, calls=%fused_computation.5 | convolution fusion | flops 81002496 | bytes 6316032 | tf_op jit(solution)/shard_map/kmn,kms->ksn/dot_general | solution.py:409
  42.3 0.2 copy.41
  42.5 37.0 %shard_map.146 = f32[8,8,384]{2,1,0:T(8,128)S(1)} custom-call(bf16[2,16,32,768]{3,2,1,0:T(8,128)(2,1)S(1)} %bitcast.55), custom_call_target="tpu_custom_call" | custom-call | tf_op jit(solution)/shard_map/pallas_call | solution.py:268
  79.5 0.0 copy-start.8
  79.5 0.0 copy-start.5
  79.6 0.0 copy-start.2
  79.6 19.7 %shard_map.147 = bf16[2,16,32,768]{3,2,1,0:T(8,128)(2,1)S(1)} custom-call(bf16[32,768]{1,0:T(8,128)(2,1)S(1)} %bitcast.57), custom_call_target="tpu_custom_call" | custom-call | tf_op jit(solution)/shard_map/pallas_call | solution.py:342
  99.3 0.2 copy.39
  99.5 0.1 convert_reduce_fusion
  99.6 0.7 bitcast_reduce_fusion
  100.3 0.6 compare_and_fusion
  100.9 1.3 %multiply_subtract_fusion = (f32[672]{0:T(1024)}, f32[672]{0:T(1024)}) fusion(f32[672]{0:T(1024)S(1)} %copy-done.5, f32[16384]{0:T(1024)} %bitcast.64, f32[672]{0:T(1024)S(1)} %copy-done.6), kind=kLoop, calls=%fused_computation.28 | loop fusion | flops 2688 | bytes 13440 | tf_op jit(solution)/shard_map/sub | solution.py:443
  102.2 2.3 %fusion = bf16[1,8,48,3072]{3,2,1,0:T(8,128)(2,1)} fusion(bf16[8,48,32]{1,2,0:T(8,128)(2,1)S(1)} %convolution_convert_fusion.1, bf16[8,32,3072]{2,1,0:T(8,128)(2,1)S(1)} %bitcast.58, bf16[1,8,48,3072]{3,2,1,0:T(8,128)(2,1)S(1)} %copy-done.1, bf16[1,8,48,3072]{3,2,1,0:T(8,128)(2,1)S(1)} %copy-done.2), kind=kOutput, calls=%fused_computation.4 | convolution fusion | flops 83755008 | bytes 8675328 | tf_op jit(solution)/shard_map/kms,ksn->kmn/dot_general | solution.py:426
  107.1 1.7 %convolution_add_fusion = f32[48,3072]{1,0:T(8,128)S(1)} fusion(f32[1,1,48,3072]{3,2,1,0:T(8,128)} %param.15, bf16[8,32,3072]{2,1,0:T(8,128)(2,1)S(1)} %bitcast.59, s32[]{:T(128)} %bitcast.12, f32[]{:T(128)S(6)} %convert_element_type.124, bf16[8,48,32]{1,2,0:T(8,128)(2,1)S(1)} %collective-permute-done), kind=kOutput, calls=%fused_computation.6 | convolution fusion | flops 57117696 | bytes 1386496 | tf_op jit(solution)/shard_map/cmr,crn->cmn/dot_general | solution.py:433
  108.9 0.8 copy-done.3
  109.7 1.9 %fusion.2 = f32[1,1,48,3072]{3,2,1,0:T(8,128)} fusion(f32[1,1,48,3072]{3,2,1,0:T(8,128)} %param.16, f32[48,3072]{1,0:T(8,128)S(1)} %convolution_add_fusion), kind=kLoop, calls=%fused_computation.11 | loop fusion | flops 294912 | bytes 1769472 | tf_op jit(solution)/shard_map/broadcast_in_dim | solution.py:447
  111.6 4.4 %gather_fusion = bf16[8,48,3072]{2,1,0:T(8,128)(2,1)} fusion(bf16[16,48,3072]{2,1,0:T(8,128)(2,1)} %bitcast.63, s32[1024]{0:T(1024)S(1)} %pad_clamp_fusion), kind=kCustom, calls=%fused_computation | custom fusion | bytes 4718624 | tf_op jit(solution)/shard_map/jit(_take)/gather | solution.py:440
  116.1 4.0 %subtract_convert_fusion = bf16[8,48,3072]{2,1,0:T(8,128)(2,1)} fusion(bf16[8,48,32]{1,2,0:T(8,128)(2,1)S(1)} %collective-permute-done, bf16[8,32,3072]{2,1,0:T(8,128)(2,1)S(1)} %bitcast.60, bf16[8,48,3072]{2,1,0:T(8,128)(2,1)} %gather_fusion, pred[8]{0:T(512)(128)(4,1)S(1)} %get-tuple-element.32), kind=kOutput, calls=%fused_computation.1 | convolution fusion | flops 81395712 | bytes 6316040 | tf_op jit(solution)/shard_map/kms,ksn->kmn/dot_general | solution.py:436
  (16 shorter events, 0.1 us)
Async XLA Ops:
  7.2 2.2 %copy-start = (bf16[8,3072,32]{1,2,0:T(8,128)(2,1)S(1)}, bf16[8,3072,32]{1,2,0:T(8,128)(2,1)}, u32[]{:S(2)}) copy-start(bf16[8,3072,32]{1,2,0:T(8,128)(2,1)} %param.12) | copy-start | bytes 4718596
  7.2 104.5 %all-gather.3.cloned.1.call-start = ((), (), s32[]{:S(2)}) async-start(), calls=%async_computation | async-start | bytes 5013504 | tf_op jit(solution)/shard_map/all_gather | solution.py:388
  9.4 3.4 %copy-start.7 = (f32[1,672]{1,0:T(1,128)S(1)}, f32[1,672]{1,0:T(1,128)}, u32[]{:S(2)}) copy-start(f32[1,672]{1,0:T(1,128)} %param.17) | copy-start | bytes 8068
  9.4 25.9 %copy-start.4 = (f32[8,32,32]{2,1,0:T(8,128)S(1)}, f32[8,32,32]{2,1,0:T(8,128)}, u32[]{:S(2)}) copy-start(f32[8,32,32]{2,1,0:T(8,128)} %param.13) | copy-start | bytes 98308
  35.8 71.3 %collective-permute-start = (bf16[8,48,32]{1,2,0:T(8,128)(2,1)S(1)}, bf16[8,48,32]{1,2,0:T(8,128)(2,1)S(1)}, u32[]{:S(2)}, u32[]{:S(2)}) collective-permute-start(bf16[8,48,32]{1,2,0:T(8,128)(2,1)S(1)} %convolution_convert_fusion.1), channel_id=1, source_target_pairs={{0,0},{1,16},{2,32},{3,48},{4,64},{5,80},{6,96},{7,112},{8,128},{9... | collective-permute-start | bytes 73736 | tf_op jit(solution)/shard_map/ppermute | solution.py:425
  79.5 20.0 %copy-start.8 = (s32[8]{0:T(128)S(1)}, s32[8]{0:T(128)}, u32[]{:S(2)}) copy-start(s32[8]{0:T(128)} %param.14) | copy-start | bytes 100
  79.5 21.4 %copy-start.5 = (f32[672]{0:T(1024)S(1)}, f32[672]{0:T(1024)}, u32[]{:S(2)}) copy-start(f32[672]{0:T(1024)} %param.19) | copy-start | bytes 8068
  79.5 21.4 %copy-start.6 = (f32[672]{0:T(1024)S(1)}, f32[672]{0:T(1024)}, u32[]{:S(2)}) copy-start(f32[672]{0:T(1024)} %param.18) | copy-start | bytes 8068
  79.6 22.6 %copy-start.1 = (bf16[1,8,48,3072]{3,2,1,0:T(8,128)(2,1)S(1)}, bf16[1,8,48,3072]{3,2,1,0:T(8,128)(2,1)}, u32[]{:S(2)}) copy-start(bf16[1,8,48,3072]{3,2,1,0:T(8,128)(2,1)} %param.11) | copy-start | bytes 7077892
  79.6 22.6 %copy-start.2 = (bf16[1,8,48,3072]{3,2,1,0:T(8,128)(2,1)S(1)}, bf16[1,8,48,3072]{3,2,1,0:T(8,128)(2,1)}, u32[]{:S(2)}) copy-start(bf16[1,8,48,3072]{3,2,1,0:T(8,128)(2,1)} %param.10) | copy-start | bytes 7077892
  108.9 0.8 copy-start.3
Sparse Core Ops, SparseCore 0:
  11.0 71.3 all-gather.2

commit v16 on v15

--- a/solution.py
+++ b/solution.py
@@ -259,7 +259,9 @@
         part = part + first[s]
     middle[...] = part
     round_trip(1, lambda peer: middle, second)
-    o_ref[...] = second[...]
+    for p in range(chips):
+        r, c = (p // 2) * rows, (p % 2) * cols
+        o_ref[r : r + rows, c : c + cols] = second[p]
 
 
 def reduce_right(x, chips, cid):
@@ -267,7 +269,7 @@
     rows, cols = x.shape[2] // (chips // 2), x.shape[3] // 2
     return pl.pallas_call(
         functools.partial(_reduce_kernel, n, chips),
-        out_shape=jax.ShapeDtypeStruct((chips, rows, cols), jnp.float32),
+        out_shape=jax.ShapeDtypeStruct(x.shape[2:], jnp.float32),
         in_specs=[pl.BlockSpec(memory_space=pltpu.VMEM)],
         out_specs=pl.BlockSpec(memory_space=pltpu.VMEM),
         scratch_shapes=[
@@ -411,9 +413,7 @@
     )
     right_terms = right_terms.reshape(matrices, -1, pieces, width).transpose(0, 2, 1, 3)
     right_terms = right_terms.astype(jnp.bfloat16).reshape(cores, owners_count, -1, width)
-    right_part = reduce_right(right_terms, chips, 2)
-    right_part = right_part.reshape(chips // 2, 2, *right_part.shape[1:]).transpose(0, 2, 1, 3)
-    right_part = right_part.reshape(right_terms.shape[2:]).astype(jnp.bfloat16)
+    right_part = reduce_right(right_terms, chips, 2).astype(jnp.bfloat16)
     right_new = gather_right(right_part, owners_count, 4)
     right_new = right_new.reshape(matrices, pieces, -1, width).transpose(0, 2, 1, 3)
     right_new = right_new.reshape(matrices, -1, compensated.shape[2])

time: 127 us -> 127 us (level)
  no operation moved by 1% of the time
where the time goes in v16:
time: 127 us
  Pallas kernels  77.7 us (61%)
  between operations  16.8 us (13%)
  matrix products  14.9 us (12%)
  other arithmetic  7.41 us (6%)
  local copies, waits for them, and re-layouts  6.67 us (5%)
  starting transfers between devices  3.44 us (3%)
    pallas_call x1, Pallas kernels, reduce_right(): pl.pallas_call(functools.partial(_reduce_kernel, n, chips), out_shape=jax...  37 us
    pallas_call x1, Pallas kernels, allreduce_replica(): pl.pallas_call(functools.partial(_allreduce_kernel, n, stride), out_shape...  21 us
    pallas_call x1, Pallas kernels, gather_right(): pl.pallas_call(functools.partial(_gather_kernel, n), out_shape=jax.ShapeD...  19.7 us
    gather x1, local copies, waits for them, and re-layouts, per_device(): jnp.take(weight_slots, slots, axis=0).astype(jnp.float32)  4.44 us
    dot_general x1, matrix products, per_device(): jnp.einsum('kms,ksn->kmn', left_block, right_new, preferred_element_type=...  4.04 us
    ppermute x1, starting transfers between devices, per_device(): left_block = lax.ppermute(left_rows, ('replica', 'mp'), pairs)  3.4 us
    dot_general x1, matrix products, per_device(): jnp.einsum('kmn,knr->kmr', compensated, right_init, preferred_element_typ...  3.21 us
    dot_general x1, matrix products, per_device(): jnp.einsum('kmn,kms->ksn', compensated, left_rows, preferred_element_type...  3.09 us
  transfers between devices with their start and end apart: 2, of which 0 were waited for; matrix products, arithmetic and copies ran while one was open for 14% of the time, Pallas kernels for 61%

profile of v16, /device:TPU:1, one launch (start us, length us, event | category | flops | bytes accessed | tf_op | source)
XLA Modules:
  0.0 127.0 jit_solution(117764831714265622)
XLA Ops:
  7.2 0.0 copy-start
  7.2 0.0 all-gather.3.cloned.1.call-start
  7.2 2.1 %subtract_convert_fusion.2 = bf16[1,1,48,3072]{3,2,1,0:T(8,128)(2,1)} fusion(f32[1,1,48,3072]{3,2,1,0:T(8,128)} %param.16, f32[1,1,48,3072]{3,2,1,0:T(8,128)} %param.15), kind=kLoop, calls=%fused_computation.12 | loop fusion | flops 442368 | bytes 1474560 | tf_op jit(solution)/shard_map/convert_element_type | solution.py:390
  9.4 0.0 all-gather.3.cloned.1.call-update
  9.4 0.0 copy-start.7
  9.4 0.0 copy-start.4
  9.4 3.2 %fusion.17 = f32[8,48,32]{2,1,0:T(8,128)S(1)} fusion(bf16[8,3072,32]{1,2,0:T(8,128)(2,1)S(1)} %copy-done, bf16[1,8,48,3072]{3,2,1,0:T(8,128)(2,1)} %param.11, bf16[1,8,48,3072]{3,2,1,0:T(8,128)(2,1)} %param.10), kind=kOutput, calls=%fused_computation.37 | convolution fusion | flops 80216064 | bytes 6340608 | tf_op jit(solution)/shard_map/kmn,knr->kmr/dot_general | solution.py:391
  12.6 0.1 reshape.144
  12.8 0.6 fusion.8.x_ref
  13.4 21.0 %shard_map.145 = f32[16,8,128]{2,1,0:T(8,128)} custom-call(f32[16,8,128]{2,1,0:T(8,128)} %fusion.8.x_ref), custom_call_target="tpu_custom_call" | custom-call | tf_op jit(solution)/shard_map/pallas_call | solution.py:140
  34.4 0.8 slice.7
  35.2 0.1 reshape.146
  35.3 0.5 convolution_convert_fusion.1
  35.8 3.4 %collective-permute-start = (bf16[8,48,32]{1,2,0:T(8,128)(2,1)S(1)}, bf16[8,48,32]{1,2,0:T(8,128)(2,1)S(1)}, u32[]{:S(2)}, u32[]{:S(2)}) collective-permute-start(bf16[8,48,32]{1,2,0:T(8,128)(2,1)S(1)} %convolution_convert_fusion.1), channel_id=1, source_target_pairs={{0,0},{1,16},{2,32},{3,48},{4,64},{5,80},{6,96},{7,112},{8,128},{9... | collective-permute-start | bytes 73736 | tf_op jit(solution)/shard_map/ppermute | solution.py:425
  39.2 3.1 %convolution_convert_fusion = bf16[8,32,3072]{2,1,0:T(8,128)(2,1)S(1)} fusion(bf16[8,48,32]{1,2,0:T(8,128)(2,1)S(1)} %convolution_convert_fusion.1, bf16[1,8,48,3072]{3,2,1,0:T(8,128)(2,1)} %param.11, bf16[1,8,48,3072]{3,2,1,0:T(8,128)(2,1)} %param.10), kind=kOutput, calls=%fused_computation.5 | convolution fusion | flops 81002496 | bytes 6316032 | tf_op jit(solution)/shard_map/kmn,kms->ksn/dot_general | solution.py:411
  42.3 0.2 copy.41
  42.5 37.0 %shard_map.146 = f32[32,768]{1,0:T(8,128)S(1)} custom-call(bf16[2,16,32,768]{3,2,1,0:T(8,128)(2,1)S(1)} %bitcast.50), custom_call_target="tpu_custom_call" | custom-call | tf_op jit(solution)/shard_map/pallas_call | solution.py:270
  79.5 0.0 copy-start.8
  79.5 0.0 copy-start.6
  79.6 0.0 copy-start.1
  79.6 19.7 %shard_map.147 = bf16[2,16,32,768]{3,2,1,0:T(8,128)(2,1)S(1)} custom-call(bf16[32,768]{1,0:T(8,128)(2,1)S(1)} %convert_element_type.111.x_ref), custom_call_target="tpu_custom_call" | custom-call | tf_op jit(solution)/shard_map/pallas_call | solution.py:344
  99.3 0.2 copy.39
  99.5 0.1 convert_reduce_fusion
  99.6 0.7 bitcast_reduce_fusion
  100.3 0.6 compare_and_fusion
  100.9 1.3 %multiply_subtract_fusion = (f32[672]{0:T(1024)}, f32[672]{0:T(1024)}) fusion(f32[672]{0:T(1024)S(1)} %copy-done.5, f32[16384]{0:T(1024)} %bitcast.58, f32[672]{0:T(1024)S(1)} %copy-done.6), kind=kLoop, calls=%fused_computation.28 | loop fusion | flops 2688 | bytes 13440 | tf_op jit(solution)/shard_map/sub | solution.py:443
  102.2 2.3 %fusion = bf16[1,8,48,3072]{3,2,1,0:T(8,128)(2,1)} fusion(bf16[8,48,32]{1,2,0:T(8,128)(2,1)S(1)} %convolution_convert_fusion.1, bf16[8,32,3072]{2,1,0:T(8,128)(2,1)S(1)} %bitcast.52, bf16[1,8,48,3072]{3,2,1,0:T(8,128)(2,1)S(1)} %copy-done.1, bf16[1,8,48,3072]{3,2,1,0:T(8,128)(2,1)S(1)} %copy-done.2), kind=kOutput, calls=%fused_computation.4 | convolution fusion | flops 83755008 | bytes 8675328 | tf_op jit(solution)/shard_map/kms,ksn->kmn/dot_general | solution.py:426
  107.1 1.7 %convolution_add_fusion = f32[48,3072]{1,0:T(8,128)S(1)} fusion(f32[1,1,48,3072]{3,2,1,0:T(8,128)} %param.15, bf16[8,32,3072]{2,1,0:T(8,128)(2,1)S(1)} %bitcast.53, s32[]{:T(128)} %bitcast.9, f32[]{:T(128)S(6)} %convert_element_type.115, bf16[8,48,32]{1,2,0:T(8,128)(2,1)S(1)} %collective-permute-done), kind=kOutput, calls=%fused_computation.6 | convolution fusion | flops 57117696 | bytes 1386496 | tf_op jit(solution)/shard_map/cmr,crn->cmn/dot_general | solution.py:433
  108.9 0.8 copy-done.3
  109.7 1.9 %fusion.2 = f32[1,1,48,3072]{3,2,1,0:T(8,128)} fusion(f32[1,1,48,3072]{3,2,1,0:T(8,128)} %param.16, f32[48,3072]{1,0:T(8,128)S(1)} %convolution_add_fusion), kind=kLoop, calls=%fused_computation.11 | loop fusion | flops 294912 | bytes 1769472 | tf_op jit(solution)/shard_map/broadcast_in_dim | solution.py:447
  111.6 4.4 %gather_fusion = bf16[8,48,3072]{2,1,0:T(8,128)(2,1)} fusion(bf16[16,48,3072]{2,1,0:T(8,128)(2,1)} %bitcast.57, s32[1024]{0:T(1024)S(1)} %pad_clamp_fusion), kind=kCustom, calls=%fused_computation | custom fusion | bytes 4718624 | tf_op jit(solution)/shard_map/jit(_take)/gather | solution.py:440
  116.1 4.0 %subtract_convert_fusion = bf16[8,48,3072]{2,1,0:T(8,128)(2,1)} fusion(bf16[8,48,32]{1,2,0:T(8,128)(2,1)S(1)} %collective-permute-done, bf16[8,32,3072]{2,1,0:T(8,128)(2,1)S(1)} %bitcast.54, bf16[8,48,3072]{2,1,0:T(8,128)(2,1)} %gather_fusion, pred[8]{0:T(512)(128)(4,1)S(1)} %get-tuple-element.32), kind=kOutput, calls=%fused_computation.1 | convolution fusion | flops 81395712 | bytes 6316040 | tf_op jit(solution)/shard_map/kms,ksn->kmn/dot_general | solution.py:436
  (16 shorter events, 0.1 us)
Async XLA Ops:
  7.2 2.2 %copy-start = (bf16[8,3072,32]{1,2,0:T(8,128)(2,1)S(1)}, bf16[8,3072,32]{1,2,0:T(8,128)(2,1)}, u32[]{:S(2)}) copy-start(bf16[8,3072,32]{1,2,0:T(8,128)(2,1)} %param.12) | copy-start | bytes 4718596
  7.2 104.5 %all-gather.3.cloned.1.call-start = ((), (), s32[]{:S(2)}) async-start(), calls=%async_computation | async-start | bytes 5013504 | tf_op jit(solution)/shard_map/all_gather | solution.py:390
  9.4 3.4 %copy-start.7 = (f32[1,672]{1,0:T(1,128)S(1)}, f32[1,672]{1,0:T(1,128)}, u32[]{:S(2)}) copy-start(f32[1,672]{1,0:T(1,128)} %param.17) | copy-start | bytes 8068
  9.4 25.9 %copy-start.4 = (f32[8,32,32]{2,1,0:T(8,128)S(1)}, f32[8,32,32]{2,1,0:T(8,128)}, u32[]{:S(2)}) copy-start(f32[8,32,32]{2,1,0:T(8,128)} %param.13) | copy-start | bytes 98308
  35.8 71.3 %collective-permute-start = (bf16[8,48,32]{1,2,0:T(8,128)(2,1)S(1)}, bf16[8,48,32]{1,2,0:T(8,128)(2,1)S(1)}, u32[]{:S(2)}, u32[]{:S(2)}) collective-permute-start(bf16[8,48,32]{1,2,0:T(8,128)(2,1)S(1)} %convolution_convert_fusion.1), channel_id=1, source_target_pairs={{0,0},{1,16},{2,32},{3,48},{4,64},{5,80},{6,96},{7,112},{8,128},{9... | collective-permute-start | bytes 73736 | tf_op jit(solution)/shard_map/ppermute | solution.py:425
  79.5 20.0 %copy-start.8 = (s32[8]{0:T(128)S(1)}, s32[8]{0:T(128)}, u32[]{:S(2)}) copy-start(s32[8]{0:T(128)} %param.14) | copy-start | bytes 100
  79.5 21.4 %copy-start.5 = (f32[672]{0:T(1024)S(1)}, f32[672]{0:T(1024)}, u32[]{:S(2)}) copy-start(f32[672]{0:T(1024)} %param.19) | copy-start | bytes 8068
  79.5 21.4 %copy-start.6 = (f32[672]{0:T(1024)S(1)}, f32[672]{0:T(1024)}, u32[]{:S(2)}) copy-start(f32[672]{0:T(1024)} %param.18) | copy-start | bytes 8068
  79.6 22.6 %copy-start.1 = (bf16[1,8,48,3072]{3,2,1,0:T(8,128)(2,1)S(1)}, bf16[1,8,48,3072]{3,2,1,0:T(8,128)(2,1)}, u32[]{:S(2)}) copy-start(bf16[1,8,48,3072]{3,2,1,0:T(8,128)(2,1)} %param.11) | copy-start | bytes 7077892
  79.6 22.6 %copy-start.2 = (bf16[1,8,48,3072]{3,2,1,0:T(8,128)(2,1)S(1)}, bf16[1,8,48,3072]{3,2,1,0:T(8,128)(2,1)}, u32[]{:S(2)}) copy-start(bf16[1,8,48,3072]{3,2,1,0:T(8,128)(2,1)} %param.10) | copy-start | bytes 7077892
  108.9 0.8 copy-start.3
Sparse Core Ops, SparseCore 0:
  11.0 71.3 all-gather.2

commit v17 on v16

--- a/solution.py
+++ b/solution.py
@@ -289,7 +289,7 @@
     )(x)
 
 
-def _gather_kernel(n, x_ref, o_ref, half, full, sems):
+def _gather_kernel(n, x_ref, o_ref, mine, half, full, sems):
     rank = lax.axis_index("replica")
     me = lax.axis_index("mp")
     core = lax.rem(rank, 2)
@@ -300,11 +300,12 @@
         pl.semaphore_signal(barrier, inc=1, device_id=(rank, peer), device_id_type=MESH_IDS)
     pl.semaphore_signal(barrier, inc=1, device_id=(partner, me), device_id_type=MESH_IDS)
     pl.semaphore_wait(barrier, n)
+    mine[...] = x_ref[...].astype(mine.dtype)
     copies = []
     for d in range(1, n):
         peer = lax.rem(me + d, n)
         copy = pltpu.make_async_remote_copy(
-            src_ref=x_ref,
+            src_ref=mine,
             dst_ref=half.at[me],
             send_sem=sems.at[0, d],
             recv_sem=sems.at[1, me],
@@ -313,11 +314,11 @@
         )
         copy.start()
         copies.append(copy)
-    half[me] = x_ref[...]
+    half[me] = mine[...]
     for d in range(1, n):
         source = lax.rem(me + n - d, n)
         pltpu.make_async_remote_copy(
-            src_ref=x_ref,
+            src_ref=mine,
             dst_ref=half.at[source],
             send_sem=sems.at[0, d],
             recv_sem=sems.at[1, source],
@@ -343,12 +344,13 @@
 def gather_right(x, n, cid):
     return pl.pallas_call(
         functools.partial(_gather_kernel, n),
-        out_shape=jax.ShapeDtypeStruct((2, n) + x.shape, x.dtype),
+        out_shape=jax.ShapeDtypeStruct((2, n) + x.shape, jnp.bfloat16),
         in_specs=[pl.BlockSpec(memory_space=pltpu.VMEM)],
         out_specs=pl.BlockSpec(memory_space=pltpu.VMEM),
         scratch_shapes=[
-            pltpu.VMEM((n,) + x.shape, x.dtype),
-            pltpu.VMEM((2, n) + x.shape, x.dtype),
+            pltpu.VMEM(x.shape, jnp.bfloat16),
+            pltpu.VMEM((n,) + x.shape, jnp.bfloat16),
+            pltpu.VMEM((2, n) + x.shape, jnp.bfloat16),
             pltpu.SemaphoreType.DMA((3, n)),
         ],
         compiler_params=pltpu.CompilerParams(
@@ -413,7 +415,7 @@
     )
     right_terms = right_terms.reshape(matrices, -1, pieces, width).transpose(0, 2, 1, 3)
     right_terms = right_terms.astype(jnp.bfloat16).reshape(cores, owners_count, -1, width)
-    right_part = reduce_right(right_terms, chips, 2).astype(jnp.bfloat16)
+    right_part = reduce_right(right_terms, chips, 2)
     right_new = gather_right(right_part, owners_count, 4)
     right_new = right_new.reshape(matrices, pieces, -1, width).transpose(0, 2, 1, 3)
     right_new = right_new.reshape(matrices, -1, compensated.shape[2])

time: 127 us -> 127 us (level)
  no operation moved by 1% of the time
where the time goes in v17:
time: 127 us
  Pallas kernels  77.7 us (61%)
  between operations  16.8 us (13%)
  matrix products  14.9 us (12%)
  other arithmetic  7.41 us (6%)
  local copies, waits for them, and re-layouts  6.67 us (5%)
  starting transfers between devices  3.44 us (3%)
    pallas_call x1, Pallas kernels, reduce_right(): pl.pallas_call(functools.partial(_reduce_kernel, n, chips), out_shape=jax...  37 us
    pallas_call x1, Pallas kernels, allreduce_replica(): pl.pallas_call(functools.partial(_allreduce_kernel, n, stride), out_shape...  21 us
    pallas_call x1, Pallas kernels, gather_right(): pl.pallas_call(functools.partial(_gather_kernel, n), out_shape=jax.ShapeD...  19.7 us
    gather x1, local copies, waits for them, and re-layouts, per_device(): jnp.take(weight_slots, slots, axis=0).astype(jnp.float32)  4.44 us
    dot_general x1, matrix products, per_device(): jnp.einsum('kms,ksn->kmn', left_block, right_new, preferred_element_type=...  4.05 us
    ppermute x1, starting transfers between devices, per_device(): left_block = lax.ppermute(left_rows, ('replica', 'mp'), pairs)  3.4 us
    dot_general x1, matrix products, per_device(): jnp.einsum('kmn,knr->kmr', compensated, right_init, preferred_element_typ...  3.21 us
    dot_general x1, matrix products, per_device(): jnp.einsum('kmn,kms->ksn', compensated, left_rows, preferred_element_type...  3.09 us
  transfers between devices with their start and end apart: 2, of which 0 were waited for; matrix products, arithmetic and copies ran while one was open for 14% of the time, Pallas kernels for 61%

profile of v17, /device:TPU:1, one launch (start us, length us, event | category | flops | bytes accessed | tf_op | source)
XLA Modules:
  0.0 127.0 jit_solution(6772440931402025604)
XLA Ops:
  7.2 0.0 copy-start
  7.2 0.0 all-gather.3.cloned.1.call-start
  7.2 2.1 %subtract_convert_fusion.2 = bf16[1,1,48,3072]{3,2,1,0:T(8,128)(2,1)} fusion(f32[1,1,48,3072]{3,2,1,0:T(8,128)} %param.16, f32[1,1,48,3072]{3,2,1,0:T(8,128)} %param.15), kind=kLoop, calls=%fused_computation.12 | loop fusion | flops 442368 | bytes 1474560 | tf_op jit(solution)/shard_map/convert_element_type | solution.py:392
  9.4 0.0 all-gather.3.cloned.1.call-update
  9.4 0.0 copy-start.7
  9.4 0.0 copy-start.4
  9.4 3.2 %fusion.17 = f32[8,48,32]{2,1,0:T(8,128)S(1)} fusion(bf16[8,3072,32]{1,2,0:T(8,128)(2,1)S(1)} %copy-done, bf16[1,8,48,3072]{3,2,1,0:T(8,128)(2,1)} %param.11, bf16[1,8,48,3072]{3,2,1,0:T(8,128)(2,1)} %param.10), kind=kOutput, calls=%fused_computation.37 | convolution fusion | flops 80216064 | bytes 6340608 | tf_op jit(solution)/shard_map/kmn,knr->kmr/dot_general | solution.py:393
  12.6 0.1 reshape.144
  12.8 0.6 fusion.8.x_ref
  13.4 21.0 %shard_map.145 = f32[16,8,128]{2,1,0:T(8,128)} custom-call(f32[16,8,128]{2,1,0:T(8,128)} %fusion.8.x_ref), custom_call_target="tpu_custom_call" | custom-call | tf_op jit(solution)/shard_map/pallas_call | solution.py:140
  34.4 0.8 slice.7
  35.2 0.1 reshape.146
  35.3 0.5 convolution_convert_fusion.1
  35.8 3.4 %collective-permute-start = (bf16[8,48,32]{1,2,0:T(8,128)(2,1)S(1)}, bf16[8,48,32]{1,2,0:T(8,128)(2,1)S(1)}, u32[]{:S(2)}, u32[]{:S(2)}) collective-permute-start(bf16[8,48,32]{1,2,0:T(8,128)(2,1)S(1)} %convolution_convert_fusion.1), channel_id=1, source_target_pairs={{0,0},{1,16},{2,32},{3,48},{4,64},{5,80},{6,96},{7,112},{8,128},{9... | collective-permute-start | bytes 73736 | tf_op jit(solution)/shard_map/ppermute | solution.py:427
  39.2 3.1 %convolution_convert_fusion = bf16[8,32,3072]{2,1,0:T(8,128)(2,1)S(1)} fusion(bf16[8,48,32]{1,2,0:T(8,128)(2,1)S(1)} %convolution_convert_fusion.1, bf16[1,8,48,3072]{3,2,1,0:T(8,128)(2,1)} %param.11, bf16[1,8,48,3072]{3,2,1,0:T(8,128)(2,1)} %param.10), kind=kOutput, calls=%fused_computation.5 | convolution fusion | flops 81002496 | bytes 6316032 | tf_op jit(solution)/shard_map/kmn,kms->ksn/dot_general | solution.py:413
  42.3 0.2 copy.41
  42.5 37.0 %shard_map.146.x_ref = f32[32,768]{1,0:T(8,128)S(1)} custom-call(bf16[2,16,32,768]{3,2,1,0:T(8,128)(2,1)S(1)} %bitcast.50), custom_call_target="tpu_custom_call" | custom-call | tf_op jit(solution)/shard_map/pallas_call | solution.py:270
  79.5 0.0 copy-start.8
  79.5 0.0 copy-start.6
  79.5 0.0 copy-start.1
  79.6 19.7 %shard_map.147 = bf16[2,16,32,768]{3,2,1,0:T(8,128)(2,1)S(1)} custom-call(f32[32,768]{1,0:T(8,128)S(1)} %shard_map.146.x_ref), custom_call_target="tpu_custom_call" | custom-call | tf_op jit(solution)/shard_map/pallas_call | solution.py:345
  99.3 0.2 copy.39
  99.5 0.1 convert_reduce_fusion
  99.6 0.7 bitcast_reduce_fusion
  100.2 0.6 compare_and_fusion
  100.9 1.3 %multiply_subtract_fusion = (f32[672]{0:T(1024)}, f32[672]{0:T(1024)}) fusion(f32[672]{0:T(1024)S(1)} %copy-done.5, f32[16384]{0:T(1024)} %bitcast.58, f32[672]{0:T(1024)S(1)} %copy-done.6), kind=kLoop, calls=%fused_computation.28 | loop fusion | flops 2688 | bytes 13440 | tf_op jit(solution)/shard_map/sub | solution.py:445
  102.2 2.3 %fusion = bf16[1,8,48,3072]{3,2,1,0:T(8,128)(2,1)} fusion(bf16[8,48,32]{1,2,0:T(8,128)(2,1)S(1)} %convolution_convert_fusion.1, bf16[8,32,3072]{2,1,0:T(8,128)(2,1)S(1)} %bitcast.52, bf16[1,8,48,3072]{3,2,1,0:T(8,128)(2,1)S(1)} %copy-done.1, bf16[1,8,48,3072]{3,2,1,0:T(8,128)(2,1)S(1)} %copy-done.2), kind=kOutput, calls=%fused_computation.4 | convolution fusion | flops 83755008 | bytes 8675328 | tf_op jit(solution)/shard_map/kms,ksn->kmn/dot_general | solution.py:428
  107.1 1.7 %convolution_add_fusion = f32[48,3072]{1,0:T(8,128)S(1)} fusion(f32[1,1,48,3072]{3,2,1,0:T(8,128)} %param.15, bf16[8,32,3072]{2,1,0:T(8,128)(2,1)S(1)} %bitcast.53, s32[]{:T(128)} %bitcast.9, f32[]{:T(128)S(6)} %convert_element_type.111, bf16[8,48,32]{1,2,0:T(8,128)(2,1)S(1)} %collective-permute-done), kind=kOutput, calls=%fused_computation.6 | convolution fusion | flops 57117696 | bytes 1386496 | tf_op jit(solution)/shard_map/cmr,crn->cmn/dot_general | solution.py:435
  108.9 0.8 copy-done.3
  109.7 1.9 %fusion.2 = f32[1,1,48,3072]{3,2,1,0:T(8,128)} fusion(f32[1,1,48,3072]{3,2,1,0:T(8,128)} %param.16, f32[48,3072]{1,0:T(8,128)S(1)} %convolution_add_fusion), kind=kLoop, calls=%fused_computation.11 | loop fusion | flops 294912 | bytes 1769472 | tf_op jit(solution)/shard_map/broadcast_in_dim | solution.py:449
  111.6 4.4 %gather_fusion = bf16[8,48,3072]{2,1,0:T(8,128)(2,1)} fusion(bf16[16,48,3072]{2,1,0:T(8,128)(2,1)} %bitcast.57, s32[1024]{0:T(1024)S(1)} %pad_clamp_fusion), kind=kCustom, calls=%fused_computation | custom fusion | bytes 4718624 | tf_op jit(solution)/shard_map/jit(_take)/gather | solution.py:442
  116.1 4.0 %subtract_convert_fusion = bf16[8,48,3072]{2,1,0:T(8,128)(2,1)} fusion(bf16[8,48,32]{1,2,0:T(8,128)(2,1)S(1)} %collective-permute-done, bf16[8,32,3072]{2,1,0:T(8,128)(2,1)S(1)} %bitcast.54, bf16[8,48,3072]{2,1,0:T(8,128)(2,1)} %gather_fusion, pred[8]{0:T(512)(128)(4,1)S(1)} %get-tuple-element.32), kind=kOutput, calls=%fused_computation.1 | convolution fusion | flops 81395712 | bytes 6316040 | tf_op jit(solution)/shard_map/kms,ksn->kmn/dot_general | solution.py:438
  (15 shorter events, 0.1 us)
Async XLA Ops:
  7.2 2.2 %copy-start = (bf16[8,3072,32]{1,2,0:T(8,128)(2,1)S(1)}, bf16[8,3072,32]{1,2,0:T(8,128)(2,1)}, u32[]{:S(2)}) copy-start(bf16[8,3072,32]{1,2,0:T(8,128)(2,1)} %param.12) | copy-start | bytes 4718596
  7.2 104.4 %all-gather.3.cloned.1.call-start = ((), (), s32[]{:S(2)}) async-start(), calls=%async_computation | async-start | bytes 5013504 | tf_op jit(solution)/shard_map/all_gather | solution.py:392
  9.4 3.4 %copy-start.7 = (f32[1,672]{1,0:T(1,128)S(1)}, f32[1,672]{1,0:T(1,128)}, u32[]{:S(2)}) copy-start(f32[1,672]{1,0:T(1,128)} %param.17) | copy-start | bytes 8068
  9.4 25.9 %copy-start.4 = (f32[8,32,32]{2,1,0:T(8,128)S(1)}, f32[8,32,32]{2,1,0:T(8,128)}, u32[]{:S(2)}) copy-start(f32[8,32,32]{2,1,0:T(8,128)} %param.13) | copy-start | bytes 98308
  35.8 71.3 %collective-permute-start = (bf16[8,48,32]{1,2,0:T(8,128)(2,1)S(1)}, bf16[8,48,32]{1,2,0:T(8,128)(2,1)S(1)}, u32[]{:S(2)}, u32[]{:S(2)}) collective-permute-start(bf16[8,48,32]{1,2,0:T(8,128)(2,1)S(1)} %convolution_convert_fusion.1), channel_id=1, source_target_pairs={{0,0},{1,16},{2,32},{3,48},{4,64},{5,80},{6,96},{7,112},{8,128},{9... | collective-permute-start | bytes 73736 | tf_op jit(solution)/shard_map/ppermute | solution.py:427
  79.5 20.0 %copy-start.8 = (s32[8]{0:T(128)S(1)}, s32[8]{0:T(128)}, u32[]{:S(2)}) copy-start(s32[8]{0:T(128)} %param.14) | copy-start | bytes 100
  79.5 21.4 %copy-start.5 = (f32[672]{0:T(1024)S(1)}, f32[672]{0:T(1024)}, u32[]{:S(2)}) copy-start(f32[672]{0:T(1024)} %param.19) | copy-start | bytes 8068
  79.5 21.4 %copy-start.6 = (f32[672]{0:T(1024)S(1)}, f32[672]{0:T(1024)}, u32[]{:S(2)}) copy-start(f32[672]{0:T(1024)} %param.18) | copy-start | bytes 8068
  79.5 22.6 %copy-start.1 = (bf16[1,8,48,3072]{3,2,1,0:T(8,128)(2,1)S(1)}, bf16[1,8,48,3072]{3,2,1,0:T(8,128)(2,1)}, u32[]{:S(2)}) copy-start(bf16[1,8,48,3072]{3,2,1,0:T(8,128)(2,1)} %param.11) | copy-start | bytes 7077892
  79.6 22.6 %copy-start.2 = (bf16[1,8,48,3072]{3,2,1,0:T(8,128)(2,1)S(1)}, bf16[1,8,48,3072]{3,2,1,0:T(8,128)(2,1)}, u32[]{:S(2)}) copy-start(bf16[1,8,48,3072]{3,2,1,0:T(8,128)(2,1)} %param.10) | copy-start | bytes 7077892
  108.9 0.8 copy-start.3
Sparse Core Ops, SparseCore 0:
  11.0 71.3 all-gather.2
